TPU v7x, 128 devices: a whole 4x4x4 slice. The times are simulated.
128 devices in a mesh: row: 8 (over x, z_lo), col: 16 (over y, z_hi, core).
Axes of the slice: x: 4, y: 4, z: 4 (z_hi: 2, z_lo: 2; z = z_hi * 2 + z_lo), core: 2. Of those that a mesh axis runs over, the one named last changes fastest.
Arguments:
- tokens_in: bfloat16 [8192, 5120], P('row', 'col'), may hold values from -6 to 6
- token_grad: bfloat16 [8192, 5120], P('row', 'col'), may hold values from -6 to 6
- gate_gain: float32 [5120], replicated, may hold values from -4 to 4
- inner_weight: bfloat16 [5120, 13824], P(None, 'col'), may hold values from -0.078125 to 0.078125
- inner_bias: float32 [13824], P('col'), may hold values from -4 to 4
- outer_weight: bfloat16 [5120, 13824], P(None, 'col'), may hold values from -0.0546875 to 0.0546875
- inner_down: bfloat16 [5120, 64], replicated, may hold values from -0.078125 to 0.078125
- inner_up: bfloat16 [64, 13824], P(None, 'col'), may hold values from -0.1796875 to 0.1796875
- outer_down: bfloat16 [13824, 64], P('col'), may hold values from -0.0546875 to 0.0546875
- outer_up: bfloat16 [64, 5120], replicated, may hold values from -0.1796875 to 0.1796875
Outputs:
- tokens_grad: bfloat16 [8192, 5120], P('row', 'col')
- inner_down_grad: float32 [5120, 64], P('col')
- inner_up_grad: float32 [64, 13824], P(None, 'col')
- outer_down_grad: float32 [13824, 64], P('col')
- outer_up_grad: float32 [64, 5120], P(None, 'col')
All inputs are finite; a program needn't handle non-finite values.
Results may differ from a plain program's by a relative error of at most 0.023.
Values may be sent and summed in bfloat16 or wider, within the bound.
A program may use at most 128 MiB of HBM per device.

v0:
```python
import math

import jax
import jax.numpy as jnp
from jax import lax
from jax.sharding import PartitionSpec as P

SLOPE_SCALE = 0.7978845608028654
CUBIC = 0.044715


def gelu_value(pre):
    inner = SLOPE_SCALE * (pre + CUBIC * pre * pre * pre)
    return 0.5 * pre * (1.0 + jnp.tanh(inner))


def gelu_slope(pre):
    tangent = jnp.tanh(SLOPE_SCALE * (pre + CUBIC * pre * pre * pre))
    return 0.5 * (1.0 + tangent) + 0.5 * pre * (1.0 - tangent * tangent) * SLOPE_SCALE * (
        1.0 + 3.0 * CUBIC * pre * pre
    )


def plain_dot(left, right):
    return jnp.dot(left, right, preferred_element_type=jnp.float32)


def dot_rows(left, right):
    return lax.dot_general(
        left, right, (((1,), (1,)), ((), ())), preferred_element_type=jnp.float32
    )


def dot_cols(left, right):
    return lax.dot_general(
        left, right, (((0,), (0,)), ((), ())), preferred_element_type=jnp.float32
    )


def local(
    tokens_in,
    token_grad,
    gate_gain,
    inner_weight,
    inner_bias,
    outer_weight,
    inner_down,
    inner_up,
    outer_down,
    outer_up,
):
    col_index = lax.axis_index("col")
    local_width = token_grad.shape[1]
    tok_rows = tokens_in.shape[0]
    gain_local = lax.dynamic_slice_in_dim(gate_gain, col_index * local_width, local_width, 0)
    gated_local = (gain_local[None, :] * token_grad.astype(jnp.float32)).astype(jnp.bfloat16)
    tokens_full, gated_full = (
        lax.all_gather(tokens_in, "col", axis=1, tiled=True),
        lax.all_gather(gated_local, "col", axis=1, tiled=True),
    )
    inner_low = plain_dot(tokens_full, inner_down).astype(jnp.bfloat16)
    forward_sum = plain_dot(tokens_full, inner_weight)
    grad_low = dot_rows(gated_full, outer_up).astype(jnp.bfloat16)
    backward_sum = plain_dot(gated_full, outer_weight)
    pre = forward_sum + plain_dot(inner_low, inner_up) + inner_bias[None, :]
    hidden = gelu_value(pre).astype(jnp.bfloat16)
    hidden_low = lax.psum(plain_dot(hidden, outer_down).astype(jnp.bfloat16), "col")
    scale = 1.0 / math.sqrt(tok_rows * lax.axis_size("row"))
    outer_down_term = dot_cols(hidden, grad_low) * scale
    outer_up_term = dot_cols(hidden_low, gated_local) * scale
    outer_down_grad, outer_up_grad = (
        lax.psum(outer_down_term.astype(jnp.bfloat16), "row").astype(jnp.float32),
        lax.psum(outer_up_term.astype(jnp.bfloat16), "row").astype(jnp.float32),
    )
    grad_hidden = backward_sum + dot_rows(grad_low, outer_down)
    grad_pre = (grad_hidden * gelu_slope(pre)).astype(jnp.bfloat16)
    pre_low = lax.psum(dot_rows(grad_pre, inner_up).astype(jnp.bfloat16), "col")
    block_part = dot_rows(grad_pre, inner_weight).astype(jnp.bfloat16).astype(jnp.float32)
    parts = lax.psum_scatter(
        block_part.astype(jnp.bfloat16), "col", scatter_dimension=1, tiled=True
    ).astype(jnp.float32)
    down_local = lax.dynamic_slice_in_dim(inner_down, col_index * local_width, local_width, 0)
    tokens_grad = (parts + dot_rows(pre_low, down_local)).astype(jnp.bfloat16)
    inner_down_term = dot_cols(tokens_in, pre_low) * scale
    inner_up_term = dot_cols(inner_low, grad_pre) * scale
    inner_down_grad, inner_up_grad = (
        lax.psum(inner_down_term.astype(jnp.bfloat16), "row").astype(jnp.float32),
        lax.psum(inner_up_term.astype(jnp.bfloat16), "row").astype(jnp.float32),
    )
    return (tokens_grad, inner_down_grad, inner_up_grad, outer_down_grad, outer_up_grad)


def solution(mesh):
    placed = (
        P("row", "col"),
        P("row", "col"),
        P(),
        P(None, "col"),
        P("col"),
        P(None, "col"),
        P(),
        P(None, "col"),
        P("col", None),
        P(),
    )
    return jax.shard_map(
        local,
        mesh=mesh,
        in_specs=placed,
        out_specs=(P("row", "col"), P("col", None), P(None, "col"), P("col", None), P(None, "col")),
        check_vma=False,
    )
```

profile of v0, /device:TPU:1, one launch (start us, length us, event | category | flops | bytes accessed | tf_op | source)
XLA Modules:
  0.0 614.2 jit_solution(17318169945764343556)
XLA Ops:
  8.7 2.1 multiply_convert_fusion.1
  10.9 84.7 %all-gather.5.cloned.1.call-done = bf16[1024,5120]{0,1:T(8,128)(2,1)} async-done(((bf16[1024,320]{0,1:T(8,128)(2,1)}), bf16[1024,5120]{0,1:T(8,128)(2,1)}) %all-gather.5.cloned.1.call-update) | async-done | bytes 10485776 | tf_op jit(solution)/shard_map/all_gather | solution.py:58
  95.7 6.1 convolution_convert_fusion.2
  102.6 2.5 copy-done.8
  105.1 9.3 %fusion.16 = f32[1024,864]{0,1:T(8,128)S(1)} fusion(bf16[5120,864]{0,1:T(8,128)(2,1)S(1)} %copy-done.8, bf16[1024,5120]{0,1:T(8,128)(2,1)S(1)} %copy-done.1), kind=kOutput, calls=%fused_computation.31 | convolution fusion | flops 9059696640 | bytes 22872064 | tf_op jit(solution)/shard_map/dot_general | solution.py:25
  114.5 3.5 multiply_convert_fusion
  118.0 59.9 %all-gather.3.cloned.1.call-done = bf16[1024,5120]{0,1:T(8,128)(2,1)} async-done(((bf16[1024,320]{0,1:T(8,128)(2,1)}), bf16[1024,5120]{0,1:T(8,128)(2,1)}) %all-gather.3.cloned.1.call-update) | async-done | bytes 10485776 | tf_op jit(solution)/shard_map/all_gather | solution.py:59
  177.8 6.1 convolution_convert_fusion.3
  183.9 1.3 fusion.9
  185.2 1.6 convolution_convert_fusion.1
  186.8 12.1 %fusion.15 = f32[1024,864]{0,1:T(8,128)S(1)} fusion(bf16[5120,864]{0,1:T(8,128)(2,1)} %param.15, bf16[1024,5120]{0,1:T(8,128)(2,1)S(1)} %copy-done.2), kind=kOutput, calls=%fused_computation.30 | convolution fusion | flops 9059696640 | bytes 22872064 | tf_op jit(solution)/shard_map/dot_general | solution.py:25
  198.9 2.7 fusion.6
  204.2 134.1 %all-reduce.7.cloned.1.call-done = (bf16[1024,64]{0,1:T(8,128)(2,1)}, bf16[1024,64]{1,0:T(8,128)(2,1)}) async-done(((bf16[1024,64]{0,1:T(8,128)(2,1)}, bf16[1024,64]{1,0:T(8,128)(2,1)}), (bf16[1024,64]{0,1:T(8,128)(2,1)}, bf16[1024,64]{1,0:T(8,128)(2,1)})) %all-reduce.7.cloned.1.call-update) | async-done | bytes 262160 | tf_op jit(solution)/shard_map/psum | solution.py:77
  338.2 1.9 fusion.11
  340.1 2.1 fusion.12
  342.3 21.0 %convolution_convert_fusion = bf16[1024,5120]{0,1:T(8,128)(2,1)} fusion(bf16[1024,864]{0,1:T(8,128)(2,1)S(1)} %fusion.6, bf16[5120,864]{0,1:T(8,128)(2,1)} %param.13), kind=kOutput, calls=%fused_computation | convolution fusion | flops 9064939520 | bytes 21102592 | tf_op jit(solution)/shard_map/dot_general | solution.py:29
  363.4 46.8 %all-reduce.11.cloned.1.call-done = (bf16[64,864]{1,0:T(8,128)(2,1)}, bf16[864,64]{0,1:T(8,128)(2,1)}) async-done(((bf16[64,864]{1,0:T(8,128)(2,1)}, bf16[864,64]{0,1:T(8,128)(2,1)}), (bf16[64,864]{1,0:T(8,128)(2,1)}, bf16[864,64]{0,1:T(8,128)(2,1)})) %all-reduce.11.cloned.1.call-update) | async-done | bytes 221200 | tf_op jit(solution)/shard_map/psum | solution.py:88
  410.1 1.6 convert_element_type.75
  411.7 1.6 convert_element_type.78
  413.4 70.8 %all-reduce.9.cloned.1.call-done = (bf16[320,64]{0,1:T(8,128)(2,1)}, bf16[64,320]{1,0:T(8,128)(2,1)}) async-done(((bf16[320,64]{0,1:T(8,128)(2,1)}, bf16[64,320]{1,0:T(8,128)(2,1)}), (bf16[320,64]{0,1:T(8,128)(2,1)}, bf16[64,320]{1,0:T(8,128)(2,1)})) %all-reduce.9.cloned.1.call-update) | async-done | bytes 81936 | tf_op jit(solution)/shard_map/psum | solution.py:87
  484.2 1.4 convert_element_type.73
  485.6 1.4 convert_element_type.81
  487.1 117.9 %reduce-scatter.2.cloned.1.call-done = bf16[1024,320]{0,1:T(8,128)(2,1)} async-done(((bf16[1024,5120]{0,1:T(8,128)(2,1)}), bf16[1024,320]{0,1:T(8,128)(2,1)}) %reduce-scatter.2.cloned.1.call-update) | async-done | bytes 655376 | tf_op jit(solution)/shard_map/reduce_scatter | solution.py:79
  605.0 2.4 fusion.7
  (36 shorter events, 5.1 us)
Async XLA Ops:
  7.2 88.5 %copy-start = (bf16[5120,64]{0,1:T(8,128)(2,1)S(1)}, bf16[5120,64]{0,1:T(8,128)(2,1)}, u32[]{:S(2)}) copy-start(bf16[5120,64]{0,1:T(8,128)(2,1)} %param.16) | copy-start | bytes 1966084
  7.2 88.5 %all-gather.5.cloned.1.call-start = ((), (), s32[]{:S(2)}) async-start(), calls=%async_computation.2 | async-start | bytes 11141120 | tf_op jit(solution)/shard_map/all_gather | solution.py:58
  7.9 169.9 %all-gather.3.cloned.1.call-start = ((), (), s32[]{:S(2)}) async-start(), calls=%async_computation.1 | async-start | bytes 11141120 | tf_op jit(solution)/shard_map/all_gather | solution.py:59
  10.9 327.4 %all-reduce.7.cloned.1.call-start = ((), (), s32[]{:S(2)}) async-start(), calls=%async_computation.4 | async-start | bytes 786432 | tf_op jit(solution)/shard_map/psum | solution.py:77
  95.7 7.0 %copy-start.1 = (bf16[1024,5120]{0,1:T(8,128)(2,1)S(1)}, bf16[1024,5120]{0,1:T(8,128)(2,1)}, u32[]{:S(2)}) copy-start(bf16[1024,5120]{0,1:T(8,128)(2,1)} %all-gather.5.cloned.1.call-done) | copy-start | bytes 31457284
  95.7 9.5 %copy-start.8 = (bf16[5120,864]{0,1:T(8,128)(2,1)S(1)}, bf16[5120,864]{0,1:T(8,128)(2,1)}, u32[]{:S(2)}) copy-start(bf16[5120,864]{0,1:T(8,128)(2,1)} %param.13) | copy-start | bytes 26542084
  105.1 9.3 %copy-start.7 = (bf16[64,864]{1,0:T(8,128)(2,1)S(1)}, bf16[64,864]{1,0:T(8,128)(2,1)}, u32[]{:S(2)}) copy-start(bf16[64,864]{1,0:T(8,128)(2,1)} %param.17) | copy-start | bytes 331780
  105.1 9.4 %copy-start.9 = (f32[864]{0:T(1024)S(1)}, f32[864]{0:T(1024)}, u32[]{:S(2)}) copy-start(f32[864]{0:T(1024)} %param.14) | copy-start | bytes 10372
  114.5 63.3 %copy-start.4 = (bf16[64,5120]{1,0:T(8,128)(2,1)S(1)}, bf16[64,5120]{1,0:T(8,128)(2,1)}, u32[]{:S(2)}) copy-start(bf16[64,5120]{1,0:T(8,128)(2,1)} %param.19) | copy-start | bytes 1966084
  118.0 67.3 %copy-start.6 = (bf16[864,64]{0,1:T(8,128)(2,1)S(1)}, bf16[864,64]{0,1:T(8,128)(2,1)}, u32[]{:S(2)}) copy-start(bf16[864,64]{0,1:T(8,128)(2,1)} %param.18) | copy-start | bytes 331780
  177.8 9.0 %copy-start.2 = (bf16[1024,5120]{0,1:T(8,128)(2,1)S(1)}, bf16[1024,5120]{0,1:T(8,128)(2,1)}, u32[]{:S(2)}) copy-start(bf16[1024,5120]{0,1:T(8,128)(2,1)} %all-gather.3.cloned.1.call-done) | copy-start | bytes 31457284
  186.8 12.1 %copy-start.10 = (f32[1024,864]{0,1:T(8,128)S(1)}, f32[1024,864]{0,1:T(8,128)}, u32[]{:S(2)}) copy-start(f32[1024,864]{0,1:T(8,128)} %get-tuple-element.12) | copy-start | bytes 10616836
  201.6 136.6 %copy-start.3 = (bf16[1024,320]{0,1:T(8,128)(2,1)S(1)}, bf16[1024,320]{0,1:T(8,128)(2,1)}, u32[]{:S(2)}) copy-start(bf16[1024,320]{0,1:T(8,128)(2,1)} %multiply_convert_fusion.1) | copy-start | bytes 1966084
  202.7 207.4 %all-reduce.11.cloned.1.call-start = ((), (), s32[]{:S(2)}) async-start(), calls=%async_computation.6 | async-start | bytes 458752 | tf_op jit(solution)/shard_map/psum | solution.py:88
  204.1 280.1 %all-reduce.9.cloned.1.call-start = ((), (), s32[]{:S(2)}) async-start(), calls=%async_computation.5 | async-start | bytes 196608 | tf_op jit(solution)/shard_map/psum | solution.py:87
  342.3 262.7 %reduce-scatter.2.cloned.1.call-start = ((), (), s32[]{:S(2)}) async-start(), calls=%async_computation.3 | async-start | bytes 11141120 | tf_op jit(solution)/shard_map/reduce_scatter | solution.py:79
  363.3 241.7 %copy-start.5 = (bf16[1024,64]{0,1:T(8,128)(2,1)S(1)}, bf16[1024,64]{0,1:T(8,128)(2,1)}, u32[]{:S(2)}) copy-start(bf16[1024,64]{0,1:T(8,128)(2,1)} %get-tuple-element.5) | copy-start | bytes 393220
Sparse Core Ops, SparseCore 0:
  10.4 85.1 all-gather.4
  98.6 79.1 all-gather.2
  202.9 135.3 all-reduce.6
  341.4 68.7 all-reduce.10
  413.1 71.0 all-reduce.8
  489.0 115.9 reduce-scatter.1
where the time goes:
time: 615 us; the launch traced here: 614 us
  waiting for transfers between devices  515 us (84%)
  matrix products  72.4 us (12%)
  between operations  14.2 us (2%)
  other arithmetic  8.19 us (1%)
    psum x1, waiting for transfers between devices, local(): pre_low = lax.psum(dot_rows(grad_pre, inner_up).astype(jnp.bfloat16), 'col')  134 us
    reduce_scatter x1, waiting for transfers between devices, local(): lax.psum_scatter(block_part.astype(jnp.bfloat16), 'col', scatter_dimensio...  118 us
    all_gather x1, waiting for transfers between devices, local(): lax.all_gather(tokens_in, 'col', axis=1, tiled=True)  84.7 us
    psum x1, waiting for transfers between devices, local(): lax.psum(inner_down_term.astype(jnp.bfloat16), 'row').astype(jnp.float32)  70.8 us
    all_gather x1, waiting for transfers between devices, local(): lax.all_gather(gated_local, 'col', axis=1, tiled=True)  59.9 us
    psum x1, waiting for transfers between devices, local(): lax.psum(inner_up_term.astype(jnp.bfloat16), 'row').astype(jnp.float32)  46.8 us
    dot_general x5, matrix products, dot_rows(): lax.dot_general(left, right, (((1,), (1,)), ((), ())), preferred_element_...  33.2 us
    dot_general x5, matrix products, plain_dot(): return jnp.dot(left, right, preferred_element_type=jnp.float32)  32.5 us
  transfers between devices with their start and end apart: 6, of which 6 were waited for; matrix products, arithmetic and copies ran while one was open for 9% of the time, Pallas kernels for 0%

commit v1 on v0

v1 whole, which is shorter than its diff:
```python
import math

import jax
import jax.numpy as jnp
from jax import lax
from jax.sharding import PartitionSpec as P

SLOPE_SCALE = 0.7978845608028654
CUBIC = 0.044715


def gelu_value(pre):
    inner = SLOPE_SCALE * (pre + CUBIC * pre * pre * pre)
    return 0.5 * pre * (1.0 + jnp.tanh(inner))


def gelu_slope(pre):
    tangent = jnp.tanh(SLOPE_SCALE * (pre + CUBIC * pre * pre * pre))
    return 0.5 * (1.0 + tangent) + 0.5 * pre * (1.0 - tangent * tangent) * SLOPE_SCALE * (
        1.0 + 3.0 * CUBIC * pre * pre
    )


def plain_dot(left, right):
    return jnp.dot(left, right, preferred_element_type=jnp.float32)


def dot_rows(left, right):
    return lax.dot_general(
        left, right, (((1,), (1,)), ((), ())), preferred_element_type=jnp.float32
    )


def dot_cols(left, right):
    return lax.dot_general(
        left, right, (((0,), (0,)), ((), ())), preferred_element_type=jnp.float32
    )


def tree_sum(value, axis, size):
    step = 1
    while step < size:
        pairs = [(i, i ^ step) for i in range(size)]
        value = value + lax.ppermute(value, axis, pairs)
        step *= 2
    return value


def local(
    tokens_in,
    token_grad,
    gate_gain,
    inner_weight,
    inner_bias,
    outer_weight,
    inner_down,
    inner_up,
    outer_down,
    outer_up,
):
    n_col = lax.axis_size("col")
    n_row = lax.axis_size("row")
    col_index = lax.axis_index("col")
    local_width = token_grad.shape[1]
    tok_rows = tokens_in.shape[0]
    ff_local = inner_weight.shape[1]
    rank = inner_down.shape[1]
    gain_local = lax.dynamic_slice_in_dim(gate_gain, col_index * local_width, local_width, 0)
    gated_local = (gain_local[None, :] * token_grad.astype(jnp.float32)).astype(jnp.bfloat16)
    tokens_full = lax.all_gather(tokens_in, "col", axis=1, tiled=True)
    gated_full = lax.all_gather(gated_local, "col", axis=1, tiled=True)
    inner_low = plain_dot(tokens_full, inner_down).astype(jnp.bfloat16)
    forward_sum = plain_dot(tokens_full, inner_weight)
    grad_low = dot_rows(gated_full, outer_up).astype(jnp.bfloat16)
    backward_sum = plain_dot(gated_full, outer_weight)
    pre = forward_sum + plain_dot(inner_low, inner_up) + inner_bias[None, :]
    hidden = gelu_value(pre).astype(jnp.bfloat16)
    grad_hidden = backward_sum + dot_rows(grad_low, outer_down)
    grad_pre = (grad_hidden * gelu_slope(pre)).astype(jnp.bfloat16)
    pre_low_part = dot_rows(grad_pre, inner_up)
    block_part = dot_rows(grad_pre, inner_weight).astype(jnp.bfloat16).astype(jnp.float32)
    low_part = dot_rows(pre_low_part.astype(jnp.bfloat16), inner_down)
    tokens_grad = lax.psum_scatter(
        (block_part + low_part).astype(jnp.bfloat16), "col", scatter_dimension=1, tiled=True
    )

    hidden_low_part = plain_dot(hidden, outer_down)
    lows = tree_sum(jnp.concatenate([hidden_low_part, pre_low_part], axis=1), "col", n_col)
    hidden_low = lows[:, :rank].astype(jnp.bfloat16)
    pre_low = lows[:, rank:].astype(jnp.bfloat16)

    scale = 1.0 / math.sqrt(tok_rows * n_row)
    outer_down_term = dot_cols(hidden, grad_low)
    outer_up_term = dot_cols(gated_local, hidden_low)
    inner_down_term = dot_cols(tokens_in, pre_low)
    inner_up_term = dot_cols(grad_pre, inner_low)
    packed = jnp.concatenate([outer_down_term, inner_up_term, outer_up_term, inner_down_term], axis=0)
    packed = tree_sum(packed, "row", n_row) * scale
    outer_down_grad = packed[:ff_local]
    inner_up_grad = packed[ff_local : 2 * ff_local].T
    outer_up_grad = packed[2 * ff_local : 2 * ff_local + local_width].T
    inner_down_grad = packed[2 * ff_local + local_width :]
    return (tokens_grad, inner_down_grad, inner_up_grad, outer_down_grad, outer_up_grad)


def solution(mesh):
    placed = (
        P("row", "col"),
        P("row", "col"),
        P(),
        P(None, "col"),
        P("col"),
        P(None, "col"),
        P(),
        P(None, "col"),
        P("col", None),
        P(),
    )
    return jax.shard_map(
        local,
        mesh=mesh,
        in_specs=placed,
        out_specs=(P("row", "col"), P("col", None), P(None, "col"), P("col", None), P(None, "col")),
        check_vma=False,
    )
```

time: 615 us -> 342 us (0.56)
  waiting for transfers between devices: 515 us -> 248 us
  matrix products: 72.4 us -> 63.9 us
    psum x3 -> x0, waiting for transfers between devices: 252 us -> none  [the longest x1 134 us: local(): pre_low = lax.psum(dot_rows(grad_pre, inner_up).astype(jnp.bfloat16), 'col')]
    reduce_scatter x1, waiting for transfers between devices: 118 us -> 28.9 us  [local(): lax.psum_scatter((block_part + low_part).astype(jnp.bfloat16), 'col', sca...]
    ppermute x0 -> x7, waiting for transfers between devices: none -> 74.2 us  [tree_sum(): value = value + lax.ppermute(value, axis, pairs)]
  transfers between devices with their start and end apart: 6 -> 10, of which waited for: 6 -> 10; matrix products, arithmetic and copies ran while one was open for 9% -> 8% of each run, Pallas kernels for 0% -> 0%
where the time goes in v1:
time: 342 us
  waiting for transfers between devices  248 us (73%)
  matrix products  63.9 us (19%)
  between operations  14 us (4%)
  local copies, waits for them, and re-layouts  7.89 us (2%)
  starting transfers between devices  5.81 us (2%)
    all_gather x1, waiting for transfers between devices, local(): tokens_full = lax.all_gather(tokens_in, 'col', axis=1, tiled=True)  84.7 us
    ppermute x7, waiting for transfers between devices, tree_sum(): value = value + lax.ppermute(value, axis, pairs)  74.2 us
    all_gather x1, waiting for transfers between devices, local(): gated_full = lax.all_gather(gated_local, 'col', axis=1, tiled=True)  59.2 us
    dot_general x5, matrix products, plain_dot(): return jnp.dot(left, right, preferred_element_type=jnp.float32)  31.4 us
    dot_general x5, matrix products, dot_rows(): lax.dot_general(left, right, (((1,), (1,)), ((), ())), preferred_element_...  30.4 us
    reduce_scatter x1, waiting for transfers between devices, local(): lax.psum_scatter((block_part + low_part).astype(jnp.bfloat16), 'col', sca...  28.9 us
  transfers between devices with their start and end apart: 10, of which 10 were waited for; matrix products, arithmetic and copies ran while one was open for 8% of the time, Pallas kernels for 0%

profile of v1, /device:TPU:1, one launch (start us, length us, event | category | flops | bytes accessed | tf_op | source)
XLA Modules:
  0.0 341.9 jit_solution(5245338813247819745)
XLA Ops:
  8.7 2.1 multiply_convert_fusion.1
  10.9 84.7 %all-gather.5.cloned.1.call-done = bf16[1024,5120]{0,1:T(8,128)(2,1)} async-done(((bf16[1024,320]{0,1:T(8,128)(2,1)}), bf16[1024,5120]{0,1:T(8,128)(2,1)}) %all-gather.5.cloned.1.call-update) | async-done | bytes 10485776 | tf_op jit(solution)/shard_map/all_gather | solution.py:70
  95.7 6.1 %convolution_convert_fusion = bf16[1024,64]{0,1:T(8,128)(2,1)S(1)} fusion(bf16[5120,64]{0,1:T(8,128)(2,1)S(1)} %copy-done, bf16[1024,5120]{0,1:T(8,128)(2,1)} %all-gather.5.cloned.1.call-done), kind=kOutput, calls=%fused_computation.13 | convolution fusion | flops 671154176 | bytes 11272192 | tf_op jit(solution)/shard_map/dot_general | solution.py:25
  102.6 2.6 copy-done.14
  105.3 9.3 %fusion.17 = f32[1024,864]{0,1:T(8,128)S(1)} fusion(bf16[5120,864]{0,1:T(8,128)(2,1)S(1)} %copy-done.14, bf16[1024,5120]{0,1:T(8,128)(2,1)S(1)} %copy-done.1), kind=kOutput, calls=%fused_computation.31 | convolution fusion | flops 9059696640 | bytes 22872064 | tf_op jit(solution)/shard_map/dot_general | solution.py:25
  114.6 3.4 multiply_convert_fusion
  118.0 59.2 %all-gather.3.cloned.1.call-done = bf16[1024,5120]{0,1:T(8,128)(2,1)} async-done(((bf16[1024,320]{0,1:T(8,128)(2,1)}), bf16[1024,5120]{0,1:T(8,128)(2,1)}) %all-gather.3.cloned.1.call-update) | async-done | bytes 10485776 | tf_op jit(solution)/shard_map/all_gather | solution.py:71
  177.3 6.1 %convolution_convert_fusion.1 = bf16[1024,64]{0,1:T(8,128)(2,1)S(1)} fusion(bf16[64,5120]{1,0:T(8,128)(2,1)S(1)} %copy-done.8, bf16[1024,5120]{0,1:T(8,128)(2,1)} %all-gather.3.cloned.1.call-done), kind=kOutput, calls=%fused_computation.14 | convolution fusion | flops 671154176 | bytes 11272192 | tf_op jit(solution)/shard_map/dot_general | solution.py:29
  184.2 12.2 %fusion.16 = f32[1024,864]{0,1:T(8,128)S(1)} fusion(bf16[5120,864]{0,1:T(8,128)(2,1)} %param.15, bf16[1024,5120]{0,1:T(8,128)(2,1)S(1)} %copy-done.2), kind=kOutput, calls=%fused_computation.30 | convolution fusion | flops 9059696640 | bytes 22872064 | tf_op jit(solution)/shard_map/dot_general | solution.py:25
  196.4 2.7 fusion.6
  199.1 1.3 fusion.18
  200.4 13.6 %fusion.13 = bf16[1024,5120]{0,1:T(8,128)(2,1)S(1)} fusion(bf16[1024,864]{0,1:T(8,128)(2,1)S(1)} %fusion.6, bf16[5120,864]{0,1:T(8,128)(2,1)} %param.13), kind=kOutput, calls=%fused_computation.27 | convolution fusion | flops 9059696640 | bytes 21102592 | tf_op jit(solution)/shard_map/dot_general | solution.py:29
  214.1 6.8 %add_convert_fusion = bf16[1024,5120]{0,1:T(8,128)(2,1)} fusion(bf16[5120,64]{0,1:T(8,128)(2,1)S(1)} %copy-done, bf16[1024,5120]{0,1:T(8,128)(2,1)S(1)} %fusion.13, f32[1024,64]{0,1:T(8,128)} %fusion.18), kind=kOutput, calls=%fused_computation | convolution fusion | flops 686882816 | bytes 21889024 | tf_op jit(solution)/shard_map/dot_general | solution.py:29
  222.6 1.7 collective-permute-done
  224.5 14.7 %collective-permute-done.1 = f32[1024,128]{0,1:T(8,128)S(1)} collective-permute-done((f32[1024,128]{0,1:T(8,128)S(1)}, f32[1024,128]{0,1:T(8,128)S(1)}, u32[]{:S(2)}, u32[]{:S(2)}) %collective-permute-start.1) | collective-permute-done | bytes 524320 | tf_op jit(solution)/shard_map/ppermute | solution.py:44
  239.4 12.3 %collective-permute-done.2 = f32[1024,128]{0,1:T(8,128)S(1)} collective-permute-done((f32[1024,128]{0,1:T(8,128)S(1)}, f32[1024,128]{0,1:T(8,128)S(1)}, u32[]{:S(2)}, u32[]{:S(2)}) %collective-permute-start.2) | collective-permute-done | bytes 524320 | tf_op jit(solution)/shard_map/ppermute | solution.py:44
  251.8 1.2 collective-permute-start.3
  254.3 15.3 %collective-permute-done.3 = f32[1024,128]{0,1:T(8,128)S(1)} collective-permute-done((f32[1024,128]{0,1:T(8,128)S(1)}, f32[1024,128]{0,1:T(8,128)S(1)}, u32[]{:S(2)}, u32[]{:S(2)}) %collective-permute-start.3) | collective-permute-done | bytes 524320 | tf_op jit(solution)/shard_map/ppermute | solution.py:44
  270.7 9.5 %collective-permute-done.4 = f32[2368,64]{0,1:T(8,128)S(1)} collective-permute-done((f32[2368,64]{0,1:T(8,128)S(1)}, f32[2368,64]{0,1:T(8,128)S(1)}, u32[]{:S(2)}, u32[]{:S(2)}) %collective-permute-start.4) | collective-permute-done | bytes 606240 | tf_op jit(solution)/shard_map/ppermute | solution.py:44
  280.2 1.1 collective-permute-start.5
  281.4 8.5 %collective-permute-done.5 = f32[2368,64]{0,1:T(8,128)S(1)} collective-permute-done((f32[2368,64]{0,1:T(8,128)S(1)}, f32[2368,64]{0,1:T(8,128)S(1)}, u32[]{:S(2)}, u32[]{:S(2)}) %collective-permute-start.5) | collective-permute-done | bytes 606240 | tf_op jit(solution)/shard_map/ppermute | solution.py:44
  289.9 2.7 collective-permute-start.6
  292.6 12.3 %collective-permute-done.6 = f32[2368,64]{0,1:T(8,128)S(1)} collective-permute-done((f32[2368,64]{0,1:T(8,128)S(1)}, f32[2368,64]{0,1:T(8,128)S(1)}, u32[]{:S(2)}, u32[]{:S(2)}) %collective-permute-start.6) | collective-permute-done | bytes 606240 | tf_op jit(solution)/shard_map/ppermute | solution.py:44
  306.5 28.9 %reduce-scatter.2.cloned.1.call-done = bf16[1024,320]{0,1:T(8,128)(2,1)} async-done(((bf16[1024,5120]{0,1:T(8,128)(2,1)}), bf16[1024,320]{0,1:T(8,128)(2,1)}) %reduce-scatter.2.cloned.1.call-update) | async-done | bytes 655376 | tf_op jit(solution)/shard_map/reduce_scatter | solution.py:83
  (60 shorter events, 9.7 us)
Async XLA Ops:
  7.2 88.5 %copy-start = (bf16[5120,64]{0,1:T(8,128)(2,1)S(1)}, bf16[5120,64]{0,1:T(8,128)(2,1)}, u32[]{:S(2)}) copy-start(bf16[5120,64]{0,1:T(8,128)(2,1)} %param.16) | copy-start | bytes 1966084
  7.2 88.5 %all-gather.5.cloned.1.call-start = ((), (), s32[]{:S(2)}) async-start(), calls=%async_computation.2 | async-start | bytes 11141120 | tf_op jit(solution)/shard_map/all_gather | solution.py:70
  7.9 169.3 %all-gather.3.cloned.1.call-start = ((), (), s32[]{:S(2)}) async-start(), calls=%async_computation.1 | async-start | bytes 11141120 | tf_op jit(solution)/shard_map/all_gather | solution.py:71
  10.9 324.5 %reduce-scatter.2.cloned.1.call-start = ((), (), s32[]{:S(2)}) async-start(), calls=%async_computation.3 | async-start | bytes 11141120 | tf_op jit(solution)/shard_map/reduce_scatter | solution.py:83
  95.7 7.0 %copy-start.1 = (bf16[1024,5120]{0,1:T(8,128)(2,1)S(1)}, bf16[1024,5120]{0,1:T(8,128)(2,1)}, u32[]{:S(2)}) copy-start(bf16[1024,5120]{0,1:T(8,128)(2,1)} %all-gather.5.cloned.1.call-done) | copy-start | bytes 31457284
  95.7 9.6 %copy-start.14 = (bf16[5120,864]{0,1:T(8,128)(2,1)S(1)}, bf16[5120,864]{0,1:T(8,128)(2,1)}, u32[]{:S(2)}) copy-start(bf16[5120,864]{0,1:T(8,128)(2,1)} %param.13) | copy-start | bytes 26542084
  105.2 9.3 %copy-start.11 = (bf16[64,864]{1,0:T(8,128)(2,1)S(1)}, bf16[64,864]{1,0:T(8,128)(2,1)}, u32[]{:S(2)}) copy-start(bf16[64,864]{1,0:T(8,128)(2,1)} %param.17) | copy-start | bytes 331780
  105.3 9.4 %copy-start.15 = (f32[864]{0:T(1024)S(1)}, f32[864]{0:T(1024)}, u32[]{:S(2)}) copy-start(f32[864]{0:T(1024)} %param.14) | copy-start | bytes 10372
  114.6 62.6 %copy-start.8 = (bf16[64,5120]{1,0:T(8,128)(2,1)S(1)}, bf16[64,5120]{1,0:T(8,128)(2,1)}, u32[]{:S(2)}) copy-start(bf16[64,5120]{1,0:T(8,128)(2,1)} %param.19) | copy-start | bytes 1966084
  177.3 7.0 %copy-start.2 = (bf16[1024,5120]{0,1:T(8,128)(2,1)S(1)}, bf16[1024,5120]{0,1:T(8,128)(2,1)}, u32[]{:S(2)}) copy-start(bf16[1024,5120]{0,1:T(8,128)(2,1)} %all-gather.3.cloned.1.call-done) | copy-start | bytes 31457284
  184.2 12.2 %copy-start.9 = (bf16[1024,64]{0,1:T(8,128)(2,1)}, bf16[1024,64]{0,1:T(8,128)(2,1)S(1)}, u32[]{:S(2)}) copy-start(bf16[1024,64]{0,1:T(8,128)(2,1)S(1)} %convolution_convert_fusion.1) | copy-start | bytes 393220
  184.2 12.2 %copy-start.12 = (bf16[864,64]{0,1:T(8,128)(2,1)S(1)}, bf16[864,64]{0,1:T(8,128)(2,1)}, u32[]{:S(2)}) copy-start(bf16[864,64]{0,1:T(8,128)(2,1)} %param.18) | copy-start | bytes 331780
  184.2 12.2 %copy-start.16 = (f32[1024,864]{0,1:T(8,128)S(1)}, f32[1024,864]{0,1:T(8,128)}, u32[]{:S(2)}) copy-start(f32[1024,864]{0,1:T(8,128)} %get-tuple-element.10) | copy-start | bytes 10616836
  221.8 31.2 %copy-start.10 = (bf16[1024,64]{0,1:T(8,128)(2,1)S(1)}, bf16[1024,64]{0,1:T(8,128)(2,1)}, u32[]{:S(2)}) copy-start(bf16[1024,64]{0,1:T(8,128)(2,1)} %copy-done.9) | copy-start | bytes 393220
  222.3 31.4 %copy-start.4 = (bf16[1024,864]{0,1:T(8,128)(2,1)S(1)}, bf16[1024,864]{0,1:T(8,128)(2,1)}, u32[]{:S(2)}) copy-start(bf16[1024,864]{0,1:T(8,128)(2,1)} %copy-done.3) | copy-start | bytes 5308420
  222.3 2.0 collective-permute-start
  224.3 14.9 %collective-permute-start.1 = (f32[1024,128]{0,1:T(8,128)S(1)}, f32[1024,128]{0,1:T(8,128)S(1)}, u32[]{:S(2)}, u32[]{:S(2)}) collective-permute-start(f32[1024,128]{0,1:T(8,128)S(1)} %fusion.11), channel_id=1, source_target_pairs={{0,2},{1,3},{2,0},{3,1},{4,6},{5,7},{6,4},{7,5},{8,10},{9,11},{10,... | collective-permute-start | bytes 1572872 | tf_op jit(solution)/shard_map/ppermute | solution.py:44
  239.3 30.4 %copy-start.5 = (bf16[1024,320]{0,1:T(8,128)(2,1)S(1)}, bf16[1024,320]{0,1:T(8,128)(2,1)}, u32[]{:S(2)}) copy-start(bf16[1024,320]{0,1:T(8,128)(2,1)} %multiply_convert_fusion.1) | copy-start | bytes 1966084
  239.3 12.4 %collective-permute-start.2 = (f32[1024,128]{0,1:T(8,128)S(1)}, f32[1024,128]{0,1:T(8,128)S(1)}, u32[]{:S(2)}, u32[]{:S(2)}) collective-permute-start(f32[1024,128]{0,1:T(8,128)S(1)} %add.68), channel_id=1, source_target_pairs={{0,4},{1,5},{2,6},{3,7},{4,0},{5,1},{6,2},{7,3},{8,12},{9,13},{10,... | collective-permute-start | bytes 1572872 | tf_op jit(solution)/shard_map/ppermute | solution.py:44
  251.8 18.3 %copy-start.7 = (bf16[1024,320]{0,1:T(8,128)(2,1)S(1)}, bf16[1024,320]{0,1:T(8,128)(2,1)}, u32[]{:S(2)}) copy-start(bf16[1024,320]{0,1:T(8,128)(2,1)} %param.10) | copy-start | bytes 1966084
  251.8 17.8 %collective-permute-start.3 = (f32[1024,128]{0,1:T(8,128)S(1)}, f32[1024,128]{0,1:T(8,128)S(1)}, u32[]{:S(2)}, u32[]{:S(2)}) collective-permute-start(f32[1024,128]{0,1:T(8,128)S(1)} %add.69), channel_id=1, source_target_pairs={{0,8},{1,9},{2,10},{3,11},{4,12},{5,13},{6,14},{7,15},{8,0},{9,1},... | collective-permute-start | bytes 1572872 | tf_op jit(solution)/shard_map/ppermute | solution.py:44
  270.6 9.6 %collective-permute-start.4 = (f32[2368,64]{0,1:T(8,128)S(1)}, f32[2368,64]{0,1:T(8,128)S(1)}, u32[]{:S(2)}, u32[]{:S(2)}) collective-permute-start(f32[2368,64]{0,1:T(8,128)S(1)} %concatenate.7), channel_id=1, source_target_pairs={{0,16},{16,0},{32,48},{48,32},{64,80},{80,64},{96,112},{112,96},{1... | collective-permute-start | bytes 1818632 | tf_op jit(solution)/shard_map/ppermute | solution.py:44
  280.2 9.6 %collective-permute-start.5 = (f32[2368,64]{0,1:T(8,128)S(1)}, f32[2368,64]{0,1:T(8,128)S(1)}, u32[]{:S(2)}, u32[]{:S(2)}) collective-permute-start(f32[2368,64]{0,1:T(8,128)S(1)} %add.71), channel_id=1, source_target_pairs={{0,32},{16,48},{32,0},{48,16},{64,96},{80,112},{96,64},{112,80},{1... | collective-permute-start | bytes 1818632 | tf_op jit(solution)/shard_map/ppermute | solution.py:44
  289.9 15.0 %collective-permute-start.6 = (f32[2368,64]{0,1:T(8,128)S(1)}, f32[2368,64]{0,1:T(8,128)S(1)}, u32[]{:S(2)}, u32[]{:S(2)}) collective-permute-start(f32[2368,64]{0,1:T(8,128)S(1)} %add.72), channel_id=1, source_target_pairs={{0,64},{16,80},{32,96},{48,112},{64,0},{80,16},{96,32},{112,48},{1... | collective-permute-start | bytes 1818632 | tf_op jit(solution)/shard_map/ppermute | solution.py:44
  (3 other events, 3.6 us)
Sparse Core Ops, SparseCore 0:
  10.4 85.1 all-gather.4
  98.0 79.1 all-gather.2
  221.0 114.3 reduce-scatter.1

commit v2 on v1

--- a/solution.py
+++ b/solution.py
@@ -3,10 +3,12 @@
 import jax
 import jax.numpy as jnp
 from jax import lax
+from jax.sharding import Mesh
 from jax.sharding import PartitionSpec as P
 
 SLOPE_SCALE = 0.7978845608028654
 CUBIC = 0.044715
+COL = ("cc", "core")
 
 
 def gelu_value(pre):
@@ -46,6 +48,17 @@
     return value
 
 
+def core_major(rows, n_cc, n_core):
+    shape = rows.shape
+    split = rows.reshape((n_cc, n_core, shape[0] // (n_cc * n_core)) + shape[1:])
+    return jnp.swapaxes(split, 0, 1).reshape(shape)
+
+
+def gather_features(block, n_cc, n_core):
+    over_chips = lax.all_gather(block, "cc", axis=1, tiled=True)
+    return lax.all_gather(over_chips, "core", axis=1, tiled=True)
+
+
 def local(
     tokens_in,
     token_grad,
@@ -58,34 +71,41 @@
     outer_down,
     outer_up,
 ):
-    n_col = lax.axis_size("col")
+    n_cc = lax.axis_size("cc")
+    n_core = lax.axis_size("core")
+    n_col = n_cc * n_core
     n_row = lax.axis_size("row")
-    col_index = lax.axis_index("col")
+    col_index = lax.axis_index("cc") * n_core + lax.axis_index("core")
     local_width = token_grad.shape[1]
     tok_rows = tokens_in.shape[0]
     ff_local = inner_weight.shape[1]
     rank = inner_down.shape[1]
     gain_local = lax.dynamic_slice_in_dim(gate_gain, col_index * local_width, local_width, 0)
     gated_local = (gain_local[None, :] * token_grad.astype(jnp.float32)).astype(jnp.bfloat16)
-    tokens_full = lax.all_gather(tokens_in, "col", axis=1, tiled=True)
-    gated_full = lax.all_gather(gated_local, "col", axis=1, tiled=True)
-    inner_low = plain_dot(tokens_full, inner_down).astype(jnp.bfloat16)
-    forward_sum = plain_dot(tokens_full, inner_weight)
-    grad_low = dot_rows(gated_full, outer_up).astype(jnp.bfloat16)
-    backward_sum = plain_dot(gated_full, outer_weight)
+    tokens_full = gather_features(tokens_in, n_cc, n_core)
+    gated_full = gather_features(gated_local, n_cc, n_core)
+    inner_weight_p = core_major(inner_weight, n_cc, n_core)
+    outer_weight_p = core_major(outer_weight, n_cc, n_core)
+    inner_down_p = core_major(inner_down, n_cc, n_core)
+    outer_up_p = core_major(outer_up.T, n_cc, n_core)
+
+    inner_low = plain_dot(tokens_full, inner_down_p).astype(jnp.bfloat16)
+    forward_sum = plain_dot(tokens_full, inner_weight_p)
+    grad_low = plain_dot(gated_full, outer_up_p).astype(jnp.bfloat16)
+    backward_sum = plain_dot(gated_full, outer_weight_p)
     pre = forward_sum + plain_dot(inner_low, inner_up) + inner_bias[None, :]
     hidden = gelu_value(pre).astype(jnp.bfloat16)
     grad_hidden = backward_sum + dot_rows(grad_low, outer_down)
     grad_pre = (grad_hidden * gelu_slope(pre)).astype(jnp.bfloat16)
     pre_low_part = dot_rows(grad_pre, inner_up)
-    block_part = dot_rows(grad_pre, inner_weight).astype(jnp.bfloat16).astype(jnp.float32)
-    low_part = dot_rows(pre_low_part.astype(jnp.bfloat16), inner_down)
-    tokens_grad = lax.psum_scatter(
-        (block_part + low_part).astype(jnp.bfloat16), "col", scatter_dimension=1, tiled=True
-    )
+    block_part = dot_rows(grad_pre, inner_weight_p).astype(jnp.bfloat16).astype(jnp.float32)
+    low_part = dot_rows(pre_low_part.astype(jnp.bfloat16), inner_down_p)
+    summed = (block_part + low_part).astype(jnp.bfloat16)
+    on_chip = lax.psum_scatter(summed, "core", scatter_dimension=1, tiled=True)
+    tokens_grad = lax.psum_scatter(on_chip, "cc", scatter_dimension=1, tiled=True)
 
     hidden_low_part = plain_dot(hidden, outer_down)
-    lows = tree_sum(jnp.concatenate([hidden_low_part, pre_low_part], axis=1), "col", n_col)
+    lows = tree_sum(jnp.concatenate([hidden_low_part, pre_low_part], axis=1), COL, n_col)
     hidden_low = lows[:, :rank].astype(jnp.bfloat16)
     pre_low = lows[:, rank:].astype(jnp.bfloat16)
 
@@ -104,22 +124,24 @@
 
 
 def solution(mesh):
+    n_row, n_col = mesh.devices.shape
+    split = Mesh(mesh.devices.reshape(n_row, n_col // 2, 2), ("row", "cc", "core"))
     placed = (
-        P("row", "col"),
-        P("row", "col"),
+        P("row", COL),
+        P("row", COL),
         P(),
-        P(None, "col"),
-        P("col"),
-        P(None, "col"),
+        P(None, COL),
+        P(COL),
+        P(None, COL),
         P(),
-        P(None, "col"),
-        P("col", None),
+        P(None, COL),
+        P(COL, None),
         P(),
     )
     return jax.shard_map(
         local,
-        mesh=mesh,
+        mesh=split,
         in_specs=placed,
-        out_specs=(P("row", "col"), P("col", None), P(None, "col"), P("col", None), P(None, "col")),
+        out_specs=(P("row", COL), P(COL, None), P(None, COL), P(COL, None), P(None, COL)),
         check_vma=False,
     )

time: 342 us -> 454 us (1.33)
  local copies, waits for them, and re-layouts: 7.89 us -> 63 us
  waiting for transfers between devices: 248 us -> 285 us
  matrix products: 63.9 us -> 74.7 us
  starting transfers between devices: 5.81 us -> 11.6 us
    unnamed x34 -> x33, local copies, waits for them, and re-layouts: 5.36 us -> 36.6 us
    ppermute x7, waiting for transfers between devices: 74.2 us -> 101 us  [tree_sum(): value = value + lax.ppermute(value, axis, pairs)]
    transpose x0 -> x2, local copies, waits for them, and re-layouts: none -> 20.8 us  [core_major(): return jnp.swapaxes(split, 0, 1).reshape(shape)]
    all_gather x2 -> x4, waiting for transfers between devices: 144 us -> 163 us  [the longest x2 163 us: gather_features(): over_chips = lax.all_gather(block, 'cc', axis=1, tiled=True)]
    dot_general x5 -> x6, matrix products: 31.4 us -> 48.2 us  [plain_dot(): return jnp.dot(left, right, preferred_element_type=jnp.float32)]
    reduce_scatter x1, waiting for transfers between devices: 28.9 us -> 20.2 us  [local(): on_chip = lax.psum_scatter(summed, 'core', scatter_dimension=1, tiled=True)]
    dot_general x5 -> x4, matrix products: 30.4 us -> 24.6 us  [dot_rows(): lax.dot_general(left, right, (((1,), (1,)), ((), ())), preferred_element_...]
    ppermute x7, starting transfers between devices: 5.69 us -> 11.3 us  [tree_sum(): value = value + lax.ppermute(value, axis, pairs)]
  transfers between devices with their start and end apart: 10 -> 13, of which waited for: 10 -> 10; matrix products, arithmetic and copies ran while one was open for 8% -> 14% of each run, Pallas kernels for 0% -> 0%
where the time goes in v2:
time: 454 us; the launch traced here: 451 us
  waiting for transfers between devices  285 us (63%)
  matrix products  74.7 us (16%)
  local copies, waits for them, and re-layouts  63 us (14%)
  between operations  14.5 us (3%)
  starting transfers between devices  11.6 us (3%)
    all_gather x2, waiting for transfers between devices, gather_features(): over_chips = lax.all_gather(block, 'cc', axis=1, tiled=True)  163 us
    ppermute x7, waiting for transfers between devices, tree_sum(): value = value + lax.ppermute(value, axis, pairs)  101 us
    dot_general x6, matrix products, plain_dot(): return jnp.dot(left, right, preferred_element_type=jnp.float32)  48.2 us
    unnamed x33, local copies, waits for them, and re-layouts  36.6 us
    dot_general x4, matrix products, dot_rows(): lax.dot_general(left, right, (((1,), (1,)), ((), ())), preferred_element_...  24.6 us
    transpose x2, local copies, waits for them, and re-layouts, core_major(): return jnp.swapaxes(split, 0, 1).reshape(shape)  20.8 us
    reduce_scatter x1, waiting for transfers between devices, local(): on_chip = lax.psum_scatter(summed, 'core', scatter_dimension=1, tiled=True)  20.2 us
    ppermute x7, starting transfers between devices, tree_sum(): value = value + lax.ppermute(value, axis, pairs)  11.3 us
  transfers between devices with their start and end apart: 13, of which 10 were waited for; matrix products, arithmetic and copies ran while one was open for 14% of the time, Pallas kernels for 0%

profile of v2, /device:TPU:1, one launch (start us, length us, event | category | flops | bytes accessed | tf_op | source)
XLA Modules:
  0.0 451.3 jit_solution(1446664084841437667)
XLA Ops:
  10.9 82.6 %all-gather.5.cloned.1.call-done = bf16[1024,2560]{0,1:T(8,128)(2,1)} async-done(((bf16[1024,320]{0,1:T(8,128)(2,1)}), bf16[1024,2560]{0,1:T(8,128)(2,1)}) %all-gather.5.cloned.1.call-update) | async-done | bytes 5242896 | tf_op jit(solution)/shard_map/all_gather | solution.py:58
  93.6 80.3 %all-gather.9.cloned.1.call-done = bf16[1024,2560]{0,1:T(8,128)(2,1)} async-done(((bf16[1024,320]{0,1:T(8,128)(2,1)}), bf16[1024,2560]{0,1:T(8,128)(2,1)}) %all-gather.9.cloned.1.call-update) | async-done | bytes 5242896 | tf_op jit(solution)/shard_map/all_gather | solution.py:58
  177.2 13.6 %copy.26 = bf16[5120,864]{1,0:T(8,128)(2,1)} copy(bf16[5120,864]{0,1:T(8,128)(2,1)} %param.13) | data formatting | bytes 17694720 | tf_op args[3]
  190.8 9.7 %copy.27 = bf16[2,8,320,864]{3,2,1,0:T(8,128)(2,1)} copy(bf16[2,8,320,864]{3,2,0,1:T(8,128)(2,1)} %bitcast.60) | data formatting | bytes 17694720 | tf_op jit(solution)/shard_map/transpose | solution.py:54
  200.6 12.8 %copy.23 = bf16[5120,864]{1,0:T(8,128)(2,1)} copy(bf16[5120,864]{0,1:T(8,128)(2,1)} %param.15) | data formatting | bytes 17694720 | tf_op args[5]
  213.4 11.0 %copy.24 = bf16[2,8,320,864]{3,2,1,0:T(8,128)(2,1)} copy(bf16[2,8,320,864]{3,2,0,1:T(8,128)(2,1)} %bitcast.61) | data formatting | bytes 17694720 | tf_op jit(solution)/shard_map/transpose | solution.py:54
  224.4 5.9 %convolution_convert_fusion.1 = bf16[1024,64]{0,1:T(8,128)(2,1)S(1)} fusion(bf16[5120,64]{0,1:T(8,128)(2,1)S(1)} %reshape.39, bf16[1024,5120]{0,1:T(8,128)(2,1)} %all-gather.7.cloned.1.call-done), kind=kOutput, calls=%fused_computation.14 | convolution fusion | flops 671154176 | bytes 11272192 | tf_op jit(solution)/shard_map/dot_general | solution.py:27
  230.4 2.4 fusion.13
  232.9 5.9 %convolution_convert_fusion = bf16[1024,64]{0,1:T(8,128)(2,1)S(1)} fusion(bf16[5120,64]{0,1:T(8,128)(2,1)S(1)} %reshape.43, bf16[1024,5120]{0,1:T(8,128)(2,1)} %all-gather.11.cloned.1.call-done), kind=kOutput, calls=%fused_computation.13 | convolution fusion | flops 671154176 | bytes 11272192 | tf_op jit(solution)/shard_map/dot_general | solution.py:27
  239.5 17.1 %multiply_convert_fusion = (bf16[1024,864]{0,1:T(8,128)(2,1)S(1)}, f32[1024,864]{0,1:T(8,128)}) fusion(f32[864]{0:T(1024)S(1)} %copy-done.14, f32[1024,864]{0,1:T(8,128)S(1)} %fusion.14, bf16[1024,5120]{0,1:T(8,128)(2,1)} %all-gather.11.cloned.1.call-done, bf16[5120,864]{1,0:T(8,128)(2,1)} %bitcast.63), kind=kOutput, calls=%fused_computation.10 | convolution fusion | flops 9069428736 | bytes 28183936 | tf_op jit(solution)/shard_map/dot_general | solution.py:27
  256.6 18.2 %fusion.6 = bf16[1024,864]{0,1:T(8,128)(2,1)S(1)} fusion(f32[1024,864]{0,1:T(8,128)} %get-tuple-element.25, f32[1024,864]{0,1:T(8,128)} %fusion.13, bf16[1024,5120]{0,1:T(8,128)(2,1)} %all-gather.7.cloned.1.call-done, bf16[5120,864]{1,0:T(8,128)(2,1)} %bitcast.65), kind=kOutput, calls=%fused_computation.9 | convolution fusion | flops 9077391360 | bytes 28180480 | tf_op jit(solution)/shard_map/dot_general | solution.py:27
  277.2 14.2 %fusion.15 = bf16[1024,5120]{1,0:T(8,128)(2,1)S(1)} fusion(bf16[1024,864]{0,1:T(8,128)(2,1)} %copy-done.1, bf16[5120,864]{1,0:T(8,128)(2,1)} %bitcast.64), kind=kOutput, calls=%fused_computation.31 | convolution fusion | flops 9059696640 | bytes 21102592 | tf_op jit(solution)/shard_map/dot_general | solution.py:31
  291.4 6.7 %add_convert_fusion = bf16[1024,5120]{1,0:T(8,128)(2,1)} fusion(bf16[5120,64]{0,1:T(8,128)(2,1)S(1)} %reshape.43, bf16[1024,5120]{1,0:T(8,128)(2,1)S(1)} %fusion.15, f32[1024,64]{0,1:T(8,128)} %fusion.18), kind=kOutput, calls=%fused_computation | convolution fusion | flops 686882816 | bytes 21889024 | tf_op jit(solution)/shard_map/dot_general | solution.py:31
  298.2 20.2 %reduce-scatter.5.cloned.1.call-done = bf16[1024,2560]{1,0:T(8,128)(2,1)} async-done(((bf16[1024,5120]{1,0:T(8,128)(2,1)}), bf16[1024,2560]{1,0:T(8,128)(2,1)}) %reduce-scatter.5.cloned.1.call-update) | async-done | bytes 5242896 | tf_op jit(solution)/shard_map/reduce_scatter | solution.py:104
  318.4 8.0 %copy.30 = bf16[1024,2560]{0,1:T(8,128)(2,1)} copy(bf16[1024,2560]{1,0:T(8,128)(2,1)} %reduce-scatter.5.cloned.1.call-done) | data formatting | bytes 10485760
  329.8 3.1 collective-permute-start.1
  332.9 18.1 %collective-permute-done.1 = f32[1024,128]{0,1:T(8,128)S(1)} collective-permute-done((f32[1024,128]{0,1:T(8,128)S(1)}, f32[1024,128]{0,1:T(8,128)S(1)}, u32[]{:S(2)}, u32[]{:S(2)}) %collective-permute-start.1) | collective-permute-done | bytes 524320 | tf_op jit(solution)/shard_map/ppermute | solution.py:46
  352.2 21.6 %collective-permute-done.2 = f32[1024,128]{0,1:T(8,128)S(1)} collective-permute-done((f32[1024,128]{0,1:T(8,128)S(1)}, f32[1024,128]{0,1:T(8,128)S(1)}, u32[]{:S(2)}, u32[]{:S(2)}) %collective-permute-start.2) | collective-permute-done | bytes 524320 | tf_op jit(solution)/shard_map/ppermute | solution.py:46
  373.9 2.5 collective-permute-start.3
  377.7 14.6 %collective-permute-done.3 = f32[1024,128]{0,1:T(8,128)S(1)} collective-permute-done((f32[1024,128]{0,1:T(8,128)S(1)}, f32[1024,128]{0,1:T(8,128)S(1)}, u32[]{:S(2)}, u32[]{:S(2)}) %collective-permute-start.3) | collective-permute-done | bytes 524320 | tf_op jit(solution)/shard_map/ppermute | solution.py:46
  393.5 19.4 %collective-permute-done.4 = f32[2368,64]{0,1:T(8,128)S(1)} collective-permute-done((f32[2368,64]{0,1:T(8,128)S(1)}, f32[2368,64]{0,1:T(8,128)S(1)}, u32[]{:S(2)}, u32[]{:S(2)}) %collective-permute-start.4) | collective-permute-done | bytes 606240 | tf_op jit(solution)/shard_map/ppermute | solution.py:46
  414.4 13.2 %collective-permute-done.5 = f32[2368,64]{0,1:T(8,128)S(1)} collective-permute-done((f32[2368,64]{0,1:T(8,128)S(1)}, f32[2368,64]{0,1:T(8,128)S(1)}, u32[]{:S(2)}, u32[]{:S(2)}) %collective-permute-start.5) | collective-permute-done | bytes 606240 | tf_op jit(solution)/shard_map/ppermute | solution.py:46
  427.6 2.9 collective-permute-start.6
  430.6 12.3 %collective-permute-done.6 = f32[2368,64]{0,1:T(8,128)S(1)} collective-permute-done((f32[2368,64]{0,1:T(8,128)S(1)}, f32[2368,64]{0,1:T(8,128)S(1)}, u32[]{:S(2)}, u32[]{:S(2)}) %collective-permute-start.6) | collective-permute-done | bytes 606240 | tf_op jit(solution)/shard_map/ppermute | solution.py:46
  (76 shorter events, 20.5 us)
Async XLA Ops:
  7.2 231.6 %copy-start = (bf16[64,864]{1,0:T(8,128)(2,1)S(1)}, bf16[64,864]{1,0:T(8,128)(2,1)}, u32[]{:S(2)}) copy-start(bf16[64,864]{1,0:T(8,128)(2,1)} %param.17) | copy-start | bytes 331780
  7.2 86.3 %all-gather.5.cloned.1.call-start = ((), (), s32[]{:S(2)}) async-start(), calls=%async_computation.2 | async-start | bytes 5898240 | tf_op jit(solution)/shard_map/all_gather | solution.py:58
  10.1 163.8 %all-gather.9.cloned.1.call-start = ((), (), s32[]{:S(2)}) async-start(), calls=%async_computation.4 | async-start | bytes 5898240 | tf_op jit(solution)/shard_map/all_gather | solution.py:58
  10.9 213.5 %all-gather.7.cloned.1.call-start = ((), (), s32[]{:S(2)}) async-start(), calls=%async_computation.3 | async-start | bytes 15728640 | tf_op jit(solution)/shard_map/all_gather | solution.py:59
  93.5 80.5 %copy-start.10 = (bf16[5120,64]{0,1:T(8,128)(2,1)S(1)}, bf16[5120,64]{0,1:T(8,128)(2,1)}, u32[]{:S(2)}) copy-start(bf16[5120,64]{0,1:T(8,128)(2,1)} %param.16) | copy-start | bytes 1966084
  93.6 139.3 %all-gather.11.cloned.1.call-start = ((), (), s32[]{:S(2)}) async-start(), calls=%async_computation.5 | async-start | bytes 15728640 | tf_op jit(solution)/shard_map/all_gather | solution.py:59
  173.9 1.7 copy-start.11
  174.0 144.5 %reduce-scatter.5.cloned.1.call-start = ((), (), s32[]{:S(2)}) async-start(), calls=%async_computation.6 | async-start | bytes 15728640 | tf_op jit(solution)/shard_map/reduce_scatter | solution.py:104
  224.4 6.0 %copy-start.12 = (bf16[864,64]{0,1:T(8,128)(2,1)S(1)}, bf16[864,64]{0,1:T(8,128)(2,1)}, u32[]{:S(2)}) copy-start(bf16[864,64]{0,1:T(8,128)(2,1)} %param.18) | copy-start | bytes 331780
  230.4 8.4 %copy-start.6 = (bf16[1024,64]{0,1:T(8,128)(2,1)}, bf16[1024,64]{0,1:T(8,128)(2,1)S(1)}, u32[]{:S(2)}) copy-start(bf16[1024,64]{0,1:T(8,128)(2,1)S(1)} %convolution_convert_fusion.1) | copy-start | bytes 393220
  238.8 17.8 %copy-start.8 = (bf16[1024,64]{0,1:T(8,128)(2,1)}, bf16[1024,64]{0,1:T(8,128)(2,1)S(1)}, u32[]{:S(2)}) copy-start(bf16[1024,64]{0,1:T(8,128)(2,1)S(1)} %convolution_convert_fusion) | copy-start | bytes 393220
  298.1 146.3 %reduce-scatter.7.cloned.1.call-start = ((), (), s32[]{:S(2)}) async-start(), calls=%async_computation.7 | async-start | bytes 5898240
  327.3 49.1 %copy-start.7 = (bf16[1024,64]{0,1:T(8,128)(2,1)S(1)}, bf16[1024,64]{0,1:T(8,128)(2,1)}, u32[]{:S(2)}) copy-start(bf16[1024,64]{0,1:T(8,128)(2,1)} %copy-done.6) | copy-start | bytes 393220
  327.8 49.3 %copy-start.2 = (bf16[1024,864]{0,1:T(8,128)(2,1)S(1)}, bf16[1024,864]{0,1:T(8,128)(2,1)}, u32[]{:S(2)}) copy-start(bf16[1024,864]{0,1:T(8,128)(2,1)} %copy-done.1) | copy-start | bytes 5308420
  327.8 49.3 %copy-start.9 = (bf16[1024,64]{0,1:T(8,128)(2,1)S(1)}, bf16[1024,64]{0,1:T(8,128)(2,1)}, u32[]{:S(2)}) copy-start(bf16[1024,64]{0,1:T(8,128)(2,1)} %copy-done.8) | copy-start | bytes 393220
  327.8 2.0 collective-permute-start
  329.8 21.1 %collective-permute-start.1 = (f32[1024,128]{0,1:T(8,128)S(1)}, f32[1024,128]{0,1:T(8,128)S(1)}, u32[]{:S(2)}, u32[]{:S(2)}) collective-permute-start(f32[1024,128]{0,1:T(8,128)S(1)} %fusion.11), channel_id=1, source_target_pairs={{0,2},{1,3},{2,0},{3,1},{4,6},{5,7},{6,4},{7,5},{8,10},{9,11},{10,... | collective-permute-start | bytes 1572872 | tf_op jit(solution)/shard_map/ppermute | solution.py:46
  351.0 41.4 %copy-start.4 = (bf16[1024,320]{0,1:T(8,128)(2,1)S(1)}, bf16[1024,320]{0,1:T(8,128)(2,1)}, u32[]{:S(2)}) copy-start(bf16[1024,320]{0,1:T(8,128)(2,1)} %multiply_convert_fusion.1) | copy-start | bytes 1966084
  351.0 22.7 %collective-permute-start.2 = (f32[1024,128]{0,1:T(8,128)S(1)}, f32[1024,128]{0,1:T(8,128)S(1)}, u32[]{:S(2)}, u32[]{:S(2)}) collective-permute-start(f32[1024,128]{0,1:T(8,128)S(1)} %add.74), channel_id=1, source_target_pairs={{0,4},{1,5},{2,6},{3,7},{4,0},{5,1},{6,2},{7,3},{8,12},{9,13},{10,... | collective-permute-start | bytes 1572872 | tf_op jit(solution)/shard_map/ppermute | solution.py:46
  373.9 18.9 %copy-start.5 = (bf16[1024,320]{0,1:T(8,128)(2,1)S(1)}, bf16[1024,320]{0,1:T(8,128)(2,1)}, u32[]{:S(2)}) copy-start(bf16[1024,320]{0,1:T(8,128)(2,1)} %param.10) | copy-start | bytes 1966084
  373.9 18.4 %collective-permute-start.3 = (f32[1024,128]{0,1:T(8,128)S(1)}, f32[1024,128]{0,1:T(8,128)S(1)}, u32[]{:S(2)}, u32[]{:S(2)}) collective-permute-start(f32[1024,128]{0,1:T(8,128)S(1)} %add.75), channel_id=1, source_target_pairs={{0,8},{1,9},{2,10},{3,11},{4,12},{5,13},{6,14},{7,15},{8,0},{9,1},... | collective-permute-start | bytes 1572872 | tf_op jit(solution)/shard_map/ppermute | solution.py:46
  393.3 19.6 %collective-permute-start.4 = (f32[2368,64]{0,1:T(8,128)S(1)}, f32[2368,64]{0,1:T(8,128)S(1)}, u32[]{:S(2)}, u32[]{:S(2)}) collective-permute-start(f32[2368,64]{0,1:T(8,128)S(1)} %concatenate.7), channel_id=1, source_target_pairs={{0,16},{16,0},{32,48},{48,32},{64,80},{80,64},{96,112},{112,96},{1... | collective-permute-start | bytes 1818632 | tf_op jit(solution)/shard_map/ppermute | solution.py:46
  413.0 14.6 %collective-permute-start.5 = (f32[2368,64]{0,1:T(8,128)S(1)}, f32[2368,64]{0,1:T(8,128)S(1)}, u32[]{:S(2)}, u32[]{:S(2)}) collective-permute-start(f32[2368,64]{0,1:T(8,128)S(1)} %add.77), channel_id=1, source_target_pairs={{0,32},{16,48},{32,0},{48,16},{64,96},{80,112},{96,64},{112,80},{1... | collective-permute-start | bytes 1818632 | tf_op jit(solution)/shard_map/ppermute | solution.py:46
  427.6 15.2 %collective-permute-start.6 = (f32[2368,64]{0,1:T(8,128)S(1)}, f32[2368,64]{0,1:T(8,128)S(1)}, u32[]{:S(2)}, u32[]{:S(2)}) collective-permute-start(f32[2368,64]{0,1:T(8,128)S(1)} %add.78), channel_id=1, source_target_pairs={{0,64},{16,80},{32,96},{48,112},{64,0},{80,16},{96,32},{112,48},{1... | collective-permute-start | bytes 1818632 | tf_op jit(solution)/shard_map/ppermute | solution.py:46
  (4 other events, 4.2 us)
Sparse Core Ops, SparseCore 0:
  10.3 83.1 all-gather.4
  95.8 78.0 all-gather.8
  175.6 24.0 all-gather.6
  201.2 26.8 all-gather.10
  298.3 20.0 reduce-scatter.4
  326.5 115.5 reduce-scatter.6

commit v3 on v1

--- a/solution.py
+++ b/solution.py
@@ -1,9 +1,14 @@
+import functools
 import math
 
 import jax
 import jax.numpy as jnp
 from jax import lax
+from jax.experimental import pallas as pl
+from jax.experimental.pallas import tpu as pltpu
 from jax.sharding import PartitionSpec as P
+
+MESH = pl.DeviceIdType.MESH
 
 SLOPE_SCALE = 0.7978845608028654
 CUBIC = 0.044715
@@ -46,6 +51,62 @@
     return value
 
 
+def gather_kernel(n, x_ref, out_ref, own_sem, send_sem, recv_sem):
+    me = lax.axis_index("col")
+    row = lax.axis_index("row")
+    barrier = pltpu.get_barrier_semaphore()
+    for k in range(1, n):
+        peer = lax.rem(me + k, n)
+        pl.semaphore_signal(barrier, inc=1, device_id=(row, peer), device_id_type=MESH)
+    pl.semaphore_wait(barrier, n - 1)
+    own = pltpu.make_async_copy(x_ref, out_ref.at[me], own_sem)
+    own.start()
+    sends = []
+    for k in range(1, n):
+        peer = lax.rem(me + k, n)
+        copy = pltpu.make_async_remote_copy(
+            src_ref=x_ref,
+            dst_ref=out_ref.at[me],
+            send_sem=send_sem.at[k],
+            recv_sem=recv_sem.at[k],
+            device_id=(row, peer),
+            device_id_type=MESH,
+        )
+        copy.start()
+        sends.append(copy)
+    own.wait()
+    for copy in sends:
+        copy.wait_send()
+    for k in range(1, n):
+        source = lax.rem(me + n - k, n)
+        pltpu.make_async_remote_copy(
+            src_ref=x_ref,
+            dst_ref=out_ref.at[source],
+            send_sem=send_sem.at[k],
+            recv_sem=recv_sem.at[k],
+            device_id=(row, source),
+            device_id_type=MESH,
+        ).wait_recv()
+
+
+def gather_blocks(block, n, collective_id):
+    rows, width = block.shape
+    nbytes = rows * width * block.dtype.itemsize
+    return pl.pallas_call(
+        functools.partial(gather_kernel, n),
+        out_shape=jax.ShapeDtypeStruct((n, rows, width), block.dtype),
+        in_specs=[pl.BlockSpec(memory_space=pltpu.VMEM)],
+        out_specs=pl.BlockSpec(memory_space=pl.ANY),
+        scratch_shapes=[
+            pltpu.SemaphoreType.DMA(()),
+            pltpu.SemaphoreType.DMA((n,)),
+            pltpu.SemaphoreType.DMA((n,)),
+        ],
+        compiler_params=pltpu.CompilerParams(collective_id=collective_id, has_side_effects=True),
+        cost_estimate=pl.CostEstimate(flops=0, transcendentals=0, bytes_accessed=2 * n * nbytes),
+    )(block)
+
+
 def local(
     tokens_in,
     token_grad,
@@ -67,7 +128,8 @@
     rank = inner_down.shape[1]
     gain_local = lax.dynamic_slice_in_dim(gate_gain, col_index * local_width, local_width, 0)
     gated_local = (gain_local[None, :] * token_grad.astype(jnp.float32)).astype(jnp.bfloat16)
-    tokens_full = lax.all_gather(tokens_in, "col", axis=1, tiled=True)
+    tokens_blocks = gather_blocks(tokens_in, n_col, 0)
+    tokens_full = jnp.swapaxes(tokens_blocks, 0, 1).reshape(tok_rows, n_col * local_width)
     gated_full = lax.all_gather(gated_local, "col", axis=1, tiled=True)
     inner_low = plain_dot(tokens_full, inner_down).astype(jnp.bfloat16)
     forward_sum = plain_dot(tokens_full, inner_weight)

time: 342 us -> 451 us (1.32)
  Pallas kernels: 0 us -> 211 us
  waiting for transfers between devices: 248 us -> 99.6 us
  starting transfers between devices: 5.81 us -> 36 us
  local copies, waits for them, and re-layouts: 7.89 us -> 22.5 us
    pallas_call x0 -> x1, Pallas kernels: none -> 211 us  [gather_blocks(): pl.pallas_call(functools.partial(gather_kernel, n), out_shape=jax.ShapeDt...]
    all_gather x1 -> x0, waiting for transfers between devices: 84.7 us -> none  [local(): tokens_full = lax.all_gather(tokens_in, 'col', axis=1, tiled=True)]
    all_gather x1, waiting for transfers between devices: 59.2 us -> 0.01 us  [local(): gated_full = lax.all_gather(gated_local, 'col', axis=1, tiled=True)]
    ppermute x7, starting transfers between devices: 5.69 us -> 35.9 us  [tree_sum(): value = value + lax.ppermute(value, axis, pairs)]
    transpose x0 -> x1, local copies, waits for them, and re-layouts: none -> 15.2 us  [local(): jnp.swapaxes(tokens_blocks, 0, 1).reshape(tok_rows, n_col * local_width)]
    reduce_scatter x1, waiting for transfers between devices: 28.9 us -> 22.9 us  [local(): lax.psum_scatter((block_part + low_part).astype(jnp.bfloat16), 'col', sca...]
  transfers between devices with their start and end apart: 10 -> 9, of which waited for: 10 -> 8; matrix products, arithmetic and copies ran while one was open for 8% -> 10% of each run, Pallas kernels for 0% -> 47%
where the time goes in v3:
time: 451 us
  Pallas kernels  211 us (47%)
  waiting for transfers between devices  99.6 us (22%)
  matrix products  64.1 us (14%)
  starting transfers between devices  36 us (8%)
  local copies, waits for them, and re-layouts  22.5 us (5%)
  between operations  14.4 us (3%)
    pallas_call x1, Pallas kernels, gather_blocks(): pl.pallas_call(functools.partial(gather_kernel, n), out_shape=jax.ShapeDt...  211 us
    ppermute x7, waiting for transfers between devices, tree_sum(): value = value + lax.ppermute(value, axis, pairs)  76.7 us
    ppermute x7, starting transfers between devices, tree_sum(): value = value + lax.ppermute(value, axis, pairs)  35.9 us
    dot_general x5, matrix products, plain_dot(): return jnp.dot(left, right, preferred_element_type=jnp.float32)  35.5 us
    dot_general x5, matrix products, dot_rows(): lax.dot_general(left, right, (((1,), (1,)), ((), ())), preferred_element_...  26.6 us
    reduce_scatter x1, waiting for transfers between devices, local(): lax.psum_scatter((block_part + low_part).astype(jnp.bfloat16), 'col', sca...  22.9 us
    transpose x1, local copies, waits for them, and re-layouts, local(): jnp.swapaxes(tokens_blocks, 0, 1).reshape(tok_rows, n_col * local_width)  15.2 us
  transfers between devices with their start and end apart: 9, of which 8 were waited for; matrix products, arithmetic and copies ran while one was open for 10% of the time, Pallas kernels for 47%

profile of v3, /device:TPU:1, one launch (start us, length us, event | category | flops | bytes accessed | tf_op | source)
XLA Modules:
  0.0 450.6 jit_solution(15888912244602885499)
XLA Ops:
  8.1 2.1 multiply_convert_fusion.1
  10.3 2.2 copy.16.x_ref
  12.5 211.4 %shard_map.137 = bf16[16,1024,320]{2,1,0:T(8,128)(2,1)} custom-call(bf16[1024,320]{1,0:T(8,128)(2,1)} %copy.16.x_ref), custom_call_target="tpu_custom_call" | custom-call | bytes 20971520 | tf_op jit(solution)/shard_map/pallas_call | solution.py:95
  223.9 15.2 %copy.17 = bf16[1024,16,320]{0,2,1:T(8,128)(2,1)} copy(bf16[1024,16,320]{2,0,1:T(8,128)(2,1)} %bitcast.35) | data formatting | bytes 20971520 | tf_op jit(solution)/shard_map/transpose | solution.py:132
  239.1 6.2 %convolution_convert_fusion = bf16[1024,64]{0,1:T(8,128)(2,1)S(1)} fusion(bf16[5120,64]{0,1:T(8,128)(2,1)S(1)} %copy-done, bf16[1024,5120]{0,1:T(8,128)(2,1)} %bitcast.33), kind=kOutput, calls=%fused_computation.13 | convolution fusion | flops 671154176 | bytes 11272192 | tf_op jit(solution)/shard_map/dot_general | solution.py:30
  246.2 12.0 %fusion.17 = f32[1024,864]{0,1:T(8,128)S(1)} fusion(bf16[5120,864]{0,1:T(8,128)(2,1)} %param.13, bf16[1024,5120]{0,1:T(8,128)(2,1)S(1)} %bitcast.34), kind=kOutput, calls=%fused_computation.31 | convolution fusion | flops 9059696640 | bytes 22872064 | tf_op jit(solution)/shard_map/dot_general | solution.py:30
  258.3 3.3 multiply_convert_fusion
  261.6 13.6 %fusion.16 = f32[1024,864]{0,1:T(8,128)S(1)} fusion(bf16[5120,864]{0,1:T(8,128)(2,1)} %param.15, bf16[1024,5120]{0,1:T(8,128)(2,1)} %all-gather.2.cloned.1.call-done), kind=kOutput, calls=%fused_computation.30 | convolution fusion | flops 9059696640 | bytes 22872064 | tf_op jit(solution)/shard_map/dot_general | solution.py:30
  275.2 2.0 convolution_convert_fusion.1
  277.8 2.6 fusion.6
  280.5 14.3 %fusion.13 = bf16[1024,5120]{0,1:T(8,128)(2,1)S(1)} fusion(bf16[1024,864]{0,1:T(8,128)(2,1)S(1)} %fusion.6, bf16[5120,864]{0,1:T(8,128)(2,1)} %param.13), kind=kOutput, calls=%fused_computation.27 | convolution fusion | flops 9059696640 | bytes 21102592 | tf_op jit(solution)/shard_map/dot_general | solution.py:34
  296.0 6.5 %add_convert_fusion = bf16[1024,5120]{0,1:T(8,128)(2,1)} fusion(bf16[5120,64]{0,1:T(8,128)(2,1)S(1)} %copy-done, bf16[1024,5120]{0,1:T(8,128)(2,1)S(1)} %fusion.13, f32[1024,64]{0,1:T(8,128)} %fusion.18), kind=kOutput, calls=%fused_computation | convolution fusion | flops 686882816 | bytes 21889024 | tf_op jit(solution)/shard_map/dot_general | solution.py:34
  304.0 1.8 collective-permute-start
  305.8 1.5 collective-permute-done
  307.4 25.5 %collective-permute-start.1 = (f32[1024,128]{0,1:T(8,128)S(1)}, f32[1024,128]{0,1:T(8,128)S(1)}, u32[]{:S(2)}, u32[]{:S(2)}) collective-permute-start(f32[1024,128]{0,1:T(8,128)S(1)} %fusion.11), channel_id=1, source_target_pairs={{0,2},{1,3},{2,0},{3,1},{4,6},{5,7},{6,4},{7,5},{8,10},{9,11},{10,... | collective-permute-start | bytes 1572872 | tf_op jit(solution)/shard_map/ppermute | solution.py:49
  332.9 12.0 %collective-permute-done.1 = f32[1024,128]{0,1:T(8,128)S(1)} collective-permute-done((f32[1024,128]{0,1:T(8,128)S(1)}, f32[1024,128]{0,1:T(8,128)S(1)}, u32[]{:S(2)}, u32[]{:S(2)}) %collective-permute-start.1) | collective-permute-done | bytes 524320 | tf_op jit(solution)/shard_map/ppermute | solution.py:49
  345.1 12.5 %collective-permute-done.2 = f32[1024,128]{0,1:T(8,128)S(1)} collective-permute-done((f32[1024,128]{0,1:T(8,128)S(1)}, f32[1024,128]{0,1:T(8,128)S(1)}, u32[]{:S(2)}, u32[]{:S(2)}) %collective-permute-start.2) | collective-permute-done | bytes 524320 | tf_op jit(solution)/shard_map/ppermute | solution.py:49
  357.7 4.0 collective-permute-start.3
  363.0 13.0 %collective-permute-done.3 = f32[1024,128]{0,1:T(8,128)S(1)} collective-permute-done((f32[1024,128]{0,1:T(8,128)S(1)}, f32[1024,128]{0,1:T(8,128)S(1)}, u32[]{:S(2)}, u32[]{:S(2)}) %collective-permute-start.3) | collective-permute-done | bytes 524320 | tf_op jit(solution)/shard_map/ppermute | solution.py:49
  377.1 14.8 %collective-permute-done.4 = f32[2368,64]{0,1:T(8,128)S(1)} collective-permute-done((f32[2368,64]{0,1:T(8,128)S(1)}, f32[2368,64]{0,1:T(8,128)S(1)}, u32[]{:S(2)}, u32[]{:S(2)}) %collective-permute-start.4) | collective-permute-done | bytes 606240 | tf_op jit(solution)/shard_map/ppermute | solution.py:49
  393.4 9.4 %collective-permute-done.5 = f32[2368,64]{0,1:T(8,128)S(1)} collective-permute-done((f32[2368,64]{0,1:T(8,128)S(1)}, f32[2368,64]{0,1:T(8,128)S(1)}, u32[]{:S(2)}, u32[]{:S(2)}) %collective-permute-start.5) | collective-permute-done | bytes 606240 | tf_op jit(solution)/shard_map/ppermute | solution.py:49
  402.8 3.0 collective-permute-start.6
  405.8 13.4 %collective-permute-done.6 = f32[2368,64]{0,1:T(8,128)S(1)} collective-permute-done((f32[2368,64]{0,1:T(8,128)S(1)}, f32[2368,64]{0,1:T(8,128)S(1)}, u32[]{:S(2)}, u32[]{:S(2)}) %collective-permute-start.6) | collective-permute-done | bytes 606240 | tf_op jit(solution)/shard_map/ppermute | solution.py:49
  420.9 22.9 %reduce-scatter.2.cloned.1.call-done = bf16[1024,320]{0,1:T(8,128)(2,1)} async-done(((bf16[1024,5120]{0,1:T(8,128)(2,1)}), bf16[1024,320]{0,1:T(8,128)(2,1)}) %reduce-scatter.2.cloned.1.call-update) | async-done | bytes 655376 | tf_op jit(solution)/shard_map/reduce_scatter | solution.py:145
  (60 shorter events, 10.9 us)
Async XLA Ops:
  7.2 232.0 %copy-start = (bf16[5120,64]{0,1:T(8,128)(2,1)S(1)}, bf16[5120,64]{0,1:T(8,128)(2,1)}, u32[]{:S(2)}) copy-start(bf16[5120,64]{0,1:T(8,128)(2,1)} %param.16) | copy-start | bytes 1966084
  7.2 254.4 %all-gather.2.cloned.1.call-start = ((), (), s32[]{:S(2)}) async-start(), calls=%async_computation.1 | async-start | bytes 11141120 | tf_op jit(solution)/shard_map/all_gather | solution.py:133
  10.2 433.6 %reduce-scatter.2.cloned.1.call-start = ((), (), s32[]{:S(2)}) async-start(), calls=%async_computation.2 | async-start | bytes 11141120 | tf_op jit(solution)/shard_map/reduce_scatter | solution.py:145
  239.1 7.1 %copy-start.1 = (bf16[1024,16,320]{0,2,1:T(8,128)(2,1)S(1)}, bf16[1024,16,320]{0,2,1:T(8,128)(2,1)}, u32[]{:S(2)}) copy-start(bf16[1024,16,320]{0,2,1:T(8,128)(2,1)} %copy.17) | copy-start | bytes 31457284
  246.2 12.0 %copy-start.11 = (bf16[64,864]{1,0:T(8,128)(2,1)S(1)}, bf16[64,864]{1,0:T(8,128)(2,1)}, u32[]{:S(2)}) copy-start(bf16[64,864]{1,0:T(8,128)(2,1)} %param.17) | copy-start | bytes 331780
  246.2 12.0 %copy-start.15 = (f32[864]{0:T(1024)S(1)}, f32[864]{0:T(1024)}, u32[]{:S(2)}) copy-start(f32[864]{0:T(1024)} %param.14) | copy-start | bytes 10372
  261.6 13.6 %copy-start.8 = (bf16[64,5120]{1,0:T(8,128)(2,1)S(1)}, bf16[64,5120]{1,0:T(8,128)(2,1)}, u32[]{:S(2)}) copy-start(bf16[64,5120]{1,0:T(8,128)(2,1)} %param.19) | copy-start | bytes 1966084
  261.6 13.6 %copy-start.2 = (bf16[1024,5120]{0,1:T(8,128)(2,1)S(1)}, bf16[1024,5120]{0,1:T(8,128)(2,1)}, u32[]{:S(2)}) copy-start(bf16[1024,5120]{0,1:T(8,128)(2,1)} %all-gather.2.cloned.1.call-done) | copy-start | bytes 31457284
  275.2 2.7 copy-start.13
  275.2 2.7 copy-start.16
  280.5 14.3 %copy-start.3 = (bf16[1024,864]{0,1:T(8,128)(2,1)}, bf16[1024,864]{0,1:T(8,128)(2,1)S(1)}, u32[]{:S(2)}) copy-start(bf16[1024,864]{0,1:T(8,128)(2,1)S(1)} %fusion.6) | copy-start | bytes 5308420
  280.5 14.3 %copy-start.12 = (bf16[64,864]{1,0:T(8,128)(2,1)S(1)}, bf16[64,864]{1,0:T(8,128)(2,1)}, u32[]{:S(2)}) copy-start(bf16[64,864]{1,0:T(8,128)(2,1)} %param.17) | copy-start | bytes 331780
  302.6 1.3 copy-start.6
  303.4 58.2 %copy-start.10 = (bf16[1024,64]{0,1:T(8,128)(2,1)S(1)}, bf16[1024,64]{0,1:T(8,128)(2,1)}, u32[]{:S(2)}) copy-start(bf16[1024,64]{0,1:T(8,128)(2,1)} %copy-done.9) | copy-start | bytes 393220
  303.9 58.4 %copy-start.4 = (bf16[1024,864]{0,1:T(8,128)(2,1)S(1)}, bf16[1024,864]{0,1:T(8,128)(2,1)}, u32[]{:S(2)}) copy-start(bf16[1024,864]{0,1:T(8,128)(2,1)} %copy-done.3) | copy-start | bytes 5308420
  304.0 3.4 collective-permute-start
  307.4 37.5 %collective-permute-start.1 = (f32[1024,128]{0,1:T(8,128)S(1)}, f32[1024,128]{0,1:T(8,128)S(1)}, u32[]{:S(2)}, u32[]{:S(2)}) collective-permute-start(f32[1024,128]{0,1:T(8,128)S(1)} %fusion.11), channel_id=1, source_target_pairs={{0,2},{1,3},{2,0},{3,1},{4,6},{5,7},{6,4},{7,5},{8,10},{9,11},{10,... | collective-permute-start | bytes 1572872 | tf_op jit(solution)/shard_map/ppermute | solution.py:49
  345.0 31.1 %copy-start.5 = (bf16[1024,320]{0,1:T(8,128)(2,1)S(1)}, bf16[1024,320]{0,1:T(8,128)(2,1)}, u32[]{:S(2)}) copy-start(bf16[1024,320]{0,1:T(8,128)(2,1)} %multiply_convert_fusion.1) | copy-start | bytes 1966084
  345.0 12.6 %collective-permute-start.2 = (f32[1024,128]{0,1:T(8,128)S(1)}, f32[1024,128]{0,1:T(8,128)S(1)}, u32[]{:S(2)}, u32[]{:S(2)}) collective-permute-start(f32[1024,128]{0,1:T(8,128)S(1)} %add.68), channel_id=1, source_target_pairs={{0,4},{1,5},{2,6},{3,7},{4,0},{5,1},{6,2},{7,3},{8,12},{9,13},{10,... | collective-permute-start | bytes 1572872 | tf_op jit(solution)/shard_map/ppermute | solution.py:49
  357.7 18.8 %copy-start.7 = (bf16[1024,320]{0,1:T(8,128)(2,1)S(1)}, bf16[1024,320]{0,1:T(8,128)(2,1)}, u32[]{:S(2)}) copy-start(bf16[1024,320]{0,1:T(8,128)(2,1)} %param.10) | copy-start | bytes 1966084
  357.7 18.3 %collective-permute-start.3 = (f32[1024,128]{0,1:T(8,128)S(1)}, f32[1024,128]{0,1:T(8,128)S(1)}, u32[]{:S(2)}, u32[]{:S(2)}) collective-permute-start(f32[1024,128]{0,1:T(8,128)S(1)} %add.69), channel_id=1, source_target_pairs={{0,8},{1,9},{2,10},{3,11},{4,12},{5,13},{6,14},{7,15},{8,0},{9,1},... | collective-permute-start | bytes 1572872 | tf_op jit(solution)/shard_map/ppermute | solution.py:49
  377.0 14.8 %collective-permute-start.4 = (f32[2368,64]{0,1:T(8,128)S(1)}, f32[2368,64]{0,1:T(8,128)S(1)}, u32[]{:S(2)}, u32[]{:S(2)}) collective-permute-start(f32[2368,64]{0,1:T(8,128)S(1)} %concatenate.7), channel_id=1, source_target_pairs={{0,16},{16,0},{32,48},{48,32},{64,80},{80,64},{96,112},{112,96},{1... | collective-permute-start | bytes 1818632 | tf_op jit(solution)/shard_map/ppermute | solution.py:49
  391.9 10.8 %collective-permute-start.5 = (f32[2368,64]{0,1:T(8,128)S(1)}, f32[2368,64]{0,1:T(8,128)S(1)}, u32[]{:S(2)}, u32[]{:S(2)}) collective-permute-start(f32[2368,64]{0,1:T(8,128)S(1)} %add.71), channel_id=1, source_target_pairs={{0,32},{16,48},{32,0},{48,16},{64,96},{80,112},{96,64},{112,80},{1... | collective-permute-start | bytes 1818632 | tf_op jit(solution)/shard_map/ppermute | solution.py:49
  402.8 16.4 %collective-permute-start.6 = (f32[2368,64]{0,1:T(8,128)S(1)}, f32[2368,64]{0,1:T(8,128)S(1)}, u32[]{:S(2)}, u32[]{:S(2)}) collective-permute-start(f32[2368,64]{0,1:T(8,128)S(1)} %add.72), channel_id=1, source_target_pairs={{0,64},{16,80},{32,96},{48,112},{64,0},{80,16},{96,32},{112,48},{1... | collective-permute-start | bytes 1818632 | tf_op jit(solution)/shard_map/ppermute | solution.py:49
  (2 other events, 1.6 us)
Sparse Core Ops, SparseCore 0:
  10.4 241.7 all-gather.1
  302.7 141.0 reduce-scatter.1

commit v4 on v1

--- a/solution.py
+++ b/solution.py
@@ -68,21 +68,32 @@
     gain_local = lax.dynamic_slice_in_dim(gate_gain, col_index * local_width, local_width, 0)
     gated_local = (gain_local[None, :] * token_grad.astype(jnp.float32)).astype(jnp.bfloat16)
     tokens_full = lax.all_gather(tokens_in, "col", axis=1, tiled=True)
-    gated_full = lax.all_gather(gated_local, "col", axis=1, tiled=True)
     inner_low = plain_dot(tokens_full, inner_down).astype(jnp.bfloat16)
-    forward_sum = plain_dot(tokens_full, inner_weight)
-    grad_low = dot_rows(gated_full, outer_up).astype(jnp.bfloat16)
-    backward_sum = plain_dot(gated_full, outer_weight)
-    pre = forward_sum + plain_dot(inner_low, inner_up) + inner_bias[None, :]
+    pre = plain_dot(tokens_full, inner_weight) + plain_dot(inner_low, inner_up) + inner_bias[None, :]
     hidden = gelu_value(pre).astype(jnp.bfloat16)
-    grad_hidden = backward_sum + dot_rows(grad_low, outer_down)
-    grad_pre = (grad_hidden * gelu_slope(pre)).astype(jnp.bfloat16)
-    pre_low_part = dot_rows(grad_pre, inner_up)
-    block_part = dot_rows(grad_pre, inner_weight).astype(jnp.bfloat16).astype(jnp.float32)
-    low_part = dot_rows(pre_low_part.astype(jnp.bfloat16), inner_down)
-    tokens_grad = lax.psum_scatter(
-        (block_part + low_part).astype(jnp.bfloat16), "col", scatter_dimension=1, tiled=True
-    )
+
+    half = tok_rows // 2
+    grad_lows, grad_pres, pre_low_parts, grads = [], [], [], []
+    for lo in (0, half):
+        gated_part = lax.all_gather(gated_local[lo : lo + half], "col", axis=1, tiled=True)
+        grad_low = dot_rows(gated_part, outer_up).astype(jnp.bfloat16)
+        grad_hidden = plain_dot(gated_part, outer_weight) + dot_rows(grad_low, outer_down)
+        grad_pre = (grad_hidden * gelu_slope(pre[lo : lo + half])).astype(jnp.bfloat16)
+        pre_low_part = dot_rows(grad_pre, inner_up)
+        block_part = dot_rows(grad_pre, inner_weight).astype(jnp.bfloat16).astype(jnp.float32)
+        low_part = dot_rows(pre_low_part.astype(jnp.bfloat16), inner_down)
+        grads.append(
+            lax.psum_scatter(
+                (block_part + low_part).astype(jnp.bfloat16), "col", scatter_dimension=1, tiled=True
+            )
+        )
+        grad_lows.append(grad_low)
+        grad_pres.append(grad_pre)
+        pre_low_parts.append(pre_low_part)
+    tokens_grad = jnp.concatenate(grads, axis=0)
+    grad_low = jnp.concatenate(grad_lows, axis=0)
+    grad_pre = jnp.concatenate(grad_pres, axis=0)
+    pre_low_part = jnp.concatenate(pre_low_parts, axis=0)
 
     hidden_low_part = plain_dot(hidden, outer_down)
     lows = tree_sum(jnp.concatenate([hidden_low_part, pre_low_part], axis=1), "col", n_col)

time: 342 us -> 414 us (1.21)
  waiting for transfers between devices: 248 us -> 307 us
  matrix products: 63.9 us -> 73 us
    reduce_scatter x1 -> x2, waiting for transfers between devices: 28.9 us -> 63.8 us  [local(): lax.psum_scatter((block_part + low_part).astype(jnp.bfloat16), 'col', sca...]
    all_gather x1 -> x2, waiting for transfers between devices: 59.2 us -> 86.9 us  [local(): lax.all_gather(gated_local[lo:lo + half], 'col', axis=1, tiled=True)]
    all_gather x1, waiting for transfers between devices: 84.7 us -> 70.1 us  [local(): tokens_full = lax.all_gather(tokens_in, 'col', axis=1, tiled=True)]
    ppermute x7, waiting for transfers between devices: 74.2 us -> 84.6 us  [tree_sum(): value = value + lax.ppermute(value, axis, pairs)]
    dot_general x5 -> x6, matrix products: 31.4 us -> 36.2 us  [plain_dot(): return jnp.dot(left, right, preferred_element_type=jnp.float32)]
    dot_general x5 -> x10, matrix products: 30.4 us -> 34.1 us  [dot_rows(): lax.dot_general(left, right, (((1,), (1,)), ((), ())), preferred_element_...]
  transfers between devices with their start and end apart: 10 -> 12, of which waited for: 10 -> 11; matrix products, arithmetic and copies ran while one was open for 8% -> 18% of each run, Pallas kernels for 0% -> 0%
where the time goes in v4:
time: 414 us
  waiting for transfers between devices  307 us (74%)
  matrix products  73 us (18%)
  between operations  14.2 us (3%)
  starting transfers between devices  8.59 us (2%)
  local copies, waits for them, and re-layouts  7.08 us (2%)
    all_gather x2, waiting for transfers between devices, local(): lax.all_gather(gated_local[lo:lo + half], 'col', axis=1, tiled=True)  86.9 us
    ppermute x7, waiting for transfers between devices, tree_sum(): value = value + lax.ppermute(value, axis, pairs)  84.6 us
    all_gather x1, waiting for transfers between devices, local(): tokens_full = lax.all_gather(tokens_in, 'col', axis=1, tiled=True)  70.1 us
    reduce_scatter x2, waiting for transfers between devices, local(): lax.psum_scatter((block_part + low_part).astype(jnp.bfloat16), 'col', sca...  63.8 us
    dot_general x6, matrix products, plain_dot(): return jnp.dot(left, right, preferred_element_type=jnp.float32)  36.2 us
    dot_general x10, matrix products, dot_rows(): lax.dot_general(left, right, (((1,), (1,)), ((), ())), preferred_element_...  34.1 us
    ppermute x7, starting transfers between devices, tree_sum(): value = value + lax.ppermute(value, axis, pairs)  8.39 us
  transfers between devices with their start and end apart: 12, of which 11 were waited for; matrix products, arithmetic and copies ran while one was open for 18% of the time, Pallas kernels for 0%

profile of v4, /device:TPU:1, one launch (start us, length us, event | category | flops | bytes accessed | tf_op | source)
XLA Modules:
  0.0 413.5 jit_solution(1743399059003365890)
XLA Ops:
  11.8 62.3 %all-gather.8.cloned.1.call-done = bf16[512,5120]{0,1:T(8,128)(2,1)} async-done(((bf16[512,320]{0,1:T(8,128)(2,1)}), bf16[512,5120]{0,1:T(8,128)(2,1)}) %all-gather.8.cloned.1.call-update) | async-done | bytes 5242896 | tf_op jit(solution)/shard_map/all_gather | solution.py:78
  74.1 3.6 convolution_convert_fusion.3
  78.1 8.4 %fusion.40 = f32[512,864]{0,1:T(8,128)} fusion(bf16[5120,864]{0,1:T(8,128)(2,1)} %param.15, bf16[512,5120]{0,1:T(8,128)(2,1)S(1)} %copy-done.3), kind=kOutput, calls=%fused_computation.61 | convolution fusion | flops 4529848320 | bytes 15859712 | tf_op jit(solution)/shard_map/dot_general | solution.py:25
  86.5 70.1 %all-gather.6.cloned.1.call-done = bf16[1024,5120]{0,1:T(8,128)(2,1)} async-done(((bf16[1024,320]{0,1:T(8,128)(2,1)}), bf16[1024,5120]{0,1:T(8,128)(2,1)}) %all-gather.6.cloned.1.call-update) | async-done | bytes 10485776 | tf_op jit(solution)/shard_map/all_gather | solution.py:70
  156.7 6.1 %convolution_convert_fusion.2 = bf16[1024,64]{0,1:T(8,128)(2,1)S(1)} fusion(bf16[5120,64]{0,1:T(8,128)(2,1)S(1)} %copy-done, bf16[1024,5120]{0,1:T(8,128)(2,1)} %all-gather.6.cloned.1.call-done), kind=kOutput, calls=%fused_computation.34 | convolution fusion | flops 671154176 | bytes 11272192 | tf_op jit(solution)/shard_map/dot_general | solution.py:25
  163.7 12.0 %fusion.38 = f32[1024,864]{0,1:T(8,128)S(1)} fusion(bf16[5120,864]{0,1:T(8,128)(2,1)} %param.13, bf16[1024,5120]{0,1:T(8,128)(2,1)S(1)} %copy-done.1), kind=kOutput, calls=%fused_computation.59 | convolution fusion | flops 9059696640 | bytes 22872064 | tf_op jit(solution)/shard_map/dot_general | solution.py:25
  177.3 4.8 %fusion.18 = bf16[512,864]{0,1:T(8,128)(2,1)S(1)} fusion(f32[1024,864]{0,1:T(8,128)S(1)} %get-tuple-element.12, f32[512,864]{0,1:T(8,128)} %fusion.40, bf16[512,64]{0,1:T(8,128)(2,1)S(1)} %convolution_convert_fusion.3, bf16[864,64]{0,1:T(8,128)(2,1)S(1)} %copy-done.15), kind=kOutput, calls=%fused_computation.28 | convolution fusion | flops 65470464 | bytes 4599808 | tf_op jit(solution)/shard_map/dot_general | solution.py:29
  182.5 6.1 %convolution_convert_fusion = bf16[512,5120]{0,1:T(8,128)(2,1)S(1)} fusion(bf16[512,864]{0,1:T(8,128)(2,1)S(1)} %fusion.18, bf16[5120,864]{0,1:T(8,128)(2,1)S(1)} %bitcast.41), kind=kOutput, calls=%fused_computation.2 | convolution fusion | flops 4532469760 | bytes 14974976 | tf_op jit(solution)/shard_map/dot_general | solution.py:29
  188.6 3.9 add_convert_fusion
  192.6 24.7 %all-gather.4.cloned.1.call-done = bf16[512,5120]{0,1:T(8,128)(2,1)} async-done(((bf16[512,320]{0,1:T(8,128)(2,1)}), bf16[512,5120]{0,1:T(8,128)(2,1)}) %all-gather.4.cloned.1.call-update) | async-done | bytes 5242896 | tf_op jit(solution)/shard_map/all_gather | solution.py:78
  217.3 3.8 convolution_convert_fusion.4
  221.5 7.7 %fusion.37 = f32[512,864]{0,1:T(8,128)S(1)} fusion(bf16[5120,864]{0,1:T(8,128)(2,1)} %param.15, bf16[512,5120]{0,1:T(8,128)(2,1)S(1)} %copy-done.2), kind=kOutput, calls=%fused_computation.58 | convolution fusion | flops 4529848320 | bytes 15859712 | tf_op jit(solution)/shard_map/dot_general | solution.py:25
  230.9 5.9 %convolution_convert_fusion.1 = bf16[512,5120]{0,1:T(8,128)(2,1)S(1)} fusion(bf16[512,864]{0,1:T(8,128)(2,1)S(1)} %fusion.11, bf16[5120,864]{0,1:T(8,128)(2,1)S(1)} %bitcast.43), kind=kOutput, calls=%fused_computation.3 | convolution fusion | flops 4532469760 | bytes 14974976 | tf_op jit(solution)/shard_map/dot_general | solution.py:29
  236.9 4.0 add_convert_fusion.1
  244.5 15.6 %collective-permute-done.1 = f32[1024,128]{0,1:T(8,128)S(1)} collective-permute-done((f32[1024,128]{0,1:T(8,128)S(1)}, f32[1024,128]{0,1:T(8,128)S(1)}, u32[]{:S(2)}, u32[]{:S(2)}) %collective-permute-start.1) | collective-permute-done | bytes 524320 | tf_op jit(solution)/shard_map/ppermute | solution.py:44
  260.9 12.2 %collective-permute-done.2 = f32[1024,128]{0,1:T(8,128)S(1)} collective-permute-done((f32[1024,128]{0,1:T(8,128)S(1)}, f32[1024,128]{0,1:T(8,128)S(1)}, u32[]{:S(2)}, u32[]{:S(2)}) %collective-permute-start.2) | collective-permute-done | bytes 524320 | tf_op jit(solution)/shard_map/ppermute | solution.py:44
  273.2 2.7 collective-permute-start.3
  277.9 14.2 %collective-permute-done.3 = f32[1024,128]{0,1:T(8,128)S(1)} collective-permute-done((f32[1024,128]{0,1:T(8,128)S(1)}, f32[1024,128]{0,1:T(8,128)S(1)}, u32[]{:S(2)}, u32[]{:S(2)}) %collective-permute-start.3) | collective-permute-done | bytes 524320 | tf_op jit(solution)/shard_map/ppermute | solution.py:44
  294.7 16.3 %collective-permute-done.4 = f32[2368,64]{0,1:T(8,128)S(1)} collective-permute-done((f32[2368,64]{0,1:T(8,128)S(1)}, f32[2368,64]{0,1:T(8,128)S(1)}, u32[]{:S(2)}, u32[]{:S(2)}) %collective-permute-start.4) | collective-permute-done | bytes 606240 | tf_op jit(solution)/shard_map/ppermute | solution.py:44
  312.1 11.5 %collective-permute-done.5 = f32[2368,64]{0,1:T(8,128)S(1)} collective-permute-done((f32[2368,64]{0,1:T(8,128)S(1)}, f32[2368,64]{0,1:T(8,128)S(1)}, u32[]{:S(2)}, u32[]{:S(2)}) %collective-permute-start.5) | collective-permute-done | bytes 606240 | tf_op jit(solution)/shard_map/ppermute | solution.py:44
  323.6 2.8 collective-permute-start.6
  326.4 13.1 %collective-permute-done.6 = f32[2368,64]{0,1:T(8,128)S(1)} collective-permute-done((f32[2368,64]{0,1:T(8,128)S(1)}, f32[2368,64]{0,1:T(8,128)S(1)}, u32[]{:S(2)}, u32[]{:S(2)}) %collective-permute-start.6) | collective-permute-done | bytes 606240 | tf_op jit(solution)/shard_map/ppermute | solution.py:44
  341.2 63.8 %reduce-scatter.3.cloned.1.call-done = bf16[512,320]{0,1:T(8,128)(2,1)} async-done(((bf16[512,5120]{0,1:T(8,128)(2,1)}), bf16[512,320]{0,1:T(8,128)(2,1)}) %reduce-scatter.3.cloned.1.call-update) | async-done | bytes 327696 | tf_op jit(solution)/shard_map/reduce_scatter | solution.py:86
  405.0 2.0 pad_maximum_fusion
  (96 shorter events, 21.6 us)
Async XLA Ops:
  7.2 149.5 %copy-start = (bf16[5120,64]{0,1:T(8,128)(2,1)S(1)}, bf16[5120,64]{0,1:T(8,128)(2,1)}, u32[]{:S(2)}) copy-start(bf16[5120,64]{0,1:T(8,128)(2,1)} %param.16) | copy-start | bytes 1966084
  7.2 66.9 %copy-start.4 = (bf16[64,5120]{1,0:T(8,128)(2,1)S(1)}, bf16[64,5120]{1,0:T(8,128)(2,1)}, u32[]{:S(2)}) copy-start(bf16[64,5120]{1,0:T(8,128)(2,1)} %param.19) | copy-start | bytes 1966084
  7.2 66.9 %all-gather.8.cloned.1.call-start = ((), (), s32[]{:S(2)}) async-start(), calls=%async_computation.5 | async-start | bytes 5570560 | tf_op jit(solution)/shard_map/all_gather | solution.py:78
  10.3 146.4 %all-gather.6.cloned.1.call-start = ((), (), s32[]{:S(2)}) async-start(), calls=%async_computation.3 | async-start | bytes 11141120 | tf_op jit(solution)/shard_map/all_gather | solution.py:70
  11.0 206.3 %all-gather.4.cloned.1.call-start = ((), (), s32[]{:S(2)}) async-start(), calls=%async_computation.2 | async-start | bytes 5570560 | tf_op jit(solution)/shard_map/all_gather | solution.py:78
  11.8 329.4 %reduce-scatter.5.cloned.1.call-start = ((), (), s32[]{:S(2)}) async-start(), calls=%async_computation.6 | async-start | bytes 5570560 | tf_op jit(solution)/shard_map/reduce_scatter | solution.py:86
  163.6 12.0 %copy-start.13 = (bf16[1024,64]{0,1:T(8,128)(2,1)}, bf16[1024,64]{0,1:T(8,128)(2,1)S(1)}, u32[]{:S(2)}) copy-start(bf16[1024,64]{0,1:T(8,128)(2,1)S(1)} %convolution_convert_fusion.2) | copy-start | bytes 393220
  163.7 12.0 %copy-start.10 = (bf16[64,864]{1,0:T(8,128)(2,1)S(1)}, bf16[64,864]{1,0:T(8,128)(2,1)}, u32[]{:S(2)}) copy-start(bf16[64,864]{1,0:T(8,128)(2,1)} %param.17) | copy-start | bytes 331780
  163.7 12.0 %copy-start.18 = (f32[864]{0:T(1024)S(1)}, f32[864]{0:T(1024)}, u32[]{:S(2)}) copy-start(f32[864]{0:T(1024)} %param.14) | copy-start | bytes 10372
  192.6 212.4 %reduce-scatter.3.cloned.1.call-start = ((), (), s32[]{:S(2)}) async-start(), calls=%async_computation.4 | async-start | bytes 5570560 | tf_op jit(solution)/shard_map/reduce_scatter | solution.py:86
  217.3 13.6 %slice-start.3 = ((s8[8847360]{0:T(1024)(128)(4,1)}), s8[4194304]{0:T(1024)(128)(4,1)S(1)}, s32[]{:S(2)}) async-start(s8[8847360]{0:T(1024)(128)(4,1)} %bitcast.42), calls=%async_computation.10 | async-start | bytes 8388608
  221.5 9.4 %slice-start.5 = ((s8[8847360]{0:T(1024)(128)(4,1)}), s8[458752]{0:T(1024)(128)(4,1)S(1)}, s32[]{:S(2)}) async-start(s8[8847360]{0:T(1024)(128)(4,1)} %bitcast.42), calls=%async_computation.12 | async-start | bytes 917504
  241.8 34.2 %copy-start.7 = (bf16[512,864]{0,1:T(8,128)(2,1)S(1)}, bf16[512,864]{0,1:T(8,128)(2,1)}, u32[]{:S(2)}) copy-start(bf16[512,864]{0,1:T(8,128)(2,1)} %copy-done.6) | copy-start | bytes 2654212
  241.8 34.2 %copy-start.9 = (bf16[512,864]{0,1:T(8,128)(2,1)S(1)}, bf16[512,864]{0,1:T(8,128)(2,1)}, u32[]{:S(2)}) copy-start(bf16[512,864]{0,1:T(8,128)(2,1)} %copy-done.8) | copy-start | bytes 2654212
  241.8 34.2 %copy-start.14 = (bf16[1024,64]{0,1:T(8,128)(2,1)S(1)}, bf16[1024,64]{0,1:T(8,128)(2,1)}, u32[]{:S(2)}) copy-start(bf16[1024,64]{0,1:T(8,128)(2,1)} %copy-done.13) | copy-start | bytes 393220
  242.2 2.0 collective-permute-start
  244.3 33.0 %copy-start.12 = (bf16[512,64]{0,1:T(8,128)(2,1)S(1)}, bf16[512,64]{0,1:T(8,128)(2,1)}, u32[]{:S(2)}) copy-start(bf16[512,64]{0,1:T(8,128)(2,1)} %copy-done.11) | copy-start | bytes 196612
  244.3 15.7 %collective-permute-start.1 = (f32[1024,128]{0,1:T(8,128)S(1)}, f32[1024,128]{0,1:T(8,128)S(1)}, u32[]{:S(2)}, u32[]{:S(2)}) collective-permute-start(f32[1024,128]{0,1:T(8,128)S(1)} %fusion.34), channel_id=1, source_target_pairs={{0,2},{1,3},{2,0},{3,1},{4,6},{5,7},{6,4},{7,5},{8,10},{9,11},{10,... | collective-permute-start | bytes 1572872 | tf_op jit(solution)/shard_map/ppermute | solution.py:44
  260.1 13.0 %collective-permute-start.2 = (f32[1024,128]{0,1:T(8,128)S(1)}, f32[1024,128]{0,1:T(8,128)S(1)}, u32[]{:S(2)}, u32[]{:S(2)}) collective-permute-start(f32[1024,128]{0,1:T(8,128)S(1)} %add.104), channel_id=1, source_target_pairs={{0,4},{1,5},{2,6},{3,7},{4,0},{5,1},{6,2},{7,3},{8,12},{9,13},{10,... | collective-permute-start | bytes 1572872 | tf_op jit(solution)/shard_map/ppermute | solution.py:44
  273.2 19.3 %copy-start.5 = (bf16[1024,320]{0,1:T(8,128)(2,1)S(1)}, bf16[1024,320]{0,1:T(8,128)(2,1)}, u32[]{:S(2)}) copy-start(bf16[1024,320]{0,1:T(8,128)(2,1)} %param.10) | copy-start | bytes 1966084
  273.2 18.9 %collective-permute-start.3 = (f32[1024,128]{0,1:T(8,128)S(1)}, f32[1024,128]{0,1:T(8,128)S(1)}, u32[]{:S(2)}, u32[]{:S(2)}) collective-permute-start(f32[1024,128]{0,1:T(8,128)S(1)} %add.105), channel_id=1, source_target_pairs={{0,8},{1,9},{2,10},{3,11},{4,12},{5,13},{6,14},{7,15},{8,0},{9,1},... | collective-permute-start | bytes 1572872 | tf_op jit(solution)/shard_map/ppermute | solution.py:44
  294.1 16.9 %collective-permute-start.4 = (f32[2368,64]{0,1:T(8,128)S(1)}, f32[2368,64]{0,1:T(8,128)S(1)}, u32[]{:S(2)}, u32[]{:S(2)}) collective-permute-start(f32[2368,64]{0,1:T(8,128)S(1)} %concatenate.23), channel_id=1, source_target_pairs={{0,16},{16,0},{32,48},{48,32},{64,80},{80,64},{96,112},{112,96},{1... | collective-permute-start | bytes 1818632 | tf_op jit(solution)/shard_map/ppermute | solution.py:44
  311.1 12.5 %collective-permute-start.5 = (f32[2368,64]{0,1:T(8,128)S(1)}, f32[2368,64]{0,1:T(8,128)S(1)}, u32[]{:S(2)}, u32[]{:S(2)}) collective-permute-start(f32[2368,64]{0,1:T(8,128)S(1)} %add.107), channel_id=1, source_target_pairs={{0,32},{16,48},{32,0},{48,16},{64,96},{80,112},{96,64},{112,80},{1... | collective-permute-start | bytes 1818632 | tf_op jit(solution)/shard_map/ppermute | solution.py:44
  323.6 15.9 %collective-permute-start.6 = (f32[2368,64]{0,1:T(8,128)S(1)}, f32[2368,64]{0,1:T(8,128)S(1)}, u32[]{:S(2)}, u32[]{:S(2)}) collective-permute-start(f32[2368,64]{0,1:T(8,128)S(1)} %add.108), channel_id=1, source_target_pairs={{0,64},{16,80},{32,96},{48,112},{64,0},{80,16},{96,32},{112,48},{1... | collective-permute-start | bytes 1818632 | tf_op jit(solution)/shard_map/ppermute | solution.py:44
  (15 other events, 86.7 us)
Sparse Core Ops, SparseCore 0:
  10.4 63.6 all-gather.7
  76.5 80.1 all-gather.5
  159.7 57.5 all-gather.3
  221.2 96.1 reduce-scatter.4
  321.4 83.5 reduce-scatter.2

commit v5 on v1

--- a/solution.py
+++ b/solution.py
@@ -67,8 +67,8 @@
     rank = inner_down.shape[1]
     gain_local = lax.dynamic_slice_in_dim(gate_gain, col_index * local_width, local_width, 0)
     gated_local = (gain_local[None, :] * token_grad.astype(jnp.float32)).astype(jnp.bfloat16)
-    tokens_full = lax.all_gather(tokens_in, "col", axis=1, tiled=True)
-    gated_full = lax.all_gather(gated_local, "col", axis=1, tiled=True)
+    both_full = lax.all_gather(jnp.stack([tokens_in, gated_local]), "col", axis=2, tiled=True)
+    tokens_full, gated_full = both_full[0], both_full[1]
     inner_low = plain_dot(tokens_full, inner_down).astype(jnp.bfloat16)
     forward_sum = plain_dot(tokens_full, inner_weight)
     grad_low = dot_rows(gated_full, outer_up).astype(jnp.bfloat16)

time: 342 us -> 334 us (0.977)
  waiting for transfers between devices: 248 us -> 236 us
  matrix products: 63.9 us -> 69.9 us
  local copies, waits for them, and re-layouts: 7.89 us -> 3.54 us
    all_gather x2 -> x1, waiting for transfers between devices: 144 us -> 133 us  [local(): lax.all_gather(jnp.stack([tokens_in, gated_local]), 'col', axis=2, tiled=...]
    dot_general x5, matrix products: 31.4 us -> 39.7 us  [plain_dot(): return jnp.dot(left, right, preferred_element_type=jnp.float32)]
    unnamed x34 -> x36, local copies, waits for them, and re-layouts: 5.36 us -> 0.96 us
    another operation x1 -> x3, other arithmetic: 0.06 us -> 3.65 us  [the longest x2 3.59 us: local(): jnp.stack([tokens_in, gated_local])]
  transfers between devices with their start and end apart: 10 -> 9, of which waited for: 10 -> 9; matrix products, arithmetic and copies ran while one was open for 8% -> 1% of each run, Pallas kernels for 0% -> 0%
where the time goes in v5:
time: 334 us
  waiting for transfers between devices  236 us (71%)
  matrix products  69.9 us (21%)
  between operations  14.4 us (4%)
  starting transfers between devices  6.08 us (2%)
  other arithmetic  4.09 us (1%)
  local copies, waits for them, and re-layouts  3.54 us (1%)
    all_gather x1, waiting for transfers between devices, local(): lax.all_gather(jnp.stack([tokens_in, gated_local]), 'col', axis=2, tiled=...  133 us
    ppermute x7, waiting for transfers between devices, tree_sum(): value = value + lax.ppermute(value, axis, pairs)  73 us
    dot_general x5, matrix products, plain_dot(): return jnp.dot(left, right, preferred_element_type=jnp.float32)  39.7 us
    reduce_scatter x1, waiting for transfers between devices, local(): lax.psum_scatter((block_part + low_part).astype(jnp.bfloat16), 'col', sca...  29.7 us
    dot_general x5, matrix products, dot_rows(): lax.dot_general(left, right, (((1,), (1,)), ((), ())), preferred_element_...  28.1 us
  transfers between devices with their start and end apart: 9, of which 9 were waited for; matrix products, arithmetic and copies ran while one was open for 1% of the time, Pallas kernels for 0%

profile of v5, /device:TPU:1, one launch (start us, length us, event | category | flops | bytes accessed | tf_op | source)
XLA Modules:
  0.0 334.1 jit_solution(18012506820066791098)
XLA Ops:
  8.1 1.3 fusion.14
  9.3 2.3 pad_maximum_fusion
  11.7 133.4 %all-gather.2.cloned.1.call-done = bf16[2,1024,5120]{1,2,0:T(8,128)(2,1)} async-done(((bf16[2,1024,320]{1,2,0:T(8,128)(2,1)}), bf16[2,1024,5120]{1,2,0:T(8,128)(2,1)}) %all-gather.2.cloned.1.call-update) | async-done | bytes 20971536 | tf_op jit(solution)/shard_map/all_gather | solution.py:70
  145.2 6.1 %fusion.11 = bf16[1024,64]{0,1:T(8,128)(2,1)S(1)} fusion(bf16[5120,64]{0,1:T(8,128)(2,1)S(1)} %copy-done, bf16[2,1024,5120]{1,2,0:T(8,128)(2,1)} %all-gather.2.cloned.1.call-done), kind=kOutput, calls=%fused_computation.20 | convolution fusion | flops 671154176 | bytes 11272192 | tf_op jit(solution)/shard_map/dot_general | solution.py:25
  151.3 15.2 %fusion.2 = f32[1024,864]{0,1:T(8,128)} fusion(bf16[5120,864]{0,1:T(8,128)(2,1)} %param.13, bf16[2,1024,5120]{1,2,0:T(8,128)(2,1)} %all-gather.2.cloned.1.call-done), kind=kOutput, calls=%fused_computation.5 | convolution fusion | flops 9059696640 | bytes 22872064 | tf_op jit(solution)/shard_map/dot_general | solution.py:25
  166.6 5.4 %multiply_convert_fusion = (bf16[1024,864]{0,1:T(8,128)(2,1)S(1)}, f32[1024,864]{0,1:T(8,128)}) fusion(f32[864]{0:T(1024)S(1)} %copy-done.12, f32[1024,864]{0,1:T(8,128)} %fusion.2, bf16[1024,64]{0,1:T(8,128)(2,1)S(1)} %fusion.11, bf16[64,864]{1,0:T(8,128)(2,1)S(1)} %copy-done.8), kind=kOutput, calls=%fused_computation.16 | convolution fusion | flops 122978304 | bytes 9092480 | tf_op jit(solution)/shard_map/dot_general | solution.py:25
  172.0 1.9 fusion.12
  173.9 12.6 %fusion = f32[1024,864]{0,1:T(8,128)} fusion(bf16[5120,864]{0,1:T(8,128)(2,1)} %param.15, bf16[2,1024,5120]{1,2,0:T(8,128)(2,1)S(1)} %bitcast.43), kind=kOutput, calls=%fused_computation.3 | convolution fusion | flops 9059696640 | bytes 22872064 | tf_op jit(solution)/shard_map/dot_general | solution.py:25
  186.5 4.7 %fusion.10 = bf16[1024,864]{0,1:T(8,128)(2,1)S(1)} fusion(f32[1024,864]{0,1:T(8,128)} %get-tuple-element.10, f32[1024,864]{0,1:T(8,128)} %fusion, bf16[1024,64]{0,1:T(8,128)(2,1)S(1)} %fusion.12, bf16[864,64]{0,1:T(8,128)(2,1)S(1)} %copy-done.9), kind=kOutput, calls=%fused_computation.15 | convolution fusion | flops 130940928 | bytes 9089024 | tf_op jit(solution)/shard_map/dot_general | solution.py:29
  191.2 1.3 fusion.23
  192.5 13.6 %fusion.20 = bf16[1024,5120]{0,1:T(8,128)(2,1)S(1)} fusion(bf16[1024,864]{0,1:T(8,128)(2,1)S(1)} %fusion.10, bf16[5120,864]{0,1:T(8,128)(2,1)} %param.13), kind=kOutput, calls=%fused_computation.35 | convolution fusion | flops 9059696640 | bytes 21102592 | tf_op jit(solution)/shard_map/dot_general | solution.py:29
  206.2 6.6 %add_convert_fusion = bf16[1024,5120]{0,1:T(8,128)(2,1)} fusion(bf16[5120,64]{0,1:T(8,128)(2,1)S(1)} %copy-done, bf16[1024,5120]{0,1:T(8,128)(2,1)S(1)} %fusion.20, f32[1024,64]{0,1:T(8,128)} %fusion.23), kind=kOutput, calls=%fused_computation | convolution fusion | flops 686882816 | bytes 21889024 | tf_op jit(solution)/shard_map/dot_general | solution.py:29
  212.8 0.9 copy-done.10
  214.5 1.7 collective-permute-done
  216.4 14.6 %collective-permute-done.1 = f32[1024,128]{0,1:T(8,128)S(1)} collective-permute-done((f32[1024,128]{0,1:T(8,128)S(1)}, f32[1024,128]{0,1:T(8,128)S(1)}, u32[]{:S(2)}, u32[]{:S(2)}) %collective-permute-start.1) | collective-permute-done | bytes 524320 | tf_op jit(solution)/shard_map/ppermute | solution.py:44
  231.2 12.3 %collective-permute-done.2 = f32[1024,128]{0,1:T(8,128)S(1)} collective-permute-done((f32[1024,128]{0,1:T(8,128)S(1)}, f32[1024,128]{0,1:T(8,128)S(1)}, u32[]{:S(2)}, u32[]{:S(2)}) %collective-permute-start.2) | collective-permute-done | bytes 524320 | tf_op jit(solution)/shard_map/ppermute | solution.py:44
  243.7 1.1 collective-permute-start.3
  246.1 15.6 %collective-permute-done.3 = f32[1024,128]{0,1:T(8,128)S(1)} collective-permute-done((f32[1024,128]{0,1:T(8,128)S(1)}, f32[1024,128]{0,1:T(8,128)S(1)}, u32[]{:S(2)}, u32[]{:S(2)}) %collective-permute-start.3) | collective-permute-done | bytes 524320 | tf_op jit(solution)/shard_map/ppermute | solution.py:44
  262.8 9.5 %collective-permute-done.4 = f32[2368,64]{0,1:T(8,128)S(1)} collective-permute-done((f32[2368,64]{0,1:T(8,128)S(1)}, f32[2368,64]{0,1:T(8,128)S(1)}, u32[]{:S(2)}, u32[]{:S(2)}) %collective-permute-start.4) | collective-permute-done | bytes 606240 | tf_op jit(solution)/shard_map/ppermute | solution.py:44
  272.4 1.3 collective-permute-start.5
  273.7 8.3 %collective-permute-done.5 = f32[2368,64]{0,1:T(8,128)S(1)} collective-permute-done((f32[2368,64]{0,1:T(8,128)S(1)}, f32[2368,64]{0,1:T(8,128)S(1)}, u32[]{:S(2)}, u32[]{:S(2)}) %collective-permute-start.5) | collective-permute-done | bytes 606240 | tf_op jit(solution)/shard_map/ppermute | solution.py:44
  282.0 2.9 collective-permute-start.6
  284.9 11.0 %collective-permute-done.6 = f32[2368,64]{0,1:T(8,128)S(1)} collective-permute-done((f32[2368,64]{0,1:T(8,128)S(1)}, f32[2368,64]{0,1:T(8,128)S(1)}, u32[]{:S(2)}, u32[]{:S(2)}) %collective-permute-start.6) | collective-permute-done | bytes 606240 | tf_op jit(solution)/shard_map/ppermute | solution.py:44
  297.6 29.7 %reduce-scatter.2.cloned.1.call-done = bf16[1024,320]{0,1:T(8,128)(2,1)} async-done(((bf16[1024,5120]{0,1:T(8,128)(2,1)}), bf16[1024,320]{0,1:T(8,128)(2,1)}) %reduce-scatter.2.cloned.1.call-update) | async-done | bytes 655376 | tf_op jit(solution)/shard_map/reduce_scatter | solution.py:83
  (61 shorter events, 6.5 us)
Async XLA Ops:
  7.2 138.0 %copy-start = (bf16[5120,64]{0,1:T(8,128)(2,1)S(1)}, bf16[5120,64]{0,1:T(8,128)(2,1)}, u32[]{:S(2)}) copy-start(bf16[5120,64]{0,1:T(8,128)(2,1)} %param.16) | copy-start | bytes 1966084
  7.2 138.0 %all-gather.2.cloned.1.call-start = ((), (), s32[]{:S(2)}) async-start(), calls=%async_computation.1 | async-start | bytes 22282240 | tf_op jit(solution)/shard_map/all_gather | solution.py:70
  11.7 315.6 %reduce-scatter.2.cloned.1.call-start = ((), (), s32[]{:S(2)}) async-start(), calls=%async_computation.2 | async-start | bytes 11141120 | tf_op jit(solution)/shard_map/reduce_scatter | solution.py:83
  145.2 26.8 %slice-start = ((s8[20971520]{0:T(1024)(128)(4,1)}), s8[4194304]{0:T(1024)(128)(4,1)S(1)}, s32[]{:S(2)}) async-start(s8[20971520]{0:T(1024)(128)(4,1)} %bitcast.42), calls=%async_computation.3 | async-start | bytes 8388608
  151.2 15.3 %copy-start.8 = (bf16[64,864]{1,0:T(8,128)(2,1)S(1)}, bf16[64,864]{1,0:T(8,128)(2,1)}, u32[]{:S(2)}) copy-start(bf16[64,864]{1,0:T(8,128)(2,1)} %param.17) | copy-start | bytes 331780
  151.3 15.3 %copy-start.12 = (f32[864]{0:T(1024)S(1)}, f32[864]{0:T(1024)}, u32[]{:S(2)}) copy-start(f32[864]{0:T(1024)} %param.14) | copy-start | bytes 10372
  151.3 20.7 %slice-start.1 = ((s8[20971520]{0:T(1024)(128)(4,1)}), s8[4194304]{0:T(1024)(128)(4,1)S(1)}, s32[]{:S(2)}) async-start(s8[20971520]{0:T(1024)(128)(4,1)} %bitcast.42), calls=%async_computation.4 | async-start | bytes 8388608
  151.3 20.7 %slice-start.2 = ((s8[20971520]{0:T(1024)(128)(4,1)}), s8[4194304]{0:T(1024)(128)(4,1)S(1)}, s32[]{:S(2)}) async-start(s8[20971520]{0:T(1024)(128)(4,1)} %bitcast.42), calls=%async_computation.5 | async-start | bytes 8388608
  151.3 20.7 %slice-start.3 = ((s8[20971520]{0:T(1024)(128)(4,1)}), s8[4194304]{0:T(1024)(128)(4,1)S(1)}, s32[]{:S(2)}) async-start(s8[20971520]{0:T(1024)(128)(4,1)} %bitcast.42), calls=%async_computation.6 | async-start | bytes 8388608
  151.3 20.7 %slice-start.4 = ((s8[20971520]{0:T(1024)(128)(4,1)}), s8[4194304]{0:T(1024)(128)(4,1)S(1)}, s32[]{:S(2)}) async-start(s8[20971520]{0:T(1024)(128)(4,1)} %bitcast.42), calls=%async_computation.7 | async-start | bytes 8388608
  166.5 5.4 %copy-start.11 = (bf16[64,5120]{1,0:T(8,128)(2,1)S(1)}, bf16[64,5120]{1,0:T(8,128)(2,1)}, u32[]{:S(2)}) copy-start(bf16[64,5120]{1,0:T(8,128)(2,1)} %param.19) | copy-start | bytes 1966084
  173.9 12.6 %copy-start.6 = (bf16[1024,64]{0,1:T(8,128)(2,1)}, bf16[1024,64]{0,1:T(8,128)(2,1)S(1)}, u32[]{:S(2)}) copy-start(bf16[1024,64]{0,1:T(8,128)(2,1)S(1)} %fusion.12) | copy-start | bytes 393220
  173.9 12.6 %copy-start.9 = (bf16[864,64]{0,1:T(8,128)(2,1)S(1)}, bf16[864,64]{0,1:T(8,128)(2,1)}, u32[]{:S(2)}) copy-start(bf16[864,64]{0,1:T(8,128)(2,1)} %param.18) | copy-start | bytes 331780
  213.6 31.1 %copy-start.7 = (bf16[1024,64]{0,1:T(8,128)(2,1)S(1)}, bf16[1024,64]{0,1:T(8,128)(2,1)}, u32[]{:S(2)}) copy-start(bf16[1024,64]{0,1:T(8,128)(2,1)} %copy-done.6) | copy-start | bytes 393220
  214.1 31.3 %copy-start.2 = (bf16[1024,864]{0,1:T(8,128)(2,1)S(1)}, bf16[1024,864]{0,1:T(8,128)(2,1)}, u32[]{:S(2)}) copy-start(bf16[1024,864]{0,1:T(8,128)(2,1)} %copy-done.1) | copy-start | bytes 5308420
  214.2 2.0 collective-permute-start
  216.2 14.9 %collective-permute-start.1 = (f32[1024,128]{0,1:T(8,128)S(1)}, f32[1024,128]{0,1:T(8,128)S(1)}, u32[]{:S(2)}, u32[]{:S(2)}) collective-permute-start(f32[1024,128]{0,1:T(8,128)S(1)} %fusion.18), channel_id=1, source_target_pairs={{0,2},{1,3},{2,0},{3,1},{4,6},{5,7},{6,4},{7,5},{8,10},{9,11},{10,... | collective-permute-start | bytes 1572872 | tf_op jit(solution)/shard_map/ppermute | solution.py:44
  231.1 30.6 %copy-start.4 = (bf16[1024,320]{0,1:T(8,128)(2,1)S(1)}, bf16[1024,320]{0,1:T(8,128)(2,1)}, u32[]{:S(2)}) copy-start(bf16[1024,320]{0,1:T(8,128)(2,1)} %param.10) | copy-start | bytes 1966084
  231.2 12.4 %collective-permute-start.2 = (f32[1024,128]{0,1:T(8,128)S(1)}, f32[1024,128]{0,1:T(8,128)S(1)}, u32[]{:S(2)}, u32[]{:S(2)}) collective-permute-start(f32[1024,128]{0,1:T(8,128)S(1)} %add.68), channel_id=1, source_target_pairs={{0,4},{1,5},{2,6},{3,7},{4,0},{5,1},{6,2},{7,3},{8,12},{9,13},{10,... | collective-permute-start | bytes 1572872 | tf_op jit(solution)/shard_map/ppermute | solution.py:44
  243.7 18.4 %copy-start.5 = (bf16[1024,320]{0,1:T(8,128)(2,1)S(1)}, bf16[1024,320]{0,1:T(8,128)(2,1)}, u32[]{:S(2)}) copy-start(bf16[1024,320]{0,1:T(8,128)(2,1)} %param.11) | copy-start | bytes 1966084
  243.7 18.0 %collective-permute-start.3 = (f32[1024,128]{0,1:T(8,128)S(1)}, f32[1024,128]{0,1:T(8,128)S(1)}, u32[]{:S(2)}, u32[]{:S(2)}) collective-permute-start(f32[1024,128]{0,1:T(8,128)S(1)} %add.69), channel_id=1, source_target_pairs={{0,8},{1,9},{2,10},{3,11},{4,12},{5,13},{6,14},{7,15},{8,0},{9,1},... | collective-permute-start | bytes 1572872 | tf_op jit(solution)/shard_map/ppermute | solution.py:44
  262.7 9.6 %collective-permute-start.4 = (f32[2368,64]{0,1:T(8,128)S(1)}, f32[2368,64]{0,1:T(8,128)S(1)}, u32[]{:S(2)}, u32[]{:S(2)}) collective-permute-start(f32[2368,64]{0,1:T(8,128)S(1)} %concatenate.7), channel_id=1, source_target_pairs={{0,16},{16,0},{32,48},{48,32},{64,80},{80,64},{96,112},{112,96},{1... | collective-permute-start | bytes 1818632 | tf_op jit(solution)/shard_map/ppermute | solution.py:44
  272.4 9.6 %collective-permute-start.5 = (f32[2368,64]{0,1:T(8,128)S(1)}, f32[2368,64]{0,1:T(8,128)S(1)}, u32[]{:S(2)}, u32[]{:S(2)}) collective-permute-start(f32[2368,64]{0,1:T(8,128)S(1)} %add.71), channel_id=1, source_target_pairs={{0,32},{16,48},{32,0},{48,16},{64,96},{80,112},{96,64},{112,80},{1... | collective-permute-start | bytes 1818632 | tf_op jit(solution)/shard_map/ppermute | solution.py:44
  282.0 13.9 %collective-permute-start.6 = (f32[2368,64]{0,1:T(8,128)S(1)}, f32[2368,64]{0,1:T(8,128)S(1)}, u32[]{:S(2)}, u32[]{:S(2)}) collective-permute-start(f32[2368,64]{0,1:T(8,128)S(1)} %add.72), channel_id=1, source_target_pairs={{0,64},{16,80},{32,96},{48,112},{64,0},{80,16},{96,32},{112,48},{1... | collective-permute-start | bytes 1818632 | tf_op jit(solution)/shard_map/ppermute | solution.py:44
  (3 other events, 3.6 us)
Sparse Core Ops, SparseCore 0:
  11.8 133.3 all-gather.1
  212.9 114.3 reduce-scatter.1

commit v6 on v5

--- a/solution.py
+++ b/solution.py
@@ -78,16 +78,15 @@
     grad_hidden = backward_sum + dot_rows(grad_low, outer_down)
     grad_pre = (grad_hidden * gelu_slope(pre)).astype(jnp.bfloat16)
     pre_low_part = dot_rows(grad_pre, inner_up)
-    block_part = dot_rows(grad_pre, inner_weight).astype(jnp.bfloat16).astype(jnp.float32)
-    low_part = dot_rows(pre_low_part.astype(jnp.bfloat16), inner_down)
-    tokens_grad = lax.psum_scatter(
-        (block_part + low_part).astype(jnp.bfloat16), "col", scatter_dimension=1, tiled=True
-    )
+    block_part = dot_rows(grad_pre, inner_weight).astype(jnp.bfloat16)
+    parts = lax.psum_scatter(block_part, "col", scatter_dimension=1, tiled=True)
 
     hidden_low_part = plain_dot(hidden, outer_down)
     lows = tree_sum(jnp.concatenate([hidden_low_part, pre_low_part], axis=1), "col", n_col)
     hidden_low = lows[:, :rank].astype(jnp.bfloat16)
     pre_low = lows[:, rank:].astype(jnp.bfloat16)
+    down_local = lax.dynamic_slice_in_dim(inner_down, col_index * local_width, local_width, 0)
+    tokens_grad = (parts.astype(jnp.float32) + dot_rows(pre_low, down_local)).astype(jnp.bfloat16)
 
     scale = 1.0 / math.sqrt(tok_rows * n_row)
     outer_down_term = dot_cols(hidden, grad_low)

time: 334 us -> 339 us (1.015)
  matrix products: 69.9 us -> 73.9 us
    dot_general x5, matrix products: 28.1 us -> 31.9 us  [dot_rows(): lax.dot_general(left, right, (((1,), (1,)), ((), ())), preferred_element_...]
  transfers between devices with their start and end apart: 9 -> 9, of which waited for: 9 -> 9; matrix products, arithmetic and copies ran while one was open for 1% -> 2% of each run, Pallas kernels for 0% -> 0%
where the time goes in v6:
time: 339 us
  waiting for transfers between devices  237 us (70%)
  matrix products  73.9 us (22%)
  between operations  14.4 us (4%)
  starting transfers between devices  5.91 us (2%)
  other arithmetic  4.06 us (1%)
  local copies, waits for them, and re-layouts  3.87 us (1%)
    all_gather x1, waiting for transfers between devices, local(): lax.all_gather(jnp.stack([tokens_in, gated_local]), 'col', axis=2, tiled=...  133 us
    ppermute x7, waiting for transfers between devices, tree_sum(): value = value + lax.ppermute(value, axis, pairs)  71.4 us
    dot_general x5, matrix products, plain_dot(): return jnp.dot(left, right, preferred_element_type=jnp.float32)  40 us
    reduce_scatter x1, waiting for transfers between devices, local(): parts = lax.psum_scatter(block_part, 'col', scatter_dimension=1, tiled=True)  32 us
    dot_general x5, matrix products, dot_rows(): lax.dot_general(left, right, (((1,), (1,)), ((), ())), preferred_element_...  31.9 us
  transfers between devices with their start and end apart: 9, of which 9 were waited for; matrix products, arithmetic and copies ran while one was open for 2% of the time, Pallas kernels for 0%

profile of v6, /device:TPU:1, one launch (start us, length us, event | category | flops | bytes accessed | tf_op | source)
XLA Modules:
  0.0 339.0 jit_solution(3759100685752369464)
XLA Ops:
  8.1 1.3 fusion.15
  9.3 2.3 pad_maximum_fusion
  11.7 133.4 %all-gather.2.cloned.1.call-done = bf16[2,1024,5120]{1,2,0:T(8,128)(2,1)} async-done(((bf16[2,1024,320]{1,2,0:T(8,128)(2,1)}), bf16[2,1024,5120]{1,2,0:T(8,128)(2,1)}) %all-gather.2.cloned.1.call-update) | async-done | bytes 20971536 | tf_op jit(solution)/shard_map/all_gather | solution.py:70
  145.2 6.1 %fusion.12 = bf16[1024,64]{0,1:T(8,128)(2,1)S(1)} fusion(bf16[5120,64]{0,1:T(8,128)(2,1)S(1)} %copy-done, bf16[2,1024,5120]{1,2,0:T(8,128)(2,1)} %all-gather.2.cloned.1.call-done), kind=kOutput, calls=%fused_computation.22 | convolution fusion | flops 671154176 | bytes 11272192 | tf_op jit(solution)/shard_map/dot_general | solution.py:25
  151.3 15.2 %fusion.2 = f32[1024,864]{0,1:T(8,128)} fusion(bf16[5120,864]{0,1:T(8,128)(2,1)} %param.13, bf16[2,1024,5120]{1,2,0:T(8,128)(2,1)} %all-gather.2.cloned.1.call-done), kind=kOutput, calls=%fused_computation.5 | convolution fusion | flops 9059696640 | bytes 22872064 | tf_op jit(solution)/shard_map/dot_general | solution.py:25
  166.5 5.4 %multiply_convert_fusion = (bf16[1024,864]{0,1:T(8,128)(2,1)S(1)}, f32[1024,864]{0,1:T(8,128)}) fusion(f32[864]{0:T(1024)S(1)} %copy-done.8, f32[1024,864]{0,1:T(8,128)} %fusion.2, bf16[1024,64]{0,1:T(8,128)(2,1)S(1)} %fusion.12, bf16[64,864]{1,0:T(8,128)(2,1)S(1)} %copy-done.5), kind=kOutput, calls=%fused_computation.16 | convolution fusion | flops 122978304 | bytes 9092480 | tf_op jit(solution)/shard_map/dot_general | solution.py:25
  171.9 1.9 fusion.13
  173.9 12.9 %fusion = f32[1024,864]{0,1:T(8,128)} fusion(bf16[5120,864]{0,1:T(8,128)(2,1)} %param.15, bf16[2,1024,5120]{1,2,0:T(8,128)(2,1)S(1)} %bitcast.42), kind=kOutput, calls=%fused_computation.3 | convolution fusion | flops 9059696640 | bytes 22872064 | tf_op jit(solution)/shard_map/dot_general | solution.py:25
  186.8 4.7 %fusion.10 = bf16[1024,864]{0,1:T(8,128)(2,1)S(1)} fusion(f32[1024,864]{0,1:T(8,128)} %get-tuple-element.10, f32[1024,864]{0,1:T(8,128)} %fusion, bf16[1024,64]{0,1:T(8,128)(2,1)S(1)} %fusion.13, bf16[864,64]{0,1:T(8,128)(2,1)S(1)} %copy-done.6), kind=kOutput, calls=%fused_computation.15 | convolution fusion | flops 130940928 | bytes 9089024 | tf_op jit(solution)/shard_map/dot_general | solution.py:29
  191.5 1.2 copy-done.1
  192.7 21.0 %convolution_convert_fusion = bf16[1024,5120]{0,1:T(8,128)(2,1)} fusion(bf16[1024,864]{0,1:T(8,128)(2,1)S(1)} %fusion.10, bf16[5120,864]{0,1:T(8,128)(2,1)} %param.13), kind=kOutput, calls=%fused_computation.2 | convolution fusion | flops 9064939520 | bytes 21102592 | tf_op jit(solution)/shard_map/dot_general | solution.py:29
  213.7 1.9 fusion.26
  216.5 1.7 collective-permute-done
  218.4 14.7 %collective-permute-done.1 = f32[1024,128]{0,1:T(8,128)S(1)} collective-permute-done((f32[1024,128]{0,1:T(8,128)S(1)}, f32[1024,128]{0,1:T(8,128)S(1)}, u32[]{:S(2)}, u32[]{:S(2)}) %collective-permute-start.1) | collective-permute-done | bytes 524320 | tf_op jit(solution)/shard_map/ppermute | solution.py:44
  233.3 12.3 %collective-permute-done.2 = f32[1024,128]{0,1:T(8,128)S(1)} collective-permute-done((f32[1024,128]{0,1:T(8,128)S(1)}, f32[1024,128]{0,1:T(8,128)S(1)}, u32[]{:S(2)}, u32[]{:S(2)}) %collective-permute-start.2) | collective-permute-done | bytes 524320 | tf_op jit(solution)/shard_map/ppermute | solution.py:44
  245.7 1.1 collective-permute-start.3
  248.1 16.7 %collective-permute-done.3 = f32[1024,128]{0,1:T(8,128)S(1)} collective-permute-done((f32[1024,128]{0,1:T(8,128)S(1)}, f32[1024,128]{0,1:T(8,128)S(1)}, u32[]{:S(2)}, u32[]{:S(2)}) %collective-permute-start.3) | collective-permute-done | bytes 524320 | tf_op jit(solution)/shard_map/ppermute | solution.py:44
  265.9 9.5 %collective-permute-done.4 = f32[2368,64]{0,1:T(8,128)S(1)} collective-permute-done((f32[2368,64]{0,1:T(8,128)S(1)}, f32[2368,64]{0,1:T(8,128)S(1)}, u32[]{:S(2)}, u32[]{:S(2)}) %collective-permute-start.4) | collective-permute-done | bytes 606240 | tf_op jit(solution)/shard_map/ppermute | solution.py:44
  275.5 1.2 collective-permute-start.5
  276.7 8.3 %collective-permute-done.5 = f32[2368,64]{0,1:T(8,128)S(1)} collective-permute-done((f32[2368,64]{0,1:T(8,128)S(1)}, f32[2368,64]{0,1:T(8,128)S(1)}, u32[]{:S(2)}, u32[]{:S(2)}) %collective-permute-start.5) | collective-permute-done | bytes 606240 | tf_op jit(solution)/shard_map/ppermute | solution.py:44
  285.1 2.8 collective-permute-start.6
  287.9 8.3 %collective-permute-done.6 = f32[2368,64]{0,1:T(8,128)S(1)} collective-permute-done((f32[2368,64]{0,1:T(8,128)S(1)}, f32[2368,64]{0,1:T(8,128)S(1)}, u32[]{:S(2)}, u32[]{:S(2)}) %collective-permute-start.6) | collective-permute-done | bytes 606240 | tf_op jit(solution)/shard_map/ppermute | solution.py:44
  297.8 32.0 %reduce-scatter.2.cloned.1.call-done = bf16[1024,320]{0,1:T(8,128)(2,1)} async-done(((bf16[1024,5120]{0,1:T(8,128)(2,1)}), bf16[1024,320]{0,1:T(8,128)(2,1)}) %reduce-scatter.2.cloned.1.call-update) | async-done | bytes 655376 | tf_op jit(solution)/shard_map/reduce_scatter | solution.py:82
  329.8 2.4 fusion.11
  (53 shorter events, 6.4 us)
Async XLA Ops:
  7.2 138.0 %copy-start = (bf16[5120,64]{0,1:T(8,128)(2,1)S(1)}, bf16[5120,64]{0,1:T(8,128)(2,1)}, u32[]{:S(2)}) copy-start(bf16[5120,64]{0,1:T(8,128)(2,1)} %param.16) | copy-start | bytes 1966084
  7.2 138.0 %all-gather.2.cloned.1.call-start = ((), (), s32[]{:S(2)}) async-start(), calls=%async_computation.1 | async-start | bytes 22282240 | tf_op jit(solution)/shard_map/all_gather | solution.py:70
  11.7 318.1 %reduce-scatter.2.cloned.1.call-start = ((), (), s32[]{:S(2)}) async-start(), calls=%async_computation.2 | async-start | bytes 11141120 | tf_op jit(solution)/shard_map/reduce_scatter | solution.py:82
  145.2 26.7 %slice-start = ((s8[20971520]{0:T(1024)(128)(4,1)}), s8[4194304]{0:T(1024)(128)(4,1)S(1)}, s32[]{:S(2)}) async-start(s8[20971520]{0:T(1024)(128)(4,1)} %bitcast.41), calls=%async_computation.3 | async-start | bytes 8388608
  151.2 15.3 %copy-start.5 = (bf16[64,864]{1,0:T(8,128)(2,1)S(1)}, bf16[64,864]{1,0:T(8,128)(2,1)}, u32[]{:S(2)}) copy-start(bf16[64,864]{1,0:T(8,128)(2,1)} %param.17) | copy-start | bytes 331780
  151.2 15.3 %copy-start.8 = (f32[864]{0:T(1024)S(1)}, f32[864]{0:T(1024)}, u32[]{:S(2)}) copy-start(f32[864]{0:T(1024)} %param.14) | copy-start | bytes 10372
  151.3 20.6 %slice-start.1 = ((s8[20971520]{0:T(1024)(128)(4,1)}), s8[4194304]{0:T(1024)(128)(4,1)S(1)}, s32[]{:S(2)}) async-start(s8[20971520]{0:T(1024)(128)(4,1)} %bitcast.41), calls=%async_computation.4 | async-start | bytes 8388608
  151.3 20.6 %slice-start.2 = ((s8[20971520]{0:T(1024)(128)(4,1)}), s8[4194304]{0:T(1024)(128)(4,1)S(1)}, s32[]{:S(2)}) async-start(s8[20971520]{0:T(1024)(128)(4,1)} %bitcast.41), calls=%async_computation.5 | async-start | bytes 8388608
  151.3 20.6 %slice-start.3 = ((s8[20971520]{0:T(1024)(128)(4,1)}), s8[4194304]{0:T(1024)(128)(4,1)S(1)}, s32[]{:S(2)}) async-start(s8[20971520]{0:T(1024)(128)(4,1)} %bitcast.41), calls=%async_computation.6 | async-start | bytes 8388608
  151.3 20.6 %slice-start.4 = ((s8[20971520]{0:T(1024)(128)(4,1)}), s8[4194304]{0:T(1024)(128)(4,1)S(1)}, s32[]{:S(2)}) async-start(s8[20971520]{0:T(1024)(128)(4,1)} %bitcast.41), calls=%async_computation.7 | async-start | bytes 8388608
  166.5 5.4 %copy-start.7 = (bf16[64,5120]{1,0:T(8,128)(2,1)S(1)}, bf16[64,5120]{1,0:T(8,128)(2,1)}, u32[]{:S(2)}) copy-start(bf16[64,5120]{1,0:T(8,128)(2,1)} %param.19) | copy-start | bytes 1966084
  173.9 12.9 %copy-start.6 = (bf16[864,64]{0,1:T(8,128)(2,1)S(1)}, bf16[864,64]{0,1:T(8,128)(2,1)}, u32[]{:S(2)}) copy-start(bf16[864,64]{0,1:T(8,128)(2,1)} %param.18) | copy-start | bytes 331780
  191.5 1.2 copy-start.1
  216.2 31.3 %copy-start.2 = (bf16[1024,864]{0,1:T(8,128)(2,1)S(1)}, bf16[1024,864]{0,1:T(8,128)(2,1)}, u32[]{:S(2)}) copy-start(bf16[1024,864]{0,1:T(8,128)(2,1)} %copy-done.1) | copy-start | bytes 5308420
  216.2 2.0 collective-permute-start
  218.2 14.9 %collective-permute-start.1 = (f32[1024,128]{0,1:T(8,128)S(1)}, f32[1024,128]{0,1:T(8,128)S(1)}, u32[]{:S(2)}, u32[]{:S(2)}) collective-permute-start(f32[1024,128]{0,1:T(8,128)S(1)} %fusion.21), channel_id=1, source_target_pairs={{0,2},{1,3},{2,0},{3,1},{4,6},{5,7},{6,4},{7,5},{8,10},{9,11},{10,... | collective-permute-start | bytes 1572872 | tf_op jit(solution)/shard_map/ppermute | solution.py:44
  233.1 31.7 %copy-start.3 = (bf16[1024,320]{0,1:T(8,128)(2,1)S(1)}, bf16[1024,320]{0,1:T(8,128)(2,1)}, u32[]{:S(2)}) copy-start(bf16[1024,320]{0,1:T(8,128)(2,1)} %param.10) | copy-start | bytes 1966084
  233.2 12.4 %collective-permute-start.2 = (f32[1024,128]{0,1:T(8,128)S(1)}, f32[1024,128]{0,1:T(8,128)S(1)}, u32[]{:S(2)}, u32[]{:S(2)}) collective-permute-start(f32[1024,128]{0,1:T(8,128)S(1)} %add.68), channel_id=1, source_target_pairs={{0,4},{1,5},{2,6},{3,7},{4,0},{5,1},{6,2},{7,3},{8,12},{9,13},{10,... | collective-permute-start | bytes 1572872 | tf_op jit(solution)/shard_map/ppermute | solution.py:44
  245.7 19.5 %copy-start.4 = (bf16[1024,320]{0,1:T(8,128)(2,1)S(1)}, bf16[1024,320]{0,1:T(8,128)(2,1)}, u32[]{:S(2)}) copy-start(bf16[1024,320]{0,1:T(8,128)(2,1)} %param.11) | copy-start | bytes 1966084
  245.7 19.1 %collective-permute-start.3 = (f32[1024,128]{0,1:T(8,128)S(1)}, f32[1024,128]{0,1:T(8,128)S(1)}, u32[]{:S(2)}, u32[]{:S(2)}) collective-permute-start(f32[1024,128]{0,1:T(8,128)S(1)} %add.69), channel_id=1, source_target_pairs={{0,8},{1,9},{2,10},{3,11},{4,12},{5,13},{6,14},{7,15},{8,0},{9,1},... | collective-permute-start | bytes 1572872 | tf_op jit(solution)/shard_map/ppermute | solution.py:44
  265.8 9.6 %collective-permute-start.4 = (f32[2368,64]{0,1:T(8,128)S(1)}, f32[2368,64]{0,1:T(8,128)S(1)}, u32[]{:S(2)}, u32[]{:S(2)}) collective-permute-start(f32[2368,64]{0,1:T(8,128)S(1)} %concatenate.7), channel_id=1, source_target_pairs={{0,16},{16,0},{32,48},{48,32},{64,80},{80,64},{96,112},{112,96},{1... | collective-permute-start | bytes 1818632 | tf_op jit(solution)/shard_map/ppermute | solution.py:44
  275.5 9.6 %collective-permute-start.5 = (f32[2368,64]{0,1:T(8,128)S(1)}, f32[2368,64]{0,1:T(8,128)S(1)}, u32[]{:S(2)}, u32[]{:S(2)}) collective-permute-start(f32[2368,64]{0,1:T(8,128)S(1)} %add.72), channel_id=1, source_target_pairs={{0,32},{16,48},{32,0},{48,16},{64,96},{80,112},{96,64},{112,80},{1... | collective-permute-start | bytes 1818632 | tf_op jit(solution)/shard_map/ppermute | solution.py:44
  285.1 11.1 %collective-permute-start.6 = (f32[2368,64]{0,1:T(8,128)S(1)}, f32[2368,64]{0,1:T(8,128)S(1)}, u32[]{:S(2)}, u32[]{:S(2)}) collective-permute-start(f32[2368,64]{0,1:T(8,128)S(1)} %add.73), channel_id=1, source_target_pairs={{0,64},{16,80},{32,96},{48,112},{64,0},{80,16},{96,32},{112,48},{1... | collective-permute-start | bytes 1818632 | tf_op jit(solution)/shard_map/ppermute | solution.py:44
Sparse Core Ops, SparseCore 0:
  11.8 133.3 all-gather.1
  213.9 115.8 reduce-scatter.1

commit v7 on v5

--- a/solution.py
+++ b/solution.py
@@ -69,9 +69,15 @@
     gated_local = (gain_local[None, :] * token_grad.astype(jnp.float32)).astype(jnp.bfloat16)
     both_full = lax.all_gather(jnp.stack([tokens_in, gated_local]), "col", axis=2, tiled=True)
     tokens_full, gated_full = both_full[0], both_full[1]
-    inner_low = plain_dot(tokens_full, inner_down).astype(jnp.bfloat16)
+    down_local = lax.dynamic_slice_in_dim(inner_down, col_index * local_width, local_width, 0)
+    up_local = lax.dynamic_slice_in_dim(outer_up, col_index * local_width, local_width, 1)
+    low_parts = jnp.concatenate(
+        [plain_dot(tokens_in, down_local), dot_rows(gated_local, up_local)], axis=1
+    )
+    low_sums = tree_sum(low_parts, "col", n_col)
+    inner_low = low_sums[:, :rank].astype(jnp.bfloat16)
+    grad_low = low_sums[:, rank:].astype(jnp.bfloat16)
     forward_sum = plain_dot(tokens_full, inner_weight)
-    grad_low = dot_rows(gated_full, outer_up).astype(jnp.bfloat16)
     backward_sum = plain_dot(gated_full, outer_weight)
     pre = forward_sum + plain_dot(inner_low, inner_up) + inner_bias[None, :]
     hidden = gelu_value(pre).astype(jnp.bfloat16)

time: 334 us -> 340 us (1.018)
  starting transfers between devices: 6.08 us -> 15.6 us
    all_gather x1, waiting for transfers between devices: 133 us -> 83.6 us  [local(): lax.all_gather(jnp.stack([tokens_in, gated_local]), 'col', axis=2, tiled=...]
    ppermute x7 -> x11, waiting for transfers between devices: 73 us -> 120 us  [tree_sum(): value = value + lax.ppermute(value, axis, pairs)]
    ppermute x7 -> x11, starting transfers between devices: 6 us -> 15.5 us  [tree_sum(): value = value + lax.ppermute(value, axis, pairs)]
    dot_general x5, matrix products: 39.7 us -> 36 us  [plain_dot(): return jnp.dot(left, right, preferred_element_type=jnp.float32)]
  transfers between devices with their start and end apart: 9 -> 13, of which waited for: 9 -> 13; matrix products, arithmetic and copies ran while one was open for 1% -> 3% of each run, Pallas kernels for 0% -> 0%
where the time goes in v7:
time: 340 us
  waiting for transfers between devices  234 us (69%)
  matrix products  66.9 us (20%)
  starting transfers between devices  15.6 us (5%)
  between operations  14.3 us (4%)
  other arithmetic  4.37 us (1%)
  local copies, waits for them, and re-layouts  4.24 us (1%)
    ppermute x11, waiting for transfers between devices, tree_sum(): value = value + lax.ppermute(value, axis, pairs)  120 us
    all_gather x1, waiting for transfers between devices, local(): lax.all_gather(jnp.stack([tokens_in, gated_local]), 'col', axis=2, tiled=...  83.6 us
    dot_general x5, matrix products, plain_dot(): return jnp.dot(left, right, preferred_element_type=jnp.float32)  36 us
    reduce_scatter x1, waiting for transfers between devices, local(): lax.psum_scatter((block_part + low_part).astype(jnp.bfloat16), 'col', sca...  30.8 us
    dot_general x5, matrix products, dot_rows(): lax.dot_general(left, right, (((1,), (1,)), ((), ())), preferred_element_...  27.4 us
    ppermute x11, starting transfers between devices, tree_sum(): value = value + lax.ppermute(value, axis, pairs)  15.5 us
  transfers between devices with their start and end apart: 13, of which 13 were waited for; matrix products, arithmetic and copies ran while one was open for 3% of the time, Pallas kernels for 0%

profile of v7, /device:TPU:1, one launch (start us, length us, event | category | flops | bytes accessed | tf_op | source)
XLA Modules:
  0.0 339.7 jit_solution(6539134465080865069)
XLA Ops:
  9.4 2.3 pad_maximum_fusion
  13.4 1.5 collective-permute-start
  14.9 1.5 collective-permute-done
  16.5 3.8 %collective-permute-start.1 = (f32[1024,128]{0,1:T(8,128)S(1)}, f32[1024,128]{0,1:T(8,128)S(1)}, u32[]{:S(2)}, u32[]{:S(2)}) collective-permute-start(f32[1024,128]{0,1:T(8,128)S(1)} %fusion.25), channel_id=1, source_target_pairs={{0,2},{1,3},{2,0},{3,1},{4,6},{5,7},{6,4},{7,5},{8,10},{9,11},{10,... | collective-permute-start | bytes 1572872 | tf_op jit(solution)/shard_map/ppermute | solution.py:44
  20.3 14.9 %collective-permute-done.1 = f32[1024,128]{0,1:T(8,128)S(1)} collective-permute-done((f32[1024,128]{0,1:T(8,128)S(1)}, f32[1024,128]{0,1:T(8,128)S(1)}, u32[]{:S(2)}, u32[]{:S(2)}) %collective-permute-start.1) | collective-permute-done | bytes 524320 | tf_op jit(solution)/shard_map/ppermute | solution.py:44
  36.5 19.6 %collective-permute-done.2 = f32[1024,128]{0,1:T(8,128)S(1)} collective-permute-done((f32[1024,128]{0,1:T(8,128)S(1)}, f32[1024,128]{0,1:T(8,128)S(1)}, u32[]{:S(2)}, u32[]{:S(2)}) %collective-permute-start.2) | collective-permute-done | bytes 524320 | tf_op jit(solution)/shard_map/ppermute | solution.py:44
  56.2 3.0 collective-permute-start.3
  59.2 13.5 %collective-permute-done.3 = f32[1024,128]{0,1:T(8,128)S(1)} collective-permute-done((f32[1024,128]{0,1:T(8,128)S(1)}, f32[1024,128]{0,1:T(8,128)S(1)}, u32[]{:S(2)}, u32[]{:S(2)}) %collective-permute-start.3) | collective-permute-done | bytes 524320 | tf_op jit(solution)/shard_map/ppermute | solution.py:44
  72.8 83.6 %all-gather.2.cloned.1.call-done = bf16[2,1024,5120]{1,2,0:T(8,128)(2,1)} async-done(((bf16[2,1024,320]{1,2,0:T(8,128)(2,1)}), bf16[2,1024,5120]{1,2,0:T(8,128)(2,1)}) %all-gather.2.cloned.1.call-update) | async-done | bytes 20971536 | tf_op jit(solution)/shard_map/all_gather | solution.py:70
  156.4 17.5 %fusion = f32[1024,864]{0,1:T(8,128)} fusion(bf16[5120,864]{0,1:T(8,128)(2,1)} %param.13, bf16[2,1024,5120]{1,2,0:T(8,128)(2,1)} %all-gather.2.cloned.1.call-done), kind=kOutput, calls=%fused_computation.2 | convolution fusion | flops 9059696640 | bytes 22872064 | tf_op jit(solution)/shard_map/dot_general | solution.py:25
  173.8 5.3 %multiply_convert_fusion = (bf16[1024,864]{0,1:T(8,128)(2,1)S(1)}, f32[1024,864]{0,1:T(8,128)}) fusion(f32[864]{0:T(1024)S(1)} %copy-done.13, f32[1024,864]{0,1:T(8,128)} %fusion, bf16[64,864]{1,0:T(8,128)(2,1)S(1)} %copy-done.10, bf16[1024,128]{0,1:T(8,128)(2,1)S(1)} %add_convert_fusion.2), kind=kOutput, calls=%fused_computation.14 | convolution fusion | flops 122978304 | bytes 9097216 | tf_op jit(solution)/shard_map/dot_general | solution.py:25
  179.2 12.5 %fusion.1 = f32[1024,864]{0,1:T(8,128)} fusion(bf16[5120,864]{0,1:T(8,128)(2,1)} %param.15, bf16[2,1024,5120]{1,2,0:T(8,128)(2,1)S(1)} %copy-done.12), kind=kOutput, calls=%fused_computation.4 | convolution fusion | flops 9059696640 | bytes 22872064 | tf_op jit(solution)/shard_map/dot_general | solution.py:25
  191.7 4.7 %fusion.8 = bf16[1024,864]{0,1:T(8,128)(2,1)S(1)} fusion(f32[1024,864]{0,1:T(8,128)} %get-tuple-element.10, f32[1024,864]{0,1:T(8,128)} %fusion.1, bf16[864,64]{0,1:T(8,128)(2,1)S(1)} %copy-done.11, bf16[1024,128]{0,1:T(8,128)(2,1)S(1)} %add_convert_fusion.2), kind=kOutput, calls=%fused_computation.13 | convolution fusion | flops 130940928 | bytes 9093120 | tf_op jit(solution)/shard_map/dot_general | solution.py:29
  197.7 13.6 %fusion.28 = bf16[1024,5120]{0,1:T(8,128)(2,1)S(1)} fusion(bf16[1024,864]{0,1:T(8,128)(2,1)S(1)} %fusion.8, bf16[5120,864]{0,1:T(8,128)(2,1)} %param.13), kind=kOutput, calls=%fused_computation.46 | convolution fusion | flops 9059696640 | bytes 21102592 | tf_op jit(solution)/shard_map/dot_general | solution.py:29
  211.3 6.6 %add_convert_fusion = bf16[1024,5120]{0,1:T(8,128)(2,1)} fusion(bf16[5120,64]{0,1:T(8,128)(2,1)S(1)} %copy-done, bf16[1024,5120]{0,1:T(8,128)(2,1)S(1)} %fusion.28, f32[1024,64]{0,1:T(8,128)} %fusion.29), kind=kOutput, calls=%fused_computation | convolution fusion | flops 686882816 | bytes 21889024 | tf_op jit(solution)/shard_map/dot_general | solution.py:29
  219.2 1.7 collective-permute-done.4
  221.1 14.7 %collective-permute-done.5 = f32[1024,128]{0,1:T(8,128)S(1)} collective-permute-done((f32[1024,128]{0,1:T(8,128)S(1)}, f32[1024,128]{0,1:T(8,128)S(1)}, u32[]{:S(2)}, u32[]{:S(2)}) %collective-permute-start.5) | collective-permute-done | bytes 524320 | tf_op jit(solution)/shard_map/ppermute | solution.py:44
  236.0 12.3 %collective-permute-done.6 = f32[1024,128]{0,1:T(8,128)S(1)} collective-permute-done((f32[1024,128]{0,1:T(8,128)S(1)}, f32[1024,128]{0,1:T(8,128)S(1)}, u32[]{:S(2)}, u32[]{:S(2)}) %collective-permute-start.6) | collective-permute-done | bytes 524320 | tf_op jit(solution)/shard_map/ppermute | solution.py:44
  252.2 13.7 %collective-permute-done.7 = f32[1024,128]{0,1:T(8,128)S(1)} collective-permute-done((f32[1024,128]{0,1:T(8,128)S(1)}, f32[1024,128]{0,1:T(8,128)S(1)}, u32[]{:S(2)}, u32[]{:S(2)}) %collective-permute-start.7) | collective-permute-done | bytes 524320 | tf_op jit(solution)/shard_map/ppermute | solution.py:44
  268.1 9.5 %collective-permute-done.8 = f32[2368,64]{0,1:T(8,128)S(1)} collective-permute-done((f32[2368,64]{0,1:T(8,128)S(1)}, f32[2368,64]{0,1:T(8,128)S(1)}, u32[]{:S(2)}, u32[]{:S(2)}) %collective-permute-start.8) | collective-permute-done | bytes 606240 | tf_op jit(solution)/shard_map/ppermute | solution.py:44
  279.1 8.2 %collective-permute-done.9 = f32[2368,64]{0,1:T(8,128)S(1)} collective-permute-done((f32[2368,64]{0,1:T(8,128)S(1)}, f32[2368,64]{0,1:T(8,128)S(1)}, u32[]{:S(2)}, u32[]{:S(2)}) %collective-permute-start.9) | collective-permute-done | bytes 606240 | tf_op jit(solution)/shard_map/ppermute | solution.py:44
  287.3 2.8 collective-permute-start.10
  290.1 10.3 %collective-permute-done.10 = f32[2368,64]{0,1:T(8,128)S(1)} collective-permute-done((f32[2368,64]{0,1:T(8,128)S(1)}, f32[2368,64]{0,1:T(8,128)S(1)}, u32[]{:S(2)}, u32[]{:S(2)}) %collective-permute-start.10) | collective-permute-done | bytes 606240 | tf_op jit(solution)/shard_map/ppermute | solution.py:44
  302.0 30.8 %reduce-scatter.2.cloned.1.call-done = bf16[1024,320]{0,1:T(8,128)(2,1)} async-done(((bf16[1024,5120]{0,1:T(8,128)(2,1)}), bf16[1024,320]{0,1:T(8,128)(2,1)}) %reduce-scatter.2.cloned.1.call-update) | async-done | bytes 655376 | tf_op jit(solution)/shard_map/reduce_scatter | solution.py:89
  (65 shorter events, 17.5 us)
Async XLA Ops:
  7.2 4.7 %copy-start = (bf16[5120,64]{0,1:T(8,128)(2,1)S(1)}, bf16[5120,64]{0,1:T(8,128)(2,1)}, u32[]{:S(2)}) copy-start(bf16[5120,64]{0,1:T(8,128)(2,1)} %param.16) | copy-start | bytes 1966084
  7.2 5.0 %copy-start.6 = (bf16[1024,320]{0,1:T(8,128)(2,1)S(1)}, bf16[1024,320]{0,1:T(8,128)(2,1)}, u32[]{:S(2)}) copy-start(bf16[1024,320]{0,1:T(8,128)(2,1)} %param.11) | copy-start | bytes 1966084
  7.2 149.2 %all-gather.2.cloned.1.call-start = ((), (), s32[]{:S(2)}) async-start(), calls=%async_computation.1 | async-start | bytes 22282240 | tf_op jit(solution)/shard_map/all_gather | solution.py:70
  11.8 321.0 %reduce-scatter.2.cloned.1.call-start = ((), (), s32[]{:S(2)}) async-start(), calls=%async_computation.2 | async-start | bytes 11141120 | tf_op jit(solution)/shard_map/reduce_scatter | solution.py:89
  13.4 3.0 collective-permute-start
  16.5 18.7 %collective-permute-start.1 = (f32[1024,128]{0,1:T(8,128)S(1)}, f32[1024,128]{0,1:T(8,128)S(1)}, u32[]{:S(2)}, u32[]{:S(2)}) collective-permute-start(f32[1024,128]{0,1:T(8,128)S(1)} %fusion.25), channel_id=1, source_target_pairs={{0,2},{1,3},{2,0},{3,1},{4,6},{5,7},{6,4},{7,5},{8,10},{9,11},{10,... | collective-permute-start | bytes 1572872 | tf_op jit(solution)/shard_map/ppermute | solution.py:44
  35.3 20.9 %collective-permute-start.2 = (f32[1024,128]{0,1:T(8,128)S(1)}, f32[1024,128]{0,1:T(8,128)S(1)}, u32[]{:S(2)}, u32[]{:S(2)}) collective-permute-start(f32[1024,128]{0,1:T(8,128)S(1)} %add.73), channel_id=1, source_target_pairs={{0,4},{1,5},{2,6},{3,7},{4,0},{5,1},{6,2},{7,3},{8,12},{9,13},{10,... | collective-permute-start | bytes 1572872 | tf_op jit(solution)/shard_map/ppermute | solution.py:44
  56.2 16.5 %collective-permute-start.3 = (f32[1024,128]{0,1:T(8,128)S(1)}, f32[1024,128]{0,1:T(8,128)S(1)}, u32[]{:S(2)}, u32[]{:S(2)}) collective-permute-start(f32[1024,128]{0,1:T(8,128)S(1)} %add.74), channel_id=1, source_target_pairs={{0,8},{1,9},{2,10},{3,11},{4,12},{5,13},{6,14},{7,15},{8,0},{9,1},... | collective-permute-start | bytes 1572872 | tf_op jit(solution)/shard_map/ppermute | solution.py:44
  72.8 118.9 %copy-start.8 = (bf16[1024,128]{0,1:T(8,128)(2,1)}, bf16[1024,128]{0,1:T(8,128)(2,1)S(1)}, u32[]{:S(2)}) copy-start(bf16[1024,128]{0,1:T(8,128)(2,1)S(1)} %add_convert_fusion.2) | copy-start | bytes 786436
  72.8 101.1 %copy-start.10 = (bf16[64,864]{1,0:T(8,128)(2,1)S(1)}, bf16[64,864]{1,0:T(8,128)(2,1)}, u32[]{:S(2)}) copy-start(bf16[64,864]{1,0:T(8,128)(2,1)} %param.17) | copy-start | bytes 331780
  72.8 101.1 %copy-start.13 = (f32[864]{0:T(1024)S(1)}, f32[864]{0:T(1024)}, u32[]{:S(2)}) copy-start(f32[864]{0:T(1024)} %param.14) | copy-start | bytes 10372
  156.4 22.8 %copy-start.12 = (bf16[2,1024,5120]{1,2,0:T(8,128)(2,1)S(1)}, bf16[2,1024,5120]{1,2,0:T(8,128)(2,1)}, u32[]{:S(2)}) copy-start(bf16[2,1024,5120]{1,2,0:T(8,128)(2,1)} %all-gather.2.cloned.1.call-done) | copy-start | bytes 62914564
  179.2 12.5 %copy-start.11 = (bf16[864,64]{0,1:T(8,128)(2,1)S(1)}, bf16[864,64]{0,1:T(8,128)(2,1)}, u32[]{:S(2)}) copy-start(bf16[864,64]{0,1:T(8,128)(2,1)} %param.18) | copy-start | bytes 331780
  217.9 31.6 %copy-start.2 = (bf16[1024,864]{0,1:T(8,128)(2,1)S(1)}, bf16[1024,864]{0,1:T(8,128)(2,1)}, u32[]{:S(2)}) copy-start(bf16[1024,864]{0,1:T(8,128)(2,1)} %copy-done.1) | copy-start | bytes 5308420
  217.9 31.6 %copy-start.9 = (bf16[1024,128]{0,1:T(8,128)(2,1)S(1)}, bf16[1024,128]{0,1:T(8,128)(2,1)}, u32[]{:S(2)}) copy-start(bf16[1024,128]{0,1:T(8,128)(2,1)} %copy-done.8) | copy-start | bytes 786436
  218.9 2.0 collective-permute-start.4
  220.9 14.9 %collective-permute-start.5 = (f32[1024,128]{0,1:T(8,128)S(1)}, f32[1024,128]{0,1:T(8,128)S(1)}, u32[]{:S(2)}, u32[]{:S(2)}) collective-permute-start(f32[1024,128]{0,1:T(8,128)S(1)} %fusion.24), channel_id=1, source_target_pairs={{0,2},{1,3},{2,0},{3,1},{4,6},{5,7},{6,4},{7,5},{8,10},{9,11},{10,... | collective-permute-start | bytes 1572872 | tf_op jit(solution)/shard_map/ppermute | solution.py:44
  235.9 30.1 %copy-start.4 = (bf16[1024,320]{0,1:T(8,128)(2,1)S(1)}, bf16[1024,320]{0,1:T(8,128)(2,1)}, u32[]{:S(2)}) copy-start(bf16[1024,320]{0,1:T(8,128)(2,1)} %param.10) | copy-start | bytes 1966084
  235.9 12.4 %collective-permute-start.6 = (f32[1024,128]{0,1:T(8,128)S(1)}, f32[1024,128]{0,1:T(8,128)S(1)}, u32[]{:S(2)}, u32[]{:S(2)}) collective-permute-start(f32[1024,128]{0,1:T(8,128)S(1)} %add.86), channel_id=1, source_target_pairs={{0,4},{1,5},{2,6},{3,7},{4,0},{5,1},{6,2},{7,3},{8,12},{9,13},{10,... | collective-permute-start | bytes 1572872 | tf_op jit(solution)/shard_map/ppermute | solution.py:44
  248.4 18.0 %copy-start.7 = (bf16[1024,320]{0,1:T(8,128)(2,1)S(1)}, bf16[1024,320]{0,1:T(8,128)(2,1)}, u32[]{:S(2)}) copy-start(bf16[1024,320]{0,1:T(8,128)(2,1)} %param.11) | copy-start | bytes 1966084
  248.4 17.5 %collective-permute-start.7 = (f32[1024,128]{0,1:T(8,128)S(1)}, f32[1024,128]{0,1:T(8,128)S(1)}, u32[]{:S(2)}, u32[]{:S(2)}) collective-permute-start(f32[1024,128]{0,1:T(8,128)S(1)} %add.87), channel_id=1, source_target_pairs={{0,8},{1,9},{2,10},{3,11},{4,12},{5,13},{6,14},{7,15},{8,0},{9,1},... | collective-permute-start | bytes 1572872 | tf_op jit(solution)/shard_map/ppermute | solution.py:44
  268.0 9.6 %collective-permute-start.8 = (f32[2368,64]{0,1:T(8,128)S(1)}, f32[2368,64]{0,1:T(8,128)S(1)}, u32[]{:S(2)}, u32[]{:S(2)}) collective-permute-start(f32[2368,64]{0,1:T(8,128)S(1)} %concatenate.11), channel_id=1, source_target_pairs={{0,16},{16,0},{32,48},{48,32},{64,80},{80,64},{96,112},{112,96},{1... | collective-permute-start | bytes 1818632 | tf_op jit(solution)/shard_map/ppermute | solution.py:44
  277.7 9.6 %collective-permute-start.9 = (f32[2368,64]{0,1:T(8,128)S(1)}, f32[2368,64]{0,1:T(8,128)S(1)}, u32[]{:S(2)}, u32[]{:S(2)}) collective-permute-start(f32[2368,64]{0,1:T(8,128)S(1)} %add.89), channel_id=1, source_target_pairs={{0,32},{16,48},{32,0},{48,16},{64,96},{80,112},{96,64},{112,80},{1... | collective-permute-start | bytes 1818632 | tf_op jit(solution)/shard_map/ppermute | solution.py:44
  287.3 13.1 %collective-permute-start.10 = (f32[2368,64]{0,1:T(8,128)S(1)}, f32[2368,64]{0,1:T(8,128)S(1)}, u32[]{:S(2)}, u32[]{:S(2)}) collective-permute-start(f32[2368,64]{0,1:T(8,128)S(1)} %add.90), channel_id=1, source_target_pairs={{0,64},{16,80},{32,96},{48,112},{64,0},{80,16},{96,32},{112,48},{1... | collective-permute-start | bytes 1818632 | tf_op jit(solution)/shard_map/ppermute | solution.py:44
  (3 other events, 6.9 us)
Sparse Core Ops, SparseCore 0:
  11.9 144.4 all-gather.1
  218.0 114.7 reduce-scatter.1

commit v8 on v6

--- a/solution.py
+++ b/solution.py
@@ -69,24 +69,27 @@
     gated_local = (gain_local[None, :] * token_grad.astype(jnp.float32)).astype(jnp.bfloat16)
     both_full = lax.all_gather(jnp.stack([tokens_in, gated_local]), "col", axis=2, tiled=True)
     tokens_full, gated_full = both_full[0], both_full[1]
-    inner_low = plain_dot(tokens_full, inner_down).astype(jnp.bfloat16)
-    forward_sum = plain_dot(tokens_full, inner_weight)
-    grad_low = dot_rows(gated_full, outer_up).astype(jnp.bfloat16)
-    backward_sum = plain_dot(gated_full, outer_weight)
+    inner_cat = jnp.concatenate([inner_weight, inner_down], axis=1)
+    outer_cat = jnp.concatenate([outer_weight, outer_up.T], axis=1)
+    forward_all = plain_dot(tokens_full, inner_cat)
+    forward_sum = forward_all[:, :ff_local]
+    inner_low = forward_all[:, ff_local:].astype(jnp.bfloat16)
+    backward_all = plain_dot(gated_full, outer_cat)
+    backward_sum = backward_all[:, :ff_local]
+    grad_low = backward_all[:, ff_local:].astype(jnp.bfloat16)
     pre = forward_sum + plain_dot(inner_low, inner_up) + inner_bias[None, :]
     hidden = gelu_value(pre).astype(jnp.bfloat16)
     grad_hidden = backward_sum + dot_rows(grad_low, outer_down)
     grad_pre = (grad_hidden * gelu_slope(pre)).astype(jnp.bfloat16)
     pre_low_part = dot_rows(grad_pre, inner_up)
-    block_part = dot_rows(grad_pre, inner_weight).astype(jnp.bfloat16)
-    parts = lax.psum_scatter(block_part, "col", scatter_dimension=1, tiled=True)
+    grad_pre_cat = jnp.concatenate([grad_pre, pre_low_part.astype(jnp.bfloat16)], axis=1)
+    block_part = dot_rows(grad_pre_cat, inner_cat).astype(jnp.bfloat16)
+    tokens_grad = lax.psum_scatter(block_part, "col", scatter_dimension=1, tiled=True)
 
     hidden_low_part = plain_dot(hidden, outer_down)
     lows = tree_sum(jnp.concatenate([hidden_low_part, pre_low_part], axis=1), "col", n_col)
     hidden_low = lows[:, :rank].astype(jnp.bfloat16)
     pre_low = lows[:, rank:].astype(jnp.bfloat16)
-    down_local = lax.dynamic_slice_in_dim(inner_down, col_index * local_width, local_width, 0)
-    tokens_grad = (parts.astype(jnp.float32) + dot_rows(pre_low, down_local)).astype(jnp.bfloat16)
 
     scale = 1.0 / math.sqrt(tok_rows * n_row)
     outer_down_term = dot_cols(hidden, grad_low)

time: 339 us -> 331 us (0.976)
  waiting for transfers between devices: 237 us -> 227 us
  local copies, waits for them, and re-layouts: 3.87 us -> 11.1 us
  matrix products: 73.9 us -> 68.6 us
    all_gather x1, waiting for transfers between devices: 133 us -> 125 us  [local(): lax.all_gather(jnp.stack([tokens_in, gated_local]), 'col', axis=2, tiled=...]
    unnamed x28 -> x21, local copies, waits for them, and re-layouts: 1.28 us -> 7.66 us
    dot_general x5 -> x4, matrix products: 40 us -> 35.9 us  [plain_dot(): return jnp.dot(left, right, preferred_element_type=jnp.float32)]
    dot_general x5 -> x3, matrix products: 31.9 us -> 28.8 us  [dot_rows(): lax.dot_general(left, right, (((1,), (1,)), ((), ())), preferred_element_...]
  transfers between devices with their start and end apart: 9 -> 9, of which waited for: 9 -> 9; matrix products, arithmetic and copies ran while one was open for 2% -> 5% of each run, Pallas kernels for 0% -> 0%
where the time goes in v8:
time: 331 us; the launch traced here: 330 us
  waiting for transfers between devices  227 us (69%)
  matrix products  68.6 us (21%)
  between operations  14.3 us (4%)
  local copies, waits for them, and re-layouts  11.1 us (3%)
  starting transfers between devices  5.76 us (2%)
  other arithmetic  4.03 us (1%)
    all_gather x1, waiting for transfers between devices, local(): lax.all_gather(jnp.stack([tokens_in, gated_local]), 'col', axis=2, tiled=...  125 us
    ppermute x7, waiting for transfers between devices, tree_sum(): value = value + lax.ppermute(value, axis, pairs)  69.3 us
    dot_general x4, matrix products, plain_dot(): return jnp.dot(left, right, preferred_element_type=jnp.float32)  35.9 us
    reduce_scatter x1, waiting for transfers between devices, local(): lax.psum_scatter(block_part, 'col', scatter_dimension=1, tiled=True)  32.3 us
    dot_general x3, matrix products, dot_rows(): lax.dot_general(left, right, (((1,), (1,)), ((), ())), preferred_element_...  28.8 us
    unnamed x21, local copies, waits for them, and re-layouts  7.66 us
  transfers between devices with their start and end apart: 9, of which 9 were waited for; matrix products, arithmetic and copies ran while one was open for 5% of the time, Pallas kernels for 0%

profile of v8, /device:TPU:1, one launch (start us, length us, event | category | flops | bytes accessed | tf_op | source)
XLA Modules:
  0.0 330.3 jit_solution(69463386746513889)
XLA Ops:
  8.0 1.3 fusion.17
  9.3 2.3 pad_maximum_fusion
  11.6 7.6 %constant_dynamic-update-slice_fusion.1 = bf16[5120,928]{0,1:T(8,128)(2,1)} fusion(bf16[5120,864]{0,1:T(8,128)(2,1)} %param.13), kind=kLoop, calls=%fused_computation.41 | loop fusion | bytes 17694720
  19.2 0.9 constant_dynamic-update-slice_fusion
  20.1 124.9 %all-gather.2.cloned.1.call-done = bf16[2,1024,5120]{1,2,0:T(8,128)(2,1)} async-done(((bf16[2,1024,320]{1,2,0:T(8,128)(2,1)}), bf16[2,1024,5120]{1,2,0:T(8,128)(2,1)}) %all-gather.2.cloned.1.call-update) | async-done | bytes 20971536 | tf_op jit(solution)/shard_map/all_gather | solution.py:70
  145.1 14.2 %fusion = f32[1024,928]{0,1:T(8,128)S(1)} fusion(bf16[5120,928]{0,1:T(8,128)(2,1)} %constant_dynamic-update-slice_fusion, bf16[2,1024,5120]{1,2,0:T(8,128)(2,1)} %all-gather.2.cloned.1.call-done), kind=kOutput, calls=%fused_computation.1 | convolution fusion | flops 9730785280 | bytes 23789568 | tf_op jit(solution)/shard_map/dot_general | solution.py:25
  159.3 3.9 %multiply_convert_fusion = (bf16[1024,864]{0,1:T(8,128)(2,1)}, f32[1024,864]{0,1:T(8,128)}) fusion(f32[864]{0:T(1024)S(1)} %copy-done.9, bf16[64,864]{1,0:T(8,128)(2,1)S(1)} %copy-done, f32[1024,928]{0,1:T(8,128)S(1)} %fusion), kind=kOutput, calls=%fused_computation.20 | convolution fusion | flops 123043840 | bytes 9223552 | tf_op jit(solution)/shard_map/dot_general | solution.py:25
  163.2 15.9 %fusion.1 = f32[1024,928]{0,1:T(8,128)S(1)} fusion(bf16[2,1024,5120]{1,2,0:T(8,128)(2,1)} %all-gather.2.cloned.1.call-done, bf16[5120,64]{0,1:T(8,128)(2,1)S(1)} %bitcast.28, bf16[5120,864]{0,1:T(8,128)(2,1)} %param.15), kind=kOutput, calls=%fused_computation.3 | convolution fusion | flops 9749790720 | bytes 23789568 | tf_op jit(solution)/shard_map/dot_general | solution.py:25
  179.1 5.5 %fusion.11 = bf16[1024,864]{0,1:T(8,128)(2,1)S(1)} fusion(f32[1024,864]{0,1:T(8,128)} %get-tuple-element.12, f32[1024,928]{0,1:T(8,128)S(1)} %fusion.1, bf16[864,64]{0,1:T(8,128)(2,1)S(1)} %copy-done.5), kind=kOutput, calls=%fused_computation.16 | convolution fusion | flops 131006464 | bytes 9220096 | tf_op jit(solution)/shard_map/dot_general | solution.py:29
  185.1 22.8 %convolution_convert_fusion = bf16[1024,5120]{0,1:T(8,128)(2,1)} fusion(bf16[5120,928]{0,1:T(8,128)(2,1)} %constant_dynamic-update-slice_fusion, bf16[1024,64]{0,1:T(8,128)(2,1)S(1)} %get-tuple-element.9, bf16[1024,864]{0,1:T(8,128)(2,1)S(1)} %fusion.11), kind=kOutput, calls=%fused_computation.7 | convolution fusion | flops 9739829248 | bytes 21889024 | tf_op jit(solution)/shard_map/dot_general | solution.py:29
  207.9 1.9 fusion.27
  210.2 1.7 collective-permute-done
  212.1 14.7 %collective-permute-done.1 = f32[1024,128]{0,1:T(8,128)S(1)} collective-permute-done((f32[1024,128]{0,1:T(8,128)S(1)}, f32[1024,128]{0,1:T(8,128)S(1)}, u32[]{:S(2)}, u32[]{:S(2)}) %collective-permute-start.1) | collective-permute-done | bytes 524320 | tf_op jit(solution)/shard_map/ppermute | solution.py:44
  227.0 12.3 %collective-permute-done.2 = f32[1024,128]{0,1:T(8,128)S(1)} collective-permute-done((f32[1024,128]{0,1:T(8,128)S(1)}, f32[1024,128]{0,1:T(8,128)S(1)}, u32[]{:S(2)}, u32[]{:S(2)}) %collective-permute-start.2) | collective-permute-done | bytes 524320 | tf_op jit(solution)/shard_map/ppermute | solution.py:44
  239.4 1.1 collective-permute-start.3
  240.5 1.6 fusion.21
  242.1 1.6 fusion.20
  243.7 14.4 %collective-permute-done.3 = f32[1024,128]{0,1:T(8,128)S(1)} collective-permute-done((f32[1024,128]{0,1:T(8,128)S(1)}, f32[1024,128]{0,1:T(8,128)S(1)}, u32[]{:S(2)}, u32[]{:S(2)}) %collective-permute-start.3) | collective-permute-done | bytes 524320 | tf_op jit(solution)/shard_map/ppermute | solution.py:44
  259.3 9.5 %collective-permute-done.4 = f32[2368,64]{0,1:T(8,128)S(1)} collective-permute-done((f32[2368,64]{0,1:T(8,128)S(1)}, f32[2368,64]{0,1:T(8,128)S(1)}, u32[]{:S(2)}, u32[]{:S(2)}) %collective-permute-start.4) | collective-permute-done | bytes 606240 | tf_op jit(solution)/shard_map/ppermute | solution.py:44
  268.8 1.2 collective-permute-start.5
  270.1 8.3 %collective-permute-done.5 = f32[2368,64]{0,1:T(8,128)S(1)} collective-permute-done((f32[2368,64]{0,1:T(8,128)S(1)}, f32[2368,64]{0,1:T(8,128)S(1)}, u32[]{:S(2)}, u32[]{:S(2)}) %collective-permute-start.5) | collective-permute-done | bytes 606240 | tf_op jit(solution)/shard_map/ppermute | solution.py:44
  278.5 2.7 collective-permute-start.6
  281.2 8.3 %collective-permute-done.6 = f32[2368,64]{0,1:T(8,128)S(1)} collective-permute-done((f32[2368,64]{0,1:T(8,128)S(1)}, f32[2368,64]{0,1:T(8,128)S(1)}, u32[]{:S(2)}, u32[]{:S(2)}) %collective-permute-start.6) | collective-permute-done | bytes 606240 | tf_op jit(solution)/shard_map/ppermute | solution.py:44
  291.2 32.3 %reduce-scatter.2.cloned.1.call-done = bf16[1024,320]{0,1:T(8,128)(2,1)} async-done(((bf16[1024,5120]{0,1:T(8,128)(2,1)}), bf16[1024,320]{0,1:T(8,128)(2,1)}) %reduce-scatter.2.cloned.1.call-update) | async-done | bytes 655376 | tf_op jit(solution)/shard_map/reduce_scatter | solution.py:87
  (43 shorter events, 5.1 us)
Async XLA Ops:
  7.2 152.1 %copy-start = (bf16[64,864]{1,0:T(8,128)(2,1)S(1)}, bf16[64,864]{1,0:T(8,128)(2,1)}, u32[]{:S(2)}) copy-start(bf16[64,864]{1,0:T(8,128)(2,1)} %param.17) | copy-start | bytes 331780
  7.2 137.9 %all-gather.2.cloned.1.call-start = ((), (), s32[]{:S(2)}) async-start(), calls=%async_computation.1 | async-start | bytes 22282240 | tf_op jit(solution)/shard_map/all_gather | solution.py:70
  11.6 7.7 %copy-start.3 = (bf16[5120,64]{0,1:T(8,128)(2,1)S(1)}, bf16[5120,64]{0,1:T(8,128)(2,1)}, u32[]{:S(2)}) copy-start(bf16[5120,64]{0,1:T(8,128)(2,1)} %param.16) | copy-start | bytes 1966084
  11.6 311.9 %reduce-scatter.2.cloned.1.call-start = ((), (), s32[]{:S(2)}) async-start(), calls=%async_computation.2 | async-start | bytes 11141120 | tf_op jit(solution)/shard_map/reduce_scatter | solution.py:87
  20.1 139.2 %copy-start.9 = (f32[864]{0:T(1024)S(1)}, f32[864]{0:T(1024)}, u32[]{:S(2)}) copy-start(f32[864]{0:T(1024)} %param.14) | copy-start | bytes 10372
  159.3 3.9 %copy-start.6 = (f32[1024,928]{0,1:T(8,128)}, f32[1024,928]{0,1:T(8,128)S(1)}, u32[]{:S(2)}) copy-start(f32[1024,928]{0,1:T(8,128)S(1)} %fusion) | copy-start | bytes 11403268
  159.3 3.9 %copy-start.8 = (bf16[64,5120]{1,0:T(8,128)(2,1)S(1)}, bf16[64,5120]{1,0:T(8,128)(2,1)}, u32[]{:S(2)}) copy-start(bf16[64,5120]{1,0:T(8,128)(2,1)} %param.19) | copy-start | bytes 1966084
  163.2 15.9 %copy-start.5 = (bf16[864,64]{0,1:T(8,128)(2,1)S(1)}, bf16[864,64]{0,1:T(8,128)(2,1)}, u32[]{:S(2)}) copy-start(bf16[864,64]{0,1:T(8,128)(2,1)} %param.18) | copy-start | bytes 331780
  179.1 5.5 %copy-start.7 = (f32[1024,928]{0,1:T(8,128)}, f32[1024,928]{0,1:T(8,128)S(1)}, u32[]{:S(2)}) copy-start(f32[1024,928]{0,1:T(8,128)S(1)} %fusion.1) | copy-start | bytes 11403268
  209.9 32.2 %copy-start.1 = (bf16[1024,864]{0,1:T(8,128)(2,1)S(1)}, bf16[1024,864]{0,1:T(8,128)(2,1)}, u32[]{:S(2)}) copy-start(bf16[1024,864]{0,1:T(8,128)(2,1)} %get-tuple-element.11) | copy-start | bytes 5308420
  209.9 2.0 collective-permute-start
  212.0 14.9 %collective-permute-start.1 = (f32[1024,128]{0,1:T(8,128)S(1)}, f32[1024,128]{0,1:T(8,128)S(1)}, u32[]{:S(2)}, u32[]{:S(2)}) collective-permute-start(f32[1024,128]{0,1:T(8,128)S(1)} %fusion.24), channel_id=1, source_target_pairs={{0,2},{1,3},{2,0},{3,1},{4,6},{5,7},{6,4},{7,5},{8,10},{9,11},{10,... | collective-permute-start | bytes 1572872 | tf_op jit(solution)/shard_map/ppermute | solution.py:44
  226.9 31.3 %copy-start.2 = (bf16[1024,320]{0,1:T(8,128)(2,1)S(1)}, bf16[1024,320]{0,1:T(8,128)(2,1)}, u32[]{:S(2)}) copy-start(bf16[1024,320]{0,1:T(8,128)(2,1)} %param.10) | copy-start | bytes 1966084
  226.9 12.4 %collective-permute-start.2 = (f32[1024,128]{0,1:T(8,128)S(1)}, f32[1024,128]{0,1:T(8,128)S(1)}, u32[]{:S(2)}, u32[]{:S(2)}) collective-permute-start(f32[1024,128]{0,1:T(8,128)S(1)} %add.64), channel_id=1, source_target_pairs={{0,4},{1,5},{2,6},{3,7},{4,0},{5,1},{6,2},{7,3},{8,12},{9,13},{10,... | collective-permute-start | bytes 1572872 | tf_op jit(solution)/shard_map/ppermute | solution.py:44
  239.4 19.1 %copy-start.4 = (bf16[1024,320]{0,1:T(8,128)(2,1)S(1)}, bf16[1024,320]{0,1:T(8,128)(2,1)}, u32[]{:S(2)}) copy-start(bf16[1024,320]{0,1:T(8,128)(2,1)} %param.11) | copy-start | bytes 1966084
  239.4 18.7 %collective-permute-start.3 = (f32[1024,128]{0,1:T(8,128)S(1)}, f32[1024,128]{0,1:T(8,128)S(1)}, u32[]{:S(2)}, u32[]{:S(2)}) collective-permute-start(f32[1024,128]{0,1:T(8,128)S(1)} %add.65), channel_id=1, source_target_pairs={{0,8},{1,9},{2,10},{3,11},{4,12},{5,13},{6,14},{7,15},{8,0},{9,1},... | collective-permute-start | bytes 1572872 | tf_op jit(solution)/shard_map/ppermute | solution.py:44
  259.2 9.6 %collective-permute-start.4 = (f32[2368,64]{0,1:T(8,128)S(1)}, f32[2368,64]{0,1:T(8,128)S(1)}, u32[]{:S(2)}, u32[]{:S(2)}) collective-permute-start(f32[2368,64]{0,1:T(8,128)S(1)} %concatenate.19), channel_id=1, source_target_pairs={{0,16},{16,0},{32,48},{48,32},{64,80},{80,64},{96,112},{112,96},{1... | collective-permute-start | bytes 1818632 | tf_op jit(solution)/shard_map/ppermute | solution.py:44
  268.8 9.6 %collective-permute-start.5 = (f32[2368,64]{0,1:T(8,128)S(1)}, f32[2368,64]{0,1:T(8,128)S(1)}, u32[]{:S(2)}, u32[]{:S(2)}) collective-permute-start(f32[2368,64]{0,1:T(8,128)S(1)} %add.67), channel_id=1, source_target_pairs={{0,32},{16,48},{32,0},{48,16},{64,96},{80,112},{96,64},{112,80},{1... | collective-permute-start | bytes 1818632 | tf_op jit(solution)/shard_map/ppermute | solution.py:44
  278.5 11.1 %collective-permute-start.6 = (f32[2368,64]{0,1:T(8,128)S(1)}, f32[2368,64]{0,1:T(8,128)S(1)}, u32[]{:S(2)}, u32[]{:S(2)}) collective-permute-start(f32[2368,64]{0,1:T(8,128)S(1)} %add.68), channel_id=1, source_target_pairs={{0,64},{16,80},{32,96},{48,112},{64,0},{80,16},{96,32},{112,48},{1... | collective-permute-start | bytes 1818632 | tf_op jit(solution)/shard_map/ppermute | solution.py:44
Sparse Core Ops, SparseCore 0:
  11.7 133.3 all-gather.1
  208.1 115.4 reduce-scatter.1

commit v9 on v8

--- a/solution.py
+++ b/solution.py
@@ -82,9 +82,11 @@
     grad_hidden = backward_sum + dot_rows(grad_low, outer_down)
     grad_pre = (grad_hidden * gelu_slope(pre)).astype(jnp.bfloat16)
     pre_low_part = dot_rows(grad_pre, inner_up)
-    grad_pre_cat = jnp.concatenate([grad_pre, pre_low_part.astype(jnp.bfloat16)], axis=1)
-    block_part = dot_rows(grad_pre_cat, inner_cat).astype(jnp.bfloat16)
-    tokens_grad = lax.psum_scatter(block_part, "col", scatter_dimension=1, tiled=True)
+    block_part = dot_rows(grad_pre, inner_weight).astype(jnp.bfloat16).astype(jnp.float32)
+    low_part = dot_rows(pre_low_part.astype(jnp.bfloat16), inner_down)
+    tokens_grad = lax.psum_scatter(
+        (block_part + low_part).astype(jnp.bfloat16), "col", scatter_dimension=1, tiled=True
+    )
 
     hidden_low_part = plain_dot(hidden, outer_down)
     lows = tree_sum(jnp.concatenate([hidden_low_part, pre_low_part], axis=1), "col", n_col)

time: 331 us -> 330 us (level)
  local copies, waits for them, and re-layouts: 11.1 us -> 2.66 us
  waiting for transfers between devices: 227 us -> 235 us
    all_gather x1, waiting for transfers between devices: 125 us -> 133 us  [local(): lax.all_gather(jnp.stack([tokens_in, gated_local]), 'col', axis=2, tiled=...]
    unnamed x21 -> x20, local copies, waits for them, and re-layouts: 7.66 us -> 0.06 us
    dot_general x3 -> x4, matrix products: 28.8 us -> 26.4 us  [dot_rows(): lax.dot_general(left, right, (((1,), (1,)), ((), ())), preferred_element_...]
  transfers between devices with their start and end apart: 9 -> 9, of which waited for: 9 -> 9; matrix products, arithmetic and copies ran while one was open for 5% -> 3% of each run, Pallas kernels for 0% -> 0%
where the time goes in v9:
time: 330 us
  waiting for transfers between devices  235 us (71%)
  matrix products  68.1 us (21%)
  between operations  14.3 us (4%)
  starting transfers between devices  5.78 us (2%)
  other arithmetic  4.07 us (1%)
    all_gather x1, waiting for transfers between devices, local(): lax.all_gather(jnp.stack([tokens_in, gated_local]), 'col', axis=2, tiled=...  133 us
    ppermute x7, waiting for transfers between devices, tree_sum(): value = value + lax.ppermute(value, axis, pairs)  69.3 us
    dot_general x4, matrix products, plain_dot(): return jnp.dot(left, right, preferred_element_type=jnp.float32)  37.7 us
    reduce_scatter x1, waiting for transfers between devices, local(): lax.psum_scatter((block_part + low_part).astype(jnp.bfloat16), 'col', sca...  32.3 us
    dot_general x4, matrix products, dot_rows(): lax.dot_general(left, right, (((1,), (1,)), ((), ())), preferred_element_...  26.4 us
  transfers between devices with their start and end apart: 9, of which 9 were waited for; matrix products, arithmetic and copies ran while one was open for 3% of the time, Pallas kernels for 0%

profile of v9, /device:TPU:1, one launch (start us, length us, event | category | flops | bytes accessed | tf_op | source)
XLA Modules:
  0.0 329.9 jit_solution(954291616641102913)
XLA Ops:
  7.2 0.8 dynamic_slice.3
  8.1 1.3 fusion.17
  9.4 2.3 pad_maximum_fusion
  11.7 133.4 %all-gather.2.cloned.1.call-done = bf16[2,1024,5120]{1,2,0:T(8,128)(2,1)} async-done(((bf16[2,1024,320]{1,2,0:T(8,128)(2,1)}), bf16[2,1024,5120]{1,2,0:T(8,128)(2,1)}) %all-gather.2.cloned.1.call-update) | async-done | bytes 20971536 | tf_op jit(solution)/shard_map/all_gather | solution.py:70
  145.2 15.8 %fusion = f32[1024,928]{0,1:T(8,128)S(1)} fusion(bf16[2,1024,5120]{1,2,0:T(8,128)(2,1)} %all-gather.2.cloned.1.call-done, bf16[5120,64]{0,1:T(8,128)(2,1)S(1)} %copy-done.3, bf16[5120,864]{0,1:T(8,128)(2,1)} %param.13), kind=kOutput, calls=%fused_computation.2 | convolution fusion | flops 9749790720 | bytes 23789568 | tf_op jit(solution)/shard_map/dot_general | solution.py:25
  161.0 4.0 %multiply_convert_fusion = (bf16[1024,864]{0,1:T(8,128)(2,1)}, f32[1024,864]{0,1:T(8,128)}) fusion(f32[864]{0:T(1024)S(1)} %copy-done.9, bf16[64,864]{1,0:T(8,128)(2,1)S(1)} %copy-done, f32[1024,928]{0,1:T(8,128)S(1)} %fusion), kind=kOutput, calls=%fused_computation.23 | convolution fusion | flops 123043840 | bytes 9223552 | tf_op jit(solution)/shard_map/dot_general | solution.py:25
  165.0 15.9 %fusion.1 = f32[1024,928]{0,1:T(8,128)S(1)} fusion(bf16[2,1024,5120]{1,2,0:T(8,128)(2,1)} %all-gather.2.cloned.1.call-done, bf16[5120,64]{0,1:T(8,128)(2,1)S(1)} %bitcast.29, bf16[5120,864]{0,1:T(8,128)(2,1)} %param.15), kind=kOutput, calls=%fused_computation.4 | convolution fusion | flops 9749790720 | bytes 23789568 | tf_op jit(solution)/shard_map/dot_general | solution.py:25
  180.9 5.5 %fusion.14 = bf16[1024,864]{0,1:T(8,128)(2,1)S(1)} fusion(f32[1024,864]{0,1:T(8,128)} %get-tuple-element.10, f32[1024,928]{0,1:T(8,128)S(1)} %fusion.1, bf16[864,64]{0,1:T(8,128)(2,1)S(1)} %copy-done.5), kind=kOutput, calls=%fused_computation.19 | convolution fusion | flops 131006464 | bytes 9220096 | tf_op jit(solution)/shard_map/dot_general | solution.py:29
  186.9 13.7 %fusion.27 = bf16[1024,5120]{0,1:T(8,128)(2,1)S(1)} fusion(bf16[1024,864]{0,1:T(8,128)(2,1)S(1)} %fusion.14, bf16[5120,864]{0,1:T(8,128)(2,1)} %param.13), kind=kOutput, calls=%fused_computation.45 | convolution fusion | flops 9059696640 | bytes 21102592 | tf_op jit(solution)/shard_map/dot_general | solution.py:29
  200.6 6.8 %add_convert_fusion = bf16[1024,5120]{0,1:T(8,128)(2,1)} fusion(bf16[5120,64]{0,1:T(8,128)(2,1)} %param.16, bf16[1024,5120]{0,1:T(8,128)(2,1)S(1)} %fusion.27, f32[1024,64]{0,1:T(8,128)S(1)} %fusion.28), kind=kOutput, calls=%fused_computation | convolution fusion | flops 686882816 | bytes 21889024 | tf_op jit(solution)/shard_map/dot_general | solution.py:29
  207.4 2.0 fusion.29
  209.8 1.7 collective-permute-done
  211.7 14.7 %collective-permute-done.1 = f32[1024,128]{0,1:T(8,128)S(1)} collective-permute-done((f32[1024,128]{0,1:T(8,128)S(1)}, f32[1024,128]{0,1:T(8,128)S(1)}, u32[]{:S(2)}, u32[]{:S(2)}) %collective-permute-start.1) | collective-permute-done | bytes 524320 | tf_op jit(solution)/shard_map/ppermute | solution.py:44
  226.6 12.3 %collective-permute-done.2 = f32[1024,128]{0,1:T(8,128)S(1)} collective-permute-done((f32[1024,128]{0,1:T(8,128)S(1)}, f32[1024,128]{0,1:T(8,128)S(1)}, u32[]{:S(2)}, u32[]{:S(2)}) %collective-permute-start.2) | collective-permute-done | bytes 524320 | tf_op jit(solution)/shard_map/ppermute | solution.py:44
  239.0 1.1 collective-permute-start.3
  240.2 1.6 fusion.21
  241.8 1.6 fusion.22
  243.4 14.5 %collective-permute-done.3 = f32[1024,128]{0,1:T(8,128)S(1)} collective-permute-done((f32[1024,128]{0,1:T(8,128)S(1)}, f32[1024,128]{0,1:T(8,128)S(1)}, u32[]{:S(2)}, u32[]{:S(2)}) %collective-permute-start.3) | collective-permute-done | bytes 524320 | tf_op jit(solution)/shard_map/ppermute | solution.py:44
  259.0 9.5 %collective-permute-done.4 = f32[2368,64]{0,1:T(8,128)S(1)} collective-permute-done((f32[2368,64]{0,1:T(8,128)S(1)}, f32[2368,64]{0,1:T(8,128)S(1)}, u32[]{:S(2)}, u32[]{:S(2)}) %collective-permute-start.4) | collective-permute-done | bytes 606240 | tf_op jit(solution)/shard_map/ppermute | solution.py:44
  268.5 1.3 collective-permute-start.5
  269.8 8.3 %collective-permute-done.5 = f32[2368,64]{0,1:T(8,128)S(1)} collective-permute-done((f32[2368,64]{0,1:T(8,128)S(1)}, f32[2368,64]{0,1:T(8,128)S(1)}, u32[]{:S(2)}, u32[]{:S(2)}) %collective-permute-start.5) | collective-permute-done | bytes 606240 | tf_op jit(solution)/shard_map/ppermute | solution.py:44
  278.2 2.6 collective-permute-start.6
  280.7 8.5 %collective-permute-done.6 = f32[2368,64]{0,1:T(8,128)S(1)} collective-permute-done((f32[2368,64]{0,1:T(8,128)S(1)}, f32[2368,64]{0,1:T(8,128)S(1)}, u32[]{:S(2)}, u32[]{:S(2)}) %collective-permute-start.6) | collective-permute-done | bytes 606240 | tf_op jit(solution)/shard_map/ppermute | solution.py:44
  290.9 32.3 %reduce-scatter.2.cloned.1.call-done = bf16[1024,320]{0,1:T(8,128)(2,1)} async-done(((bf16[1024,5120]{0,1:T(8,128)(2,1)}), bf16[1024,320]{0,1:T(8,128)(2,1)}) %reduce-scatter.2.cloned.1.call-update) | async-done | bytes 655376 | tf_op jit(solution)/shard_map/reduce_scatter | solution.py:87
  (42 shorter events, 4.3 us)
Async XLA Ops:
  7.2 153.8 %copy-start = (bf16[64,864]{1,0:T(8,128)(2,1)S(1)}, bf16[64,864]{1,0:T(8,128)(2,1)}, u32[]{:S(2)}) copy-start(bf16[64,864]{1,0:T(8,128)(2,1)} %param.17) | copy-start | bytes 331780
  7.2 138.0 %copy-start.3 = (bf16[5120,64]{0,1:T(8,128)(2,1)S(1)}, bf16[5120,64]{0,1:T(8,128)(2,1)}, u32[]{:S(2)}) copy-start(bf16[5120,64]{0,1:T(8,128)(2,1)} %param.16) | copy-start | bytes 1966084
  7.2 138.0 %all-gather.2.cloned.1.call-start = ((), (), s32[]{:S(2)}) async-start(), calls=%async_computation.1 | async-start | bytes 22282240 | tf_op jit(solution)/shard_map/all_gather | solution.py:70
  11.7 149.3 %copy-start.9 = (f32[864]{0:T(1024)S(1)}, f32[864]{0:T(1024)}, u32[]{:S(2)}) copy-start(f32[864]{0:T(1024)} %param.14) | copy-start | bytes 10372
  11.7 311.4 %reduce-scatter.2.cloned.1.call-start = ((), (), s32[]{:S(2)}) async-start(), calls=%async_computation.2 | async-start | bytes 11141120 | tf_op jit(solution)/shard_map/reduce_scatter | solution.py:87
  161.0 4.0 %copy-start.6 = (f32[1024,928]{0,1:T(8,128)}, f32[1024,928]{0,1:T(8,128)S(1)}, u32[]{:S(2)}) copy-start(f32[1024,928]{0,1:T(8,128)S(1)} %fusion) | copy-start | bytes 11403268
  161.0 4.0 %copy-start.8 = (bf16[64,5120]{1,0:T(8,128)(2,1)S(1)}, bf16[64,5120]{1,0:T(8,128)(2,1)}, u32[]{:S(2)}) copy-start(bf16[64,5120]{1,0:T(8,128)(2,1)} %param.19) | copy-start | bytes 1966084
  165.0 15.9 %copy-start.5 = (bf16[864,64]{0,1:T(8,128)(2,1)S(1)}, bf16[864,64]{0,1:T(8,128)(2,1)}, u32[]{:S(2)}) copy-start(bf16[864,64]{0,1:T(8,128)(2,1)} %param.18) | copy-start | bytes 331780
  180.9 5.5 %copy-start.7 = (f32[1024,928]{0,1:T(8,128)}, f32[1024,928]{0,1:T(8,128)S(1)}, u32[]{:S(2)}) copy-start(f32[1024,928]{0,1:T(8,128)S(1)} %fusion.1) | copy-start | bytes 11403268
  207.4 32.8 %copy-start.1 = (bf16[1024,864]{0,1:T(8,128)(2,1)S(1)}, bf16[1024,864]{0,1:T(8,128)(2,1)}, u32[]{:S(2)}) copy-start(bf16[1024,864]{0,1:T(8,128)(2,1)} %get-tuple-element.9) | copy-start | bytes 5308420
  209.5 2.0 collective-permute-start
  211.6 14.9 %collective-permute-start.1 = (f32[1024,128]{0,1:T(8,128)S(1)}, f32[1024,128]{0,1:T(8,128)S(1)}, u32[]{:S(2)}, u32[]{:S(2)}) collective-permute-start(f32[1024,128]{0,1:T(8,128)S(1)} %fusion.25), channel_id=1, source_target_pairs={{0,2},{1,3},{2,0},{3,1},{4,6},{5,7},{6,4},{7,5},{8,10},{9,11},{10,... | collective-permute-start | bytes 1572872 | tf_op jit(solution)/shard_map/ppermute | solution.py:44
  226.5 31.4 %copy-start.2 = (bf16[1024,320]{0,1:T(8,128)(2,1)S(1)}, bf16[1024,320]{0,1:T(8,128)(2,1)}, u32[]{:S(2)}) copy-start(bf16[1024,320]{0,1:T(8,128)(2,1)} %param.10) | copy-start | bytes 1966084
  226.5 12.4 %collective-permute-start.2 = (f32[1024,128]{0,1:T(8,128)S(1)}, f32[1024,128]{0,1:T(8,128)S(1)}, u32[]{:S(2)}, u32[]{:S(2)}) collective-permute-start(f32[1024,128]{0,1:T(8,128)S(1)} %add.68), channel_id=1, source_target_pairs={{0,4},{1,5},{2,6},{3,7},{4,0},{5,1},{6,2},{7,3},{8,12},{9,13},{10,... | collective-permute-start | bytes 1572872 | tf_op jit(solution)/shard_map/ppermute | solution.py:44
  239.0 19.2 %copy-start.4 = (bf16[1024,320]{0,1:T(8,128)(2,1)S(1)}, bf16[1024,320]{0,1:T(8,128)(2,1)}, u32[]{:S(2)}) copy-start(bf16[1024,320]{0,1:T(8,128)(2,1)} %param.11) | copy-start | bytes 1966084
  239.0 18.8 %collective-permute-start.3 = (f32[1024,128]{0,1:T(8,128)S(1)}, f32[1024,128]{0,1:T(8,128)S(1)}, u32[]{:S(2)}, u32[]{:S(2)}) collective-permute-start(f32[1024,128]{0,1:T(8,128)S(1)} %add.69), channel_id=1, source_target_pairs={{0,8},{1,9},{2,10},{3,11},{4,12},{5,13},{6,14},{7,15},{8,0},{9,1},... | collective-permute-start | bytes 1572872 | tf_op jit(solution)/shard_map/ppermute | solution.py:44
  258.9 9.6 %collective-permute-start.4 = (f32[2368,64]{0,1:T(8,128)S(1)}, f32[2368,64]{0,1:T(8,128)S(1)}, u32[]{:S(2)}, u32[]{:S(2)}) collective-permute-start(f32[2368,64]{0,1:T(8,128)S(1)} %concatenate.15), channel_id=1, source_target_pairs={{0,16},{16,0},{32,48},{48,32},{64,80},{80,64},{96,112},{112,96},{1... | collective-permute-start | bytes 1818632 | tf_op jit(solution)/shard_map/ppermute | solution.py:44
  268.5 9.6 %collective-permute-start.5 = (f32[2368,64]{0,1:T(8,128)S(1)}, f32[2368,64]{0,1:T(8,128)S(1)}, u32[]{:S(2)}, u32[]{:S(2)}) collective-permute-start(f32[2368,64]{0,1:T(8,128)S(1)} %add.71), channel_id=1, source_target_pairs={{0,32},{16,48},{32,0},{48,16},{64,96},{80,112},{96,64},{112,80},{1... | collective-permute-start | bytes 1818632 | tf_op jit(solution)/shard_map/ppermute | solution.py:44
  278.2 11.1 %collective-permute-start.6 = (f32[2368,64]{0,1:T(8,128)S(1)}, f32[2368,64]{0,1:T(8,128)S(1)}, u32[]{:S(2)}, u32[]{:S(2)}) collective-permute-start(f32[2368,64]{0,1:T(8,128)S(1)} %add.72), channel_id=1, source_target_pairs={{0,64},{16,80},{32,96},{48,112},{64,0},{80,16},{96,32},{112,48},{1... | collective-permute-start | bytes 1818632 | tf_op jit(solution)/shard_map/ppermute | solution.py:44
Sparse Core Ops, SparseCore 0:
  11.8 133.3 all-gather.1
  207.5 115.5 reduce-scatter.1

commit v10 on v8

--- a/solution.py
+++ b/solution.py
@@ -3,6 +3,8 @@
 import jax
 import jax.numpy as jnp
 from jax import lax
+from jax.experimental import pallas as pl
+from jax.experimental.pallas import tpu as pltpu
 from jax.sharding import PartitionSpec as P
 
 SLOPE_SCALE = 0.7978845608028654
@@ -46,6 +48,37 @@
     return value
 
 
+def block_kernel(weight_ref, grad_ref, down_ref, low_ref, out_ref):
+    contract_rows = (((0,), (0,)), ((), ()))
+    block = lax.dot_general(
+        weight_ref[...], grad_ref[...], contract_rows, preferred_element_type=jnp.float32
+    )
+    low = lax.dot_general(down_ref[...], low_ref[...], contract_rows, preferred_element_type=jnp.float32)
+    out_ref[...] = (block.astype(jnp.bfloat16).astype(jnp.float32) + low).astype(out_ref.dtype)
+
+
+def block_product(weight_t, grad_t, down_t, low_t, tile=640):
+    ff, features = weight_t.shape
+    rank, tokens = low_t.shape
+    return pl.pallas_call(
+        block_kernel,
+        out_shape=jax.ShapeDtypeStruct((features, tokens), jnp.bfloat16),
+        grid=(features // tile,),
+        in_specs=[
+            pl.BlockSpec((ff, tile), lambda i: (0, i)),
+            pl.BlockSpec((ff, tokens), lambda i: (0, 0)),
+            pl.BlockSpec((rank, tile), lambda i: (0, i)),
+            pl.BlockSpec((rank, tokens), lambda i: (0, 0)),
+        ],
+        out_specs=pl.BlockSpec((tile, tokens), lambda i: (i, 0)),
+        cost_estimate=pl.CostEstimate(
+            flops=2 * features * tokens * (ff + rank),
+            transcendentals=0,
+            bytes_accessed=2 * (ff * features + ff * tokens + features * tokens),
+        ),
+    )(weight_t, grad_t, down_t, low_t)
+
+
 def local(
     tokens_in,
     token_grad,
@@ -82,9 +115,8 @@
     grad_hidden = backward_sum + dot_rows(grad_low, outer_down)
     grad_pre = (grad_hidden * gelu_slope(pre)).astype(jnp.bfloat16)
     pre_low_part = dot_rows(grad_pre, inner_up)
-    grad_pre_cat = jnp.concatenate([grad_pre, pre_low_part.astype(jnp.bfloat16)], axis=1)
-    block_part = dot_rows(grad_pre_cat, inner_cat).astype(jnp.bfloat16)
-    tokens_grad = lax.psum_scatter(block_part, "col", scatter_dimension=1, tiled=True)
+    block_t = block_product(inner_weight.T, grad_pre.T, inner_down.T, pre_low_part.astype(jnp.bfloat16).T)
+    tokens_grad = lax.psum_scatter(block_t.T, "col", scatter_dimension=1, tiled=True)
 
     hidden_low_part = plain_dot(hidden, outer_down)
     lows = tree_sum(jnp.concatenate([hidden_low_part, pre_low_part], axis=1), "col", n_col)

time: 331 us -> 329 us (level)
  matrix products: 68.6 us -> 46 us
  Pallas kernels: 0 us -> 18.3 us
  waiting for transfers between devices: 227 us -> 235 us
  local copies, waits for them, and re-layouts: 11.1 us -> 4.14 us
    dot_general x3 -> x2, matrix products: 28.8 us -> 5.94 us  [dot_rows(): lax.dot_general(left, right, (((1,), (1,)), ((), ())), preferred_element_...]
    pallas_call x0 -> x1, Pallas kernels: none -> 18.3 us  [block_product(): pl.pallas_call(block_kernel, out_shape=jax.ShapeDtypeStruct((features, to...]
    all_gather x1, waiting for transfers between devices: 125 us -> 133 us  [local(): lax.all_gather(jnp.stack([tokens_in, gated_local]), 'col', axis=2, tiled=...]
    unnamed x21 -> x24, local copies, waits for them, and re-layouts: 7.66 us -> 1.54 us
  transfers between devices with their start and end apart: 9 -> 9, of which waited for: 9 -> 9; matrix products, arithmetic and copies ran while one was open for 5% -> 2% of each run, Pallas kernels for 0% -> 0%
where the time goes in v10:
time: 329 us; the launch traced here: 328 us
  waiting for transfers between devices  235 us (71%)
  matrix products  46 us (14%)
  Pallas kernels  18.3 us (6%)
  between operations  14.3 us (4%)
  starting transfers between devices  5.92 us (2%)
  other arithmetic  4.84 us (1%)
  local copies, waits for them, and re-layouts  4.14 us (1%)
    all_gather x1, waiting for transfers between devices, local(): lax.all_gather(jnp.stack([tokens_in, gated_local]), 'col', axis=2, tiled=...  133 us
    ppermute x7, waiting for transfers between devices, tree_sum(): value = value + lax.ppermute(value, axis, pairs)  69.1 us
    dot_general x4, matrix products, plain_dot(): return jnp.dot(left, right, preferred_element_type=jnp.float32)  36.1 us
    reduce_scatter x1, waiting for transfers between devices, local(): lax.psum_scatter(block_t.T, 'col', scatter_dimension=1, tiled=True)  32.3 us
    pallas_call x1, Pallas kernels, block_product(): pl.pallas_call(block_kernel, out_shape=jax.ShapeDtypeStruct((features, to...  18.3 us
  transfers between devices with their start and end apart: 9, of which 9 were waited for; matrix products, arithmetic and copies ran while one was open for 2% of the time, Pallas kernels for 0%

profile of v10, /device:TPU:1, one launch (start us, length us, event | category | flops | bytes accessed | tf_op | source)
XLA Modules:
  0.0 328.4 jit_solution(12178318644050593293)
XLA Ops:
  7.2 0.8 dynamic_slice.3
  8.1 1.3 fusion.17
  9.4 2.3 pad_maximum_fusion
  11.8 133.4 %all-gather.2.cloned.1.call-done = bf16[2,1024,5120]{1,2,0:T(8,128)(2,1)} async-done(((bf16[2,1024,320]{1,2,0:T(8,128)(2,1)}), bf16[2,1024,5120]{1,2,0:T(8,128)(2,1)}) %all-gather.2.cloned.1.call-update) | async-done | bytes 20971536 | tf_op jit(solution)/shard_map/all_gather | solution.py:103
  145.2 15.8 %fusion = f32[1024,928]{0,1:T(8,128)S(1)} fusion(bf16[2,1024,5120]{1,2,0:T(8,128)(2,1)} %all-gather.2.cloned.1.call-done, bf16[5120,64]{0,1:T(8,128)(2,1)S(1)} %copy-done.10, bf16[5120,864]{0,1:T(8,128)(2,1)} %param.13), kind=kOutput, calls=%fused_computation.1 | convolution fusion | flops 9749790720 | bytes 23789568 | tf_op jit(solution)/shard_map/dot_general | solution.py:27
  161.1 4.0 %multiply_convert_fusion = (bf16[1024,864]{0,1:T(8,128)(2,1)}, f32[1024,864]{0,1:T(8,128)}) fusion(f32[864]{0:T(1024)S(1)} %copy-done.11, bf16[64,864]{1,0:T(8,128)(2,1)S(1)} %copy-done, f32[1024,928]{0,1:T(8,128)S(1)} %fusion), kind=kOutput, calls=%fused_computation.22 | convolution fusion | flops 123043840 | bytes 9223552 | tf_op jit(solution)/shard_map/dot_general | solution.py:27
  165.0 15.9 %fusion.1 = f32[1024,928]{0,1:T(8,128)S(1)} fusion(bf16[2,1024,5120]{1,2,0:T(8,128)(2,1)} %all-gather.2.cloned.1.call-done, bf16[5120,64]{0,1:T(8,128)(2,1)S(1)} %bitcast.35, bf16[5120,864]{0,1:T(8,128)(2,1)} %param.15), kind=kOutput, calls=%fused_computation.3 | convolution fusion | flops 9749790720 | bytes 23789568 | tf_op jit(solution)/shard_map/dot_general | solution.py:27
  180.9 5.5 %fusion.14 = bf16[1024,864]{0,1:T(8,128)(2,1)S(1)} fusion(f32[1024,864]{0,1:T(8,128)} %get-tuple-element.10, f32[1024,928]{0,1:T(8,128)S(1)} %fusion.1, bf16[864,64]{0,1:T(8,128)(2,1)S(1)} %copy-done.6), kind=kOutput, calls=%fused_computation.18 | convolution fusion | flops 131006464 | bytes 9220096 | tf_op jit(solution)/shard_map/dot_general | solution.py:31
  187.7 18.3 %shard_map.137 = bf16[5120,1024]{1,0:T(8,128)(2,1)} custom-call(bf16[864,5120]{1,0:T(8,128)(2,1)} %bitcast.34, bf16[864,1024]{1,0:T(8,128)(2,1)} %bitcast.32, bf16[64,5120]{1,0:T(8,128)(2,1)} %bitcast.36, bf16[64,1024]{1,0:T(8,128)(2,1)} %convert_bitcast_fusion.low_ref), custom_call_target="tpu_custom_call" | custom-call | flops 9730785280 | bytes 21102592 | tf_op jit(solution)/shard_map/pallas_call | solution.py:63
  206.0 1.4 copy-done.3
  208.3 1.7 collective-permute-done
  210.2 14.7 %collective-permute-done.1 = f32[1024,128]{0,1:T(8,128)S(1)} collective-permute-done((f32[1024,128]{0,1:T(8,128)S(1)}, f32[1024,128]{0,1:T(8,128)S(1)}, u32[]{:S(2)}, u32[]{:S(2)}) %collective-permute-start.1) | collective-permute-done | bytes 524320 | tf_op jit(solution)/shard_map/ppermute | solution.py:46
  225.1 12.3 %collective-permute-done.2 = f32[1024,128]{0,1:T(8,128)S(1)} collective-permute-done((f32[1024,128]{0,1:T(8,128)S(1)}, f32[1024,128]{0,1:T(8,128)S(1)}, u32[]{:S(2)}, u32[]{:S(2)}) %collective-permute-start.2) | collective-permute-done | bytes 524320 | tf_op jit(solution)/shard_map/ppermute | solution.py:46
  237.5 1.1 collective-permute-start.3
  238.6 1.6 fusion.20
  240.3 1.6 fusion.21
  241.9 14.3 %collective-permute-done.3 = f32[1024,128]{0,1:T(8,128)S(1)} collective-permute-done((f32[1024,128]{0,1:T(8,128)S(1)}, f32[1024,128]{0,1:T(8,128)S(1)}, u32[]{:S(2)}, u32[]{:S(2)}) %collective-permute-start.3) | collective-permute-done | bytes 524320 | tf_op jit(solution)/shard_map/ppermute | solution.py:46
  257.3 9.5 %collective-permute-done.4 = f32[2368,64]{0,1:T(8,128)S(1)} collective-permute-done((f32[2368,64]{0,1:T(8,128)S(1)}, f32[2368,64]{0,1:T(8,128)S(1)}, u32[]{:S(2)}, u32[]{:S(2)}) %collective-permute-start.4) | collective-permute-done | bytes 606240 | tf_op jit(solution)/shard_map/ppermute | solution.py:46
  266.9 1.2 collective-permute-start.5
  268.1 8.3 %collective-permute-done.5 = f32[2368,64]{0,1:T(8,128)S(1)} collective-permute-done((f32[2368,64]{0,1:T(8,128)S(1)}, f32[2368,64]{0,1:T(8,128)S(1)}, u32[]{:S(2)}, u32[]{:S(2)}) %collective-permute-start.5) | collective-permute-done | bytes 606240 | tf_op jit(solution)/shard_map/ppermute | solution.py:46
  276.5 2.8 collective-permute-start.6
  279.3 8.3 %collective-permute-done.6 = f32[2368,64]{0,1:T(8,128)S(1)} collective-permute-done((f32[2368,64]{0,1:T(8,128)S(1)}, f32[2368,64]{0,1:T(8,128)S(1)}, u32[]{:S(2)}, u32[]{:S(2)}) %collective-permute-start.6) | collective-permute-done | bytes 606240 | tf_op jit(solution)/shard_map/ppermute | solution.py:46
  288.4 0.8 fusion.25
  289.2 32.3 %reduce-scatter.2.cloned.1.call-done = bf16[1024,320]{0,1:T(8,128)(2,1)} async-done(((bf16[1024,5120]{0,1:T(8,128)(2,1)}), bf16[1024,320]{0,1:T(8,128)(2,1)}) %reduce-scatter.2.cloned.1.call-update) | async-done | bytes 655376 | tf_op jit(solution)/shard_map/reduce_scatter | solution.py:119
  (46 shorter events, 4.8 us)
Async XLA Ops:
  7.2 153.9 %copy-start = (bf16[64,864]{1,0:T(8,128)(2,1)S(1)}, bf16[64,864]{1,0:T(8,128)(2,1)}, u32[]{:S(2)}) copy-start(bf16[64,864]{1,0:T(8,128)(2,1)} %param.17) | copy-start | bytes 331780
  7.2 138.0 %copy-start.10 = (bf16[5120,64]{0,1:T(8,128)(2,1)S(1)}, bf16[5120,64]{0,1:T(8,128)(2,1)}, u32[]{:S(2)}) copy-start(bf16[5120,64]{0,1:T(8,128)(2,1)} %param.16) | copy-start | bytes 1966084
  7.2 138.0 %all-gather.2.cloned.1.call-start = ((), (), s32[]{:S(2)}) async-start(), calls=%async_computation.1 | async-start | bytes 22282240 | tf_op jit(solution)/shard_map/all_gather | solution.py:103
  11.7 149.3 %copy-start.11 = (f32[864]{0:T(1024)S(1)}, f32[864]{0:T(1024)}, u32[]{:S(2)}) copy-start(f32[864]{0:T(1024)} %param.14) | copy-start | bytes 10372
  11.7 309.8 %reduce-scatter.2.cloned.1.call-start = ((), (), s32[]{:S(2)}) async-start(), calls=%async_computation.2 | async-start | bytes 11141120 | tf_op jit(solution)/shard_map/reduce_scatter | solution.py:119
  161.0 4.0 %copy-start.7 = (f32[1024,928]{0,1:T(8,128)}, f32[1024,928]{0,1:T(8,128)S(1)}, u32[]{:S(2)}) copy-start(f32[1024,928]{0,1:T(8,128)S(1)} %fusion) | copy-start | bytes 11403268
  161.0 4.0 %copy-start.9 = (bf16[64,5120]{1,0:T(8,128)(2,1)S(1)}, bf16[64,5120]{1,0:T(8,128)(2,1)}, u32[]{:S(2)}) copy-start(bf16[64,5120]{1,0:T(8,128)(2,1)} %param.19) | copy-start | bytes 1966084
  165.0 15.9 %copy-start.6 = (bf16[864,64]{0,1:T(8,128)(2,1)S(1)}, bf16[864,64]{0,1:T(8,128)(2,1)}, u32[]{:S(2)}) copy-start(bf16[864,64]{0,1:T(8,128)(2,1)} %param.18) | copy-start | bytes 331780
  180.9 5.5 %copy-start.8 = (f32[1024,928]{0,1:T(8,128)}, f32[1024,928]{0,1:T(8,128)S(1)}, u32[]{:S(2)}) copy-start(f32[1024,928]{0,1:T(8,128)S(1)} %fusion.1) | copy-start | bytes 11403268
  186.4 1.3 copy-start.1
  206.0 1.5 copy-start.3
  208.0 32.3 %copy-start.2 = (bf16[1024,864]{0,1:T(8,128)(2,1)S(1)}, bf16[1024,864]{0,1:T(8,128)(2,1)}, u32[]{:S(2)}) copy-start(bf16[1024,864]{0,1:T(8,128)(2,1)} %copy-done.1) | copy-start | bytes 5308420
  208.0 2.0 collective-permute-start
  210.0 14.9 %collective-permute-start.1 = (f32[1024,128]{0,1:T(8,128)S(1)}, f32[1024,128]{0,1:T(8,128)S(1)}, u32[]{:S(2)}, u32[]{:S(2)}) collective-permute-start(f32[1024,128]{0,1:T(8,128)S(1)} %fusion.24), channel_id=1, source_target_pairs={{0,2},{1,3},{2,0},{3,1},{4,6},{5,7},{6,4},{7,5},{8,10},{9,11},{10,... | collective-permute-start | bytes 1572872 | tf_op jit(solution)/shard_map/ppermute | solution.py:46
  225.0 31.3 %copy-start.4 = (bf16[1024,320]{0,1:T(8,128)(2,1)S(1)}, bf16[1024,320]{0,1:T(8,128)(2,1)}, u32[]{:S(2)}) copy-start(bf16[1024,320]{0,1:T(8,128)(2,1)} %param.10) | copy-start | bytes 1966084
  225.0 12.4 %collective-permute-start.2 = (f32[1024,128]{0,1:T(8,128)S(1)}, f32[1024,128]{0,1:T(8,128)S(1)}, u32[]{:S(2)}, u32[]{:S(2)}) collective-permute-start(f32[1024,128]{0,1:T(8,128)S(1)} %add.64), channel_id=1, source_target_pairs={{0,4},{1,5},{2,6},{3,7},{4,0},{5,1},{6,2},{7,3},{8,12},{9,13},{10,... | collective-permute-start | bytes 1572872 | tf_op jit(solution)/shard_map/ppermute | solution.py:46
  237.5 19.1 %copy-start.5 = (bf16[1024,320]{0,1:T(8,128)(2,1)S(1)}, bf16[1024,320]{0,1:T(8,128)(2,1)}, u32[]{:S(2)}) copy-start(bf16[1024,320]{0,1:T(8,128)(2,1)} %param.11) | copy-start | bytes 1966084
  237.5 18.7 %collective-permute-start.3 = (f32[1024,128]{0,1:T(8,128)S(1)}, f32[1024,128]{0,1:T(8,128)S(1)}, u32[]{:S(2)}, u32[]{:S(2)}) collective-permute-start(f32[1024,128]{0,1:T(8,128)S(1)} %add.65), channel_id=1, source_target_pairs={{0,8},{1,9},{2,10},{3,11},{4,12},{5,13},{6,14},{7,15},{8,0},{9,1},... | collective-permute-start | bytes 1572872 | tf_op jit(solution)/shard_map/ppermute | solution.py:46
  257.3 9.6 %collective-permute-start.4 = (f32[2368,64]{0,1:T(8,128)S(1)}, f32[2368,64]{0,1:T(8,128)S(1)}, u32[]{:S(2)}, u32[]{:S(2)}) collective-permute-start(f32[2368,64]{0,1:T(8,128)S(1)} %concatenate.15), channel_id=1, source_target_pairs={{0,16},{16,0},{32,48},{48,32},{64,80},{80,64},{96,112},{112,96},{1... | collective-permute-start | bytes 1818632 | tf_op jit(solution)/shard_map/ppermute | solution.py:46
  266.9 9.6 %collective-permute-start.5 = (f32[2368,64]{0,1:T(8,128)S(1)}, f32[2368,64]{0,1:T(8,128)S(1)}, u32[]{:S(2)}, u32[]{:S(2)}) collective-permute-start(f32[2368,64]{0,1:T(8,128)S(1)} %add.67), channel_id=1, source_target_pairs={{0,32},{16,48},{32,0},{48,16},{64,96},{80,112},{96,64},{112,80},{1... | collective-permute-start | bytes 1818632 | tf_op jit(solution)/shard_map/ppermute | solution.py:46
  276.5 11.1 %collective-permute-start.6 = (f32[2368,64]{0,1:T(8,128)S(1)}, f32[2368,64]{0,1:T(8,128)S(1)}, u32[]{:S(2)}, u32[]{:S(2)}) collective-permute-start(f32[2368,64]{0,1:T(8,128)S(1)} %add.68), channel_id=1, source_target_pairs={{0,64},{16,80},{32,96},{48,112},{64,0},{80,16},{96,32},{112,48},{1... | collective-permute-start | bytes 1818632 | tf_op jit(solution)/shard_map/ppermute | solution.py:46
Sparse Core Ops, SparseCore 0:
  11.8 133.3 all-gather.1
  206.1 115.3 reduce-scatter.1

commit v11 on v10

--- a/solution.py
+++ b/solution.py
@@ -49,25 +49,22 @@
 
 
 def block_kernel(weight_ref, grad_ref, down_ref, low_ref, out_ref):
-    contract_rows = (((0,), (0,)), ((), ()))
-    block = lax.dot_general(
-        weight_ref[...], grad_ref[...], contract_rows, preferred_element_type=jnp.float32
-    )
-    low = lax.dot_general(down_ref[...], low_ref[...], contract_rows, preferred_element_type=jnp.float32)
+    block = jnp.dot(weight_ref[...], grad_ref[...], preferred_element_type=jnp.float32)
+    low = jnp.dot(down_ref[...], low_ref[...], preferred_element_type=jnp.float32)
     out_ref[...] = (block.astype(jnp.bfloat16).astype(jnp.float32) + low).astype(out_ref.dtype)
 
 
-def block_product(weight_t, grad_t, down_t, low_t, tile=640):
-    ff, features = weight_t.shape
+def block_product(weight, grad_t, down, low_t, tile=640):
+    features, ff = weight.shape
     rank, tokens = low_t.shape
     return pl.pallas_call(
         block_kernel,
         out_shape=jax.ShapeDtypeStruct((features, tokens), jnp.bfloat16),
         grid=(features // tile,),
         in_specs=[
-            pl.BlockSpec((ff, tile), lambda i: (0, i)),
+            pl.BlockSpec((tile, ff), lambda i: (i, 0)),
             pl.BlockSpec((ff, tokens), lambda i: (0, 0)),
-            pl.BlockSpec((rank, tile), lambda i: (0, i)),
+            pl.BlockSpec((tile, rank), lambda i: (i, 0)),
             pl.BlockSpec((rank, tokens), lambda i: (0, 0)),
         ],
         out_specs=pl.BlockSpec((tile, tokens), lambda i: (i, 0)),
@@ -76,7 +73,7 @@
             transcendentals=0,
             bytes_accessed=2 * (ff * features + ff * tokens + features * tokens),
         ),
-    )(weight_t, grad_t, down_t, low_t)
+    )(weight, grad_t, down, low_t)
 
 
 def local(
@@ -115,7 +112,7 @@
     grad_hidden = backward_sum + dot_rows(grad_low, outer_down)
     grad_pre = (grad_hidden * gelu_slope(pre)).astype(jnp.bfloat16)
     pre_low_part = dot_rows(grad_pre, inner_up)
-    block_t = block_product(inner_weight.T, grad_pre.T, inner_down.T, pre_low_part.astype(jnp.bfloat16).T)
+    block_t = block_product(inner_weight, grad_pre.T, inner_down, pre_low_part.astype(jnp.bfloat16).T)
     tokens_grad = lax.psum_scatter(block_t.T, "col", scatter_dimension=1, tiled=True)
 
     hidden_low_part = plain_dot(hidden, outer_down)

time: 329 us -> 329 us (level)
  waiting for transfers between devices: 235 us -> 220 us
  local copies, waits for them, and re-layouts: 4.14 us -> 18.4 us
    all_gather x1, waiting for transfers between devices: 133 us -> 119 us  [local(): lax.all_gather(jnp.stack([tokens_in, gated_local]), 'col', axis=2, tiled=...]
    unnamed x24 -> x26, local copies, waits for them, and re-layouts: 1.54 us -> 15.8 us
  transfers between devices with their start and end apart: 9 -> 9, of which waited for: 9 -> 9; matrix products, arithmetic and copies ran while one was open for 2% -> 6% of each run, Pallas kernels for 0% -> 0%
where the time goes in v11:
time: 329 us; the launch traced here: 328 us
  waiting for transfers between devices  220 us (67%)
  matrix products  45.9 us (14%)
  local copies, waits for them, and re-layouts  18.4 us (6%)
  Pallas kernels  18.1 us (6%)
  between operations  14.3 us (4%)
  starting transfers between devices  6.26 us (2%)
  other arithmetic  4.8 us (1%)
    all_gather x1, waiting for transfers between devices, local(): lax.all_gather(jnp.stack([tokens_in, gated_local]), 'col', axis=2, tiled=...  119 us
    ppermute x7, waiting for transfers between devices, tree_sum(): value = value + lax.ppermute(value, axis, pairs)  68.7 us
    dot_general x4, matrix products, plain_dot(): return jnp.dot(left, right, preferred_element_type=jnp.float32)  36 us
    reduce_scatter x1, waiting for transfers between devices, local(): lax.psum_scatter(block_t.T, 'col', scatter_dimension=1, tiled=True)  32.4 us
    pallas_call x1, Pallas kernels, block_product(): pl.pallas_call(block_kernel, out_shape=jax.ShapeDtypeStruct((features, to...  18.1 us
    unnamed x26, local copies, waits for them, and re-layouts  15.8 us
  transfers between devices with their start and end apart: 9, of which 9 were waited for; matrix products, arithmetic and copies ran while one was open for 6% of the time, Pallas kernels for 0%

profile of v11, /device:TPU:1, one launch (start us, length us, event | category | flops | bytes accessed | tf_op | source)
XLA Modules:
  0.0 328.1 jit_solution(5310127494868855574)
XLA Ops:
  8.1 1.3 fusion.17
  9.4 2.3 pad_maximum_fusion
  11.7 1.4 copy.16.down_ref
  13.1 12.9 %copy.15.weight_ref = bf16[5120,864]{1,0:T(8,128)(2,1)} copy(bf16[5120,864]{0,1:T(8,128)(2,1)} %param.13) | data formatting | bytes 17694720 | tf_op args[3]
  26.0 119.1 %all-gather.2.cloned.1.call-done = bf16[2,1024,5120]{1,2,0:T(8,128)(2,1)} async-done(((bf16[2,1024,320]{1,2,0:T(8,128)(2,1)}), bf16[2,1024,5120]{1,2,0:T(8,128)(2,1)}) %all-gather.2.cloned.1.call-update) | async-done | bytes 20971536 | tf_op jit(solution)/shard_map/all_gather | solution.py:100
  145.1 15.8 %fusion = f32[1024,928]{0,1:T(8,128)S(1)} fusion(bf16[2,1024,5120]{1,2,0:T(8,128)(2,1)} %all-gather.2.cloned.1.call-done, bf16[5120,64]{0,1:T(8,128)(2,1)S(1)} %copy-done.6, bf16[5120,864]{0,1:T(8,128)(2,1)} %param.13), kind=kOutput, calls=%fused_computation.1 | convolution fusion | flops 9749790720 | bytes 23789568 | tf_op jit(solution)/shard_map/dot_general | solution.py:27
  161.0 3.9 %multiply_convert_fusion = (bf16[1024,864]{0,1:T(8,128)(2,1)}, f32[1024,864]{0,1:T(8,128)}) fusion(f32[864]{0:T(1024)S(1)} %copy-done.11, bf16[64,864]{1,0:T(8,128)(2,1)S(1)} %copy-done, f32[1024,928]{0,1:T(8,128)S(1)} %fusion), kind=kOutput, calls=%fused_computation.22 | convolution fusion | flops 123043840 | bytes 9223552 | tf_op jit(solution)/shard_map/dot_general | solution.py:27
  164.9 15.9 %fusion.1 = f32[1024,928]{0,1:T(8,128)S(1)} fusion(bf16[2,1024,5120]{1,2,0:T(8,128)(2,1)} %all-gather.2.cloned.1.call-done, bf16[5120,64]{0,1:T(8,128)(2,1)S(1)} %bitcast.32, bf16[5120,864]{0,1:T(8,128)(2,1)} %param.15), kind=kOutput, calls=%fused_computation.3 | convolution fusion | flops 9749790720 | bytes 23789568 | tf_op jit(solution)/shard_map/dot_general | solution.py:27
  180.8 5.5 %fusion.14 = bf16[1024,864]{0,1:T(8,128)(2,1)S(1)} fusion(f32[1024,864]{0,1:T(8,128)} %get-tuple-element.10, f32[1024,928]{0,1:T(8,128)S(1)} %fusion.1, bf16[864,64]{0,1:T(8,128)(2,1)S(1)} %copy-done.7), kind=kOutput, calls=%fused_computation.18 | convolution fusion | flops 131006464 | bytes 9220096 | tf_op jit(solution)/shard_map/dot_general | solution.py:31
  187.6 18.1 %shard_map.137 = bf16[5120,1024]{1,0:T(8,128)(2,1)} custom-call(bf16[5120,864]{1,0:T(8,128)(2,1)} %copy.15.weight_ref, bf16[864,1024]{1,0:T(8,128)(2,1)} %bitcast.30, bf16[5120,64]{1,0:T(8,128)(2,1)} %copy.16.down_ref, bf16[64,1024]{1,0:T(8,128)(2,1)} %convert_bitcast_fusion.low_ref), custom_call_target="tpu_custom_call" | custom-call | flops 9730785280 | bytes 21102592 | tf_op jit(solution)/shard_map/pallas_call | solution.py:60
  205.7 1.4 copy-done.3
  208.0 1.6 collective-permute-done
  209.9 14.7 %collective-permute-done.1 = f32[1024,128]{0,1:T(8,128)S(1)} collective-permute-done((f32[1024,128]{0,1:T(8,128)S(1)}, f32[1024,128]{0,1:T(8,128)S(1)}, u32[]{:S(2)}, u32[]{:S(2)}) %collective-permute-start.1) | collective-permute-done | bytes 524320 | tf_op jit(solution)/shard_map/ppermute | solution.py:46
  224.7 12.3 %collective-permute-done.2 = f32[1024,128]{0,1:T(8,128)S(1)} collective-permute-done((f32[1024,128]{0,1:T(8,128)S(1)}, f32[1024,128]{0,1:T(8,128)S(1)}, u32[]{:S(2)}, u32[]{:S(2)}) %collective-permute-start.2) | collective-permute-done | bytes 524320 | tf_op jit(solution)/shard_map/ppermute | solution.py:46
  237.1 1.1 collective-permute-start.3
  238.2 1.6 fusion.20
  239.9 1.6 fusion.21
  241.5 14.2 %collective-permute-done.3 = f32[1024,128]{0,1:T(8,128)S(1)} collective-permute-done((f32[1024,128]{0,1:T(8,128)S(1)}, f32[1024,128]{0,1:T(8,128)S(1)}, u32[]{:S(2)}, u32[]{:S(2)}) %collective-permute-start.3) | collective-permute-done | bytes 524320 | tf_op jit(solution)/shard_map/ppermute | solution.py:46
  256.9 9.5 %collective-permute-done.4 = f32[2368,64]{0,1:T(8,128)S(1)} collective-permute-done((f32[2368,64]{0,1:T(8,128)S(1)}, f32[2368,64]{0,1:T(8,128)S(1)}, u32[]{:S(2)}, u32[]{:S(2)}) %collective-permute-start.4) | collective-permute-done | bytes 606240 | tf_op jit(solution)/shard_map/ppermute | solution.py:46
  266.4 1.4 collective-permute-start.5
  267.8 8.2 %collective-permute-done.5 = f32[2368,64]{0,1:T(8,128)S(1)} collective-permute-done((f32[2368,64]{0,1:T(8,128)S(1)}, f32[2368,64]{0,1:T(8,128)S(1)}, u32[]{:S(2)}, u32[]{:S(2)}) %collective-permute-start.5) | collective-permute-done | bytes 606240 | tf_op jit(solution)/shard_map/ppermute | solution.py:46
  276.0 2.9 collective-permute-start.6
  279.0 8.2 %collective-permute-done.6 = f32[2368,64]{0,1:T(8,128)S(1)} collective-permute-done((f32[2368,64]{0,1:T(8,128)S(1)}, f32[2368,64]{0,1:T(8,128)S(1)}, u32[]{:S(2)}, u32[]{:S(2)}) %collective-permute-start.6) | collective-permute-done | bytes 606240 | tf_op jit(solution)/shard_map/ppermute | solution.py:46
  288.8 32.4 %reduce-scatter.2.cloned.1.call-done = bf16[1024,320]{0,1:T(8,128)(2,1)} async-done(((bf16[1024,5120]{0,1:T(8,128)(2,1)}), bf16[1024,320]{0,1:T(8,128)(2,1)}) %reduce-scatter.2.cloned.1.call-update) | async-done | bytes 655376 | tf_op jit(solution)/shard_map/reduce_scatter | solution.py:116
  (48 shorter events, 6.4 us)
Async XLA Ops:
  7.2 153.8 %copy-start = (bf16[64,864]{1,0:T(8,128)(2,1)S(1)}, bf16[64,864]{1,0:T(8,128)(2,1)}, u32[]{:S(2)}) copy-start(bf16[64,864]{1,0:T(8,128)(2,1)} %param.17) | copy-start | bytes 331780
  7.2 4.5 %copy-start.6 = (bf16[5120,64]{0,1:T(8,128)(2,1)S(1)}, bf16[5120,64]{0,1:T(8,128)(2,1)}, u32[]{:S(2)}) copy-start(bf16[5120,64]{0,1:T(8,128)(2,1)} %param.16) | copy-start | bytes 1966084
  7.2 137.9 %all-gather.2.cloned.1.call-start = ((), (), s32[]{:S(2)}) async-start(), calls=%async_computation.1 | async-start | bytes 22282240 | tf_op jit(solution)/shard_map/all_gather | solution.py:100
  11.7 309.6 %reduce-scatter.2.cloned.1.call-start = ((), (), s32[]{:S(2)}) async-start(), calls=%async_computation.2 | async-start | bytes 11141120 | tf_op jit(solution)/shard_map/reduce_scatter | solution.py:116
  26.0 135.0 %copy-start.11 = (f32[864]{0:T(1024)S(1)}, f32[864]{0:T(1024)}, u32[]{:S(2)}) copy-start(f32[864]{0:T(1024)} %param.14) | copy-start | bytes 10372
  161.0 3.9 %copy-start.8 = (f32[1024,928]{0,1:T(8,128)}, f32[1024,928]{0,1:T(8,128)S(1)}, u32[]{:S(2)}) copy-start(f32[1024,928]{0,1:T(8,128)S(1)} %fusion) | copy-start | bytes 11403268
  161.0 3.9 %copy-start.10 = (bf16[64,5120]{1,0:T(8,128)(2,1)S(1)}, bf16[64,5120]{1,0:T(8,128)(2,1)}, u32[]{:S(2)}) copy-start(bf16[64,5120]{1,0:T(8,128)(2,1)} %param.19) | copy-start | bytes 1966084
  164.9 15.9 %copy-start.7 = (bf16[864,64]{0,1:T(8,128)(2,1)S(1)}, bf16[864,64]{0,1:T(8,128)(2,1)}, u32[]{:S(2)}) copy-start(bf16[864,64]{0,1:T(8,128)(2,1)} %param.18) | copy-start | bytes 331780
  180.8 5.5 %copy-start.9 = (f32[1024,928]{0,1:T(8,128)}, f32[1024,928]{0,1:T(8,128)S(1)}, u32[]{:S(2)}) copy-start(f32[1024,928]{0,1:T(8,128)S(1)} %fusion.1) | copy-start | bytes 11403268
  186.3 1.2 copy-start.1
  205.7 1.5 copy-start.3
  207.6 32.2 %copy-start.2 = (bf16[1024,864]{0,1:T(8,128)(2,1)S(1)}, bf16[1024,864]{0,1:T(8,128)(2,1)}, u32[]{:S(2)}) copy-start(bf16[1024,864]{0,1:T(8,128)(2,1)} %copy-done.1) | copy-start | bytes 5308420
  207.6 2.0 collective-permute-start
  209.7 14.8 %collective-permute-start.1 = (f32[1024,128]{0,1:T(8,128)S(1)}, f32[1024,128]{0,1:T(8,128)S(1)}, u32[]{:S(2)}, u32[]{:S(2)}) collective-permute-start(f32[1024,128]{0,1:T(8,128)S(1)} %fusion.24), channel_id=1, source_target_pairs={{0,2},{1,3},{2,0},{3,1},{4,6},{5,7},{6,4},{7,5},{8,10},{9,11},{10,... | collective-permute-start | bytes 1572872 | tf_op jit(solution)/shard_map/ppermute | solution.py:46
  224.6 31.2 %copy-start.4 = (bf16[1024,320]{0,1:T(8,128)(2,1)S(1)}, bf16[1024,320]{0,1:T(8,128)(2,1)}, u32[]{:S(2)}) copy-start(bf16[1024,320]{0,1:T(8,128)(2,1)} %param.10) | copy-start | bytes 1966084
  224.6 12.4 %collective-permute-start.2 = (f32[1024,128]{0,1:T(8,128)S(1)}, f32[1024,128]{0,1:T(8,128)S(1)}, u32[]{:S(2)}, u32[]{:S(2)}) collective-permute-start(f32[1024,128]{0,1:T(8,128)S(1)} %add.64), channel_id=1, source_target_pairs={{0,4},{1,5},{2,6},{3,7},{4,0},{5,1},{6,2},{7,3},{8,12},{9,13},{10,... | collective-permute-start | bytes 1572872 | tf_op jit(solution)/shard_map/ppermute | solution.py:46
  237.1 19.0 %copy-start.5 = (bf16[1024,320]{0,1:T(8,128)(2,1)S(1)}, bf16[1024,320]{0,1:T(8,128)(2,1)}, u32[]{:S(2)}) copy-start(bf16[1024,320]{0,1:T(8,128)(2,1)} %param.11) | copy-start | bytes 1966084
  237.1 18.6 %collective-permute-start.3 = (f32[1024,128]{0,1:T(8,128)S(1)}, f32[1024,128]{0,1:T(8,128)S(1)}, u32[]{:S(2)}, u32[]{:S(2)}) collective-permute-start(f32[1024,128]{0,1:T(8,128)S(1)} %add.65), channel_id=1, source_target_pairs={{0,8},{1,9},{2,10},{3,11},{4,12},{5,13},{6,14},{7,15},{8,0},{9,1},... | collective-permute-start | bytes 1572872 | tf_op jit(solution)/shard_map/ppermute | solution.py:46
  256.8 9.6 %collective-permute-start.4 = (f32[2368,64]{0,1:T(8,128)S(1)}, f32[2368,64]{0,1:T(8,128)S(1)}, u32[]{:S(2)}, u32[]{:S(2)}) collective-permute-start(f32[2368,64]{0,1:T(8,128)S(1)} %concatenate.15), channel_id=1, source_target_pairs={{0,16},{16,0},{32,48},{48,32},{64,80},{80,64},{96,112},{112,96},{1... | collective-permute-start | bytes 1818632 | tf_op jit(solution)/shard_map/ppermute | solution.py:46
  266.4 9.6 %collective-permute-start.5 = (f32[2368,64]{0,1:T(8,128)S(1)}, f32[2368,64]{0,1:T(8,128)S(1)}, u32[]{:S(2)}, u32[]{:S(2)}) collective-permute-start(f32[2368,64]{0,1:T(8,128)S(1)} %add.67), channel_id=1, source_target_pairs={{0,32},{16,48},{32,0},{48,16},{64,96},{80,112},{96,64},{112,80},{1... | collective-permute-start | bytes 1818632 | tf_op jit(solution)/shard_map/ppermute | solution.py:46
  276.0 11.1 %collective-permute-start.6 = (f32[2368,64]{0,1:T(8,128)S(1)}, f32[2368,64]{0,1:T(8,128)S(1)}, u32[]{:S(2)}, u32[]{:S(2)}) collective-permute-start(f32[2368,64]{0,1:T(8,128)S(1)} %add.68), channel_id=1, source_target_pairs={{0,64},{16,80},{32,96},{48,112},{64,0},{80,16},{96,32},{112,48},{1... | collective-permute-start | bytes 1818632 | tf_op jit(solution)/shard_map/ppermute | solution.py:46
Sparse Core Ops, SparseCore 0:
  11.8 133.3 all-gather.1
  205.8 115.3 reduce-scatter.1

commit v12 on v11

--- a/solution.py
+++ b/solution.py
@@ -54,7 +54,7 @@
     out_ref[...] = (block.astype(jnp.bfloat16).astype(jnp.float32) + low).astype(out_ref.dtype)
 
 
-def block_product(weight, grad_t, down, low_t, tile=640):
+def block_product(weight, grad_t, down, low_t, tile=1280):
     features, ff = weight.shape
     rank, tokens = low_t.shape
     return pl.pallas_call(

time: 329 us -> 329 us (level)
  no operation moved by 1% of the time
where the time goes in v12:
time: 329 us; the launch traced here: 328 us
  waiting for transfers between devices  221 us (67%)
  matrix products  45.9 us (14%)
  local copies, waits for them, and re-layouts  18.4 us (6%)
  Pallas kernels  18.2 us (6%)
  between operations  14.3 us (4%)
  starting transfers between devices  6.06 us (2%)
  other arithmetic  4.8 us (1%)
    all_gather x1, waiting for transfers between devices, local(): lax.all_gather(jnp.stack([tokens_in, gated_local]), 'col', axis=2, tiled=...  119 us
    ppermute x7, waiting for transfers between devices, tree_sum(): value = value + lax.ppermute(value, axis, pairs)  68.9 us
    dot_general x4, matrix products, plain_dot(): return jnp.dot(left, right, preferred_element_type=jnp.float32)  36 us
    reduce_scatter x1, waiting for transfers between devices, local(): lax.psum_scatter(block_t.T, 'col', scatter_dimension=1, tiled=True)  32.5 us
    pallas_call x1, Pallas kernels, block_product(): pl.pallas_call(block_kernel, out_shape=jax.ShapeDtypeStruct((features, to...  18.2 us
    unnamed x26, local copies, waits for them, and re-layouts  15.8 us
  transfers between devices with their start and end apart: 9, of which 9 were waited for; matrix products, arithmetic and copies ran while one was open for 6% of the time, Pallas kernels for 0%

profile of v12, /device:TPU:1, one launch (start us, length us, event | category | flops | bytes accessed | tf_op | source)
XLA Modules:
  0.0 328.3 jit_solution(13412998990689822525)
XLA Ops:
  8.1 1.3 fusion.17
  9.4 2.3 pad_maximum_fusion
  11.7 1.4 copy.16.down_ref
  13.1 12.9 %copy.15.weight_ref = bf16[5120,864]{1,0:T(8,128)(2,1)} copy(bf16[5120,864]{0,1:T(8,128)(2,1)} %param.13) | data formatting | bytes 17694720 | tf_op args[3]
  26.0 119.1 %all-gather.2.cloned.1.call-done = bf16[2,1024,5120]{1,2,0:T(8,128)(2,1)} async-done(((bf16[2,1024,320]{1,2,0:T(8,128)(2,1)}), bf16[2,1024,5120]{1,2,0:T(8,128)(2,1)}) %all-gather.2.cloned.1.call-update) | async-done | bytes 20971536 | tf_op jit(solution)/shard_map/all_gather | solution.py:100
  145.1 15.8 %fusion = f32[1024,928]{0,1:T(8,128)S(1)} fusion(bf16[2,1024,5120]{1,2,0:T(8,128)(2,1)} %all-gather.2.cloned.1.call-done, bf16[5120,64]{0,1:T(8,128)(2,1)S(1)} %copy-done.6, bf16[5120,864]{0,1:T(8,128)(2,1)} %param.13), kind=kOutput, calls=%fused_computation.1 | convolution fusion | flops 9749790720 | bytes 23789568 | tf_op jit(solution)/shard_map/dot_general | solution.py:27
  161.0 3.9 %multiply_convert_fusion = (bf16[1024,864]{0,1:T(8,128)(2,1)}, f32[1024,864]{0,1:T(8,128)}) fusion(f32[864]{0:T(1024)S(1)} %copy-done.11, bf16[64,864]{1,0:T(8,128)(2,1)S(1)} %copy-done, f32[1024,928]{0,1:T(8,128)S(1)} %fusion), kind=kOutput, calls=%fused_computation.22 | convolution fusion | flops 123043840 | bytes 9223552 | tf_op jit(solution)/shard_map/dot_general | solution.py:27
  164.9 15.9 %fusion.1 = f32[1024,928]{0,1:T(8,128)S(1)} fusion(bf16[2,1024,5120]{1,2,0:T(8,128)(2,1)} %all-gather.2.cloned.1.call-done, bf16[5120,64]{0,1:T(8,128)(2,1)S(1)} %bitcast.32, bf16[5120,864]{0,1:T(8,128)(2,1)} %param.15), kind=kOutput, calls=%fused_computation.3 | convolution fusion | flops 9749790720 | bytes 23789568 | tf_op jit(solution)/shard_map/dot_general | solution.py:27
  180.8 5.5 %fusion.14 = bf16[1024,864]{0,1:T(8,128)(2,1)S(1)} fusion(f32[1024,864]{0,1:T(8,128)} %get-tuple-element.10, f32[1024,928]{0,1:T(8,128)S(1)} %fusion.1, bf16[864,64]{0,1:T(8,128)(2,1)S(1)} %copy-done.7), kind=kOutput, calls=%fused_computation.18 | convolution fusion | flops 131006464 | bytes 9220096 | tf_op jit(solution)/shard_map/dot_general | solution.py:31
  187.6 18.2 %shard_map.137 = bf16[5120,1024]{1,0:T(8,128)(2,1)} custom-call(bf16[5120,864]{1,0:T(8,128)(2,1)} %copy.15.weight_ref, bf16[864,1024]{1,0:T(8,128)(2,1)} %bitcast.30, bf16[5120,64]{1,0:T(8,128)(2,1)} %copy.16.down_ref, bf16[64,1024]{1,0:T(8,128)(2,1)} %convert_bitcast_fusion.low_ref), custom_call_target="tpu_custom_call" | custom-call | flops 9730785280 | bytes 21102592 | tf_op jit(solution)/shard_map/pallas_call | solution.py:60
  205.8 1.4 copy-done.3
  208.1 1.6 collective-permute-done
  210.0 14.7 %collective-permute-done.1 = f32[1024,128]{0,1:T(8,128)S(1)} collective-permute-done((f32[1024,128]{0,1:T(8,128)S(1)}, f32[1024,128]{0,1:T(8,128)S(1)}, u32[]{:S(2)}, u32[]{:S(2)}) %collective-permute-start.1) | collective-permute-done | bytes 524320 | tf_op jit(solution)/shard_map/ppermute | solution.py:46
  224.9 12.3 %collective-permute-done.2 = f32[1024,128]{0,1:T(8,128)S(1)} collective-permute-done((f32[1024,128]{0,1:T(8,128)S(1)}, f32[1024,128]{0,1:T(8,128)S(1)}, u32[]{:S(2)}, u32[]{:S(2)}) %collective-permute-start.2) | collective-permute-done | bytes 524320 | tf_op jit(solution)/shard_map/ppermute | solution.py:46
  237.3 1.1 collective-permute-start.3
  238.4 1.6 fusion.20
  240.0 1.6 fusion.21
  241.6 14.3 %collective-permute-done.3 = f32[1024,128]{0,1:T(8,128)S(1)} collective-permute-done((f32[1024,128]{0,1:T(8,128)S(1)}, f32[1024,128]{0,1:T(8,128)S(1)}, u32[]{:S(2)}, u32[]{:S(2)}) %collective-permute-start.3) | collective-permute-done | bytes 524320 | tf_op jit(solution)/shard_map/ppermute | solution.py:46
  257.1 9.5 %collective-permute-done.4 = f32[2368,64]{0,1:T(8,128)S(1)} collective-permute-done((f32[2368,64]{0,1:T(8,128)S(1)}, f32[2368,64]{0,1:T(8,128)S(1)}, u32[]{:S(2)}, u32[]{:S(2)}) %collective-permute-start.4) | collective-permute-done | bytes 606240 | tf_op jit(solution)/shard_map/ppermute | solution.py:46
  266.6 1.3 collective-permute-start.5
  268.0 8.2 %collective-permute-done.5 = f32[2368,64]{0,1:T(8,128)S(1)} collective-permute-done((f32[2368,64]{0,1:T(8,128)S(1)}, f32[2368,64]{0,1:T(8,128)S(1)}, u32[]{:S(2)}, u32[]{:S(2)}) %collective-permute-start.5) | collective-permute-done | bytes 606240 | tf_op jit(solution)/shard_map/ppermute | solution.py:46
  276.3 2.9 collective-permute-start.6
  279.1 8.2 %collective-permute-done.6 = f32[2368,64]{0,1:T(8,128)S(1)} collective-permute-done((f32[2368,64]{0,1:T(8,128)S(1)}, f32[2368,64]{0,1:T(8,128)S(1)}, u32[]{:S(2)}, u32[]{:S(2)}) %collective-permute-start.6) | collective-permute-done | bytes 606240 | tf_op jit(solution)/shard_map/ppermute | solution.py:46
  289.0 32.5 %reduce-scatter.2.cloned.1.call-done = bf16[1024,320]{0,1:T(8,128)(2,1)} async-done(((bf16[1024,5120]{0,1:T(8,128)(2,1)}), bf16[1024,320]{0,1:T(8,128)(2,1)}) %reduce-scatter.2.cloned.1.call-update) | async-done | bytes 655376 | tf_op jit(solution)/shard_map/reduce_scatter | solution.py:116
  (48 shorter events, 6.4 us)
Async XLA Ops:
  7.2 153.8 %copy-start = (bf16[64,864]{1,0:T(8,128)(2,1)S(1)}, bf16[64,864]{1,0:T(8,128)(2,1)}, u32[]{:S(2)}) copy-start(bf16[64,864]{1,0:T(8,128)(2,1)} %param.17) | copy-start | bytes 331780
  7.2 4.5 %copy-start.6 = (bf16[5120,64]{0,1:T(8,128)(2,1)S(1)}, bf16[5120,64]{0,1:T(8,128)(2,1)}, u32[]{:S(2)}) copy-start(bf16[5120,64]{0,1:T(8,128)(2,1)} %param.16) | copy-start | bytes 1966084
  7.2 137.9 %all-gather.2.cloned.1.call-start = ((), (), s32[]{:S(2)}) async-start(), calls=%async_computation.1 | async-start | bytes 22282240 | tf_op jit(solution)/shard_map/all_gather | solution.py:100
  11.7 309.8 %reduce-scatter.2.cloned.1.call-start = ((), (), s32[]{:S(2)}) async-start(), calls=%async_computation.2 | async-start | bytes 11141120 | tf_op jit(solution)/shard_map/reduce_scatter | solution.py:116
  26.0 135.0 %copy-start.11 = (f32[864]{0:T(1024)S(1)}, f32[864]{0:T(1024)}, u32[]{:S(2)}) copy-start(f32[864]{0:T(1024)} %param.14) | copy-start | bytes 10372
  161.0 3.9 %copy-start.8 = (f32[1024,928]{0,1:T(8,128)}, f32[1024,928]{0,1:T(8,128)S(1)}, u32[]{:S(2)}) copy-start(f32[1024,928]{0,1:T(8,128)S(1)} %fusion) | copy-start | bytes 11403268
  161.0 3.9 %copy-start.10 = (bf16[64,5120]{1,0:T(8,128)(2,1)S(1)}, bf16[64,5120]{1,0:T(8,128)(2,1)}, u32[]{:S(2)}) copy-start(bf16[64,5120]{1,0:T(8,128)(2,1)} %param.19) | copy-start | bytes 1966084
  164.9 15.9 %copy-start.7 = (bf16[864,64]{0,1:T(8,128)(2,1)S(1)}, bf16[864,64]{0,1:T(8,128)(2,1)}, u32[]{:S(2)}) copy-start(bf16[864,64]{0,1:T(8,128)(2,1)} %param.18) | copy-start | bytes 331780
  180.8 5.5 %copy-start.9 = (f32[1024,928]{0,1:T(8,128)}, f32[1024,928]{0,1:T(8,128)S(1)}, u32[]{:S(2)}) copy-start(f32[1024,928]{0,1:T(8,128)S(1)} %fusion.1) | copy-start | bytes 11403268
  186.3 1.2 copy-start.1
  205.8 1.5 copy-start.3
  207.8 32.2 %copy-start.2 = (bf16[1024,864]{0,1:T(8,128)(2,1)S(1)}, bf16[1024,864]{0,1:T(8,128)(2,1)}, u32[]{:S(2)}) copy-start(bf16[1024,864]{0,1:T(8,128)(2,1)} %copy-done.1) | copy-start | bytes 5308420
  207.8 2.0 collective-permute-start
  209.8 14.8 %collective-permute-start.1 = (f32[1024,128]{0,1:T(8,128)S(1)}, f32[1024,128]{0,1:T(8,128)S(1)}, u32[]{:S(2)}, u32[]{:S(2)}) collective-permute-start(f32[1024,128]{0,1:T(8,128)S(1)} %fusion.24), channel_id=1, source_target_pairs={{0,2},{1,3},{2,0},{3,1},{4,6},{5,7},{6,4},{7,5},{8,10},{9,11},{10,... | collective-permute-start | bytes 1572872 | tf_op jit(solution)/shard_map/ppermute | solution.py:46
  224.8 31.2 %copy-start.4 = (bf16[1024,320]{0,1:T(8,128)(2,1)S(1)}, bf16[1024,320]{0,1:T(8,128)(2,1)}, u32[]{:S(2)}) copy-start(bf16[1024,320]{0,1:T(8,128)(2,1)} %param.10) | copy-start | bytes 1966084
  224.8 12.4 %collective-permute-start.2 = (f32[1024,128]{0,1:T(8,128)S(1)}, f32[1024,128]{0,1:T(8,128)S(1)}, u32[]{:S(2)}, u32[]{:S(2)}) collective-permute-start(f32[1024,128]{0,1:T(8,128)S(1)} %add.64), channel_id=1, source_target_pairs={{0,4},{1,5},{2,6},{3,7},{4,0},{5,1},{6,2},{7,3},{8,12},{9,13},{10,... | collective-permute-start | bytes 1572872 | tf_op jit(solution)/shard_map/ppermute | solution.py:46
  237.3 19.1 %copy-start.5 = (bf16[1024,320]{0,1:T(8,128)(2,1)S(1)}, bf16[1024,320]{0,1:T(8,128)(2,1)}, u32[]{:S(2)}) copy-start(bf16[1024,320]{0,1:T(8,128)(2,1)} %param.11) | copy-start | bytes 1966084
  237.3 18.7 %collective-permute-start.3 = (f32[1024,128]{0,1:T(8,128)S(1)}, f32[1024,128]{0,1:T(8,128)S(1)}, u32[]{:S(2)}, u32[]{:S(2)}) collective-permute-start(f32[1024,128]{0,1:T(8,128)S(1)} %add.65), channel_id=1, source_target_pairs={{0,8},{1,9},{2,10},{3,11},{4,12},{5,13},{6,14},{7,15},{8,0},{9,1},... | collective-permute-start | bytes 1572872 | tf_op jit(solution)/shard_map/ppermute | solution.py:46
  257.0 9.6 %collective-permute-start.4 = (f32[2368,64]{0,1:T(8,128)S(1)}, f32[2368,64]{0,1:T(8,128)S(1)}, u32[]{:S(2)}, u32[]{:S(2)}) collective-permute-start(f32[2368,64]{0,1:T(8,128)S(1)} %concatenate.15), channel_id=1, source_target_pairs={{0,16},{16,0},{32,48},{48,32},{64,80},{80,64},{96,112},{112,96},{1... | collective-permute-start | bytes 1818632 | tf_op jit(solution)/shard_map/ppermute | solution.py:46
  266.6 9.6 %collective-permute-start.5 = (f32[2368,64]{0,1:T(8,128)S(1)}, f32[2368,64]{0,1:T(8,128)S(1)}, u32[]{:S(2)}, u32[]{:S(2)}) collective-permute-start(f32[2368,64]{0,1:T(8,128)S(1)} %add.67), channel_id=1, source_target_pairs={{0,32},{16,48},{32,0},{48,16},{64,96},{80,112},{96,64},{112,80},{1... | collective-permute-start | bytes 1818632 | tf_op jit(solution)/shard_map/ppermute | solution.py:46
  276.3 11.1 %collective-permute-start.6 = (f32[2368,64]{0,1:T(8,128)S(1)}, f32[2368,64]{0,1:T(8,128)S(1)}, u32[]{:S(2)}, u32[]{:S(2)}) collective-permute-start(f32[2368,64]{0,1:T(8,128)S(1)} %add.68), channel_id=1, source_target_pairs={{0,64},{16,80},{32,96},{48,112},{64,0},{80,16},{96,32},{112,48},{1... | collective-permute-start | bytes 1818632 | tf_op jit(solution)/shard_map/ppermute | solution.py:46
Sparse Core Ops, SparseCore 0:
  11.8 133.3 all-gather.1
  206.0 115.4 reduce-scatter.1

commit v13 on v12

--- a/solution.py
+++ b/solution.py
@@ -48,32 +48,29 @@
     return value
 
 
-def block_kernel(weight_ref, grad_ref, down_ref, low_ref, out_ref):
+def block_kernel(weight_ref, grad_ref, out_ref):
     block = jnp.dot(weight_ref[...], grad_ref[...], preferred_element_type=jnp.float32)
-    low = jnp.dot(down_ref[...], low_ref[...], preferred_element_type=jnp.float32)
-    out_ref[...] = (block.astype(jnp.bfloat16).astype(jnp.float32) + low).astype(out_ref.dtype)
+    out_ref[...] = block.astype(out_ref.dtype)
 
 
-def block_product(weight, grad_t, down, low_t, tile=1280):
-    features, ff = weight.shape
-    rank, tokens = low_t.shape
+def block_product(weight, grad_t, tile=640):
+    features, depth = weight.shape
+    tokens = grad_t.shape[1]
     return pl.pallas_call(
         block_kernel,
         out_shape=jax.ShapeDtypeStruct((features, tokens), jnp.bfloat16),
         grid=(features // tile,),
         in_specs=[
-            pl.BlockSpec((tile, ff), lambda i: (i, 0)),
-            pl.BlockSpec((ff, tokens), lambda i: (0, 0)),
-            pl.BlockSpec((tile, rank), lambda i: (i, 0)),
-            pl.BlockSpec((rank, tokens), lambda i: (0, 0)),
+            pl.BlockSpec((tile, depth), lambda i: (i, 0)),
+            pl.BlockSpec((depth, tokens), lambda i: (0, 0)),
         ],
         out_specs=pl.BlockSpec((tile, tokens), lambda i: (i, 0)),
         cost_estimate=pl.CostEstimate(
-            flops=2 * features * tokens * (ff + rank),
+            flops=2 * features * tokens * depth,
             transcendentals=0,
-            bytes_accessed=2 * (ff * features + ff * tokens + features * tokens),
+            bytes_accessed=2 * (depth * features + depth * tokens + features * tokens),
         ),
-    )(weight, grad_t, down, low_t)
+    )(weight, grad_t)
 
 
 def local(
@@ -112,7 +109,9 @@
     grad_hidden = backward_sum + dot_rows(grad_low, outer_down)
     grad_pre = (grad_hidden * gelu_slope(pre)).astype(jnp.bfloat16)
     pre_low_part = dot_rows(grad_pre, inner_up)
-    block_t = block_product(inner_weight, grad_pre.T, inner_down, pre_low_part.astype(jnp.bfloat16).T)
+    block_t = block_product(
+        inner_cat, jnp.concatenate([grad_pre.T, pre_low_part.astype(jnp.bfloat16).T], axis=0)
+    )
     tokens_grad = lax.psum_scatter(block_t.T, "col", scatter_dimension=1, tiled=True)
 
     hidden_low_part = plain_dot(hidden, outer_down)

time: 329 us -> 339 us (1.030)
  matrix products: 45.9 us -> 58.4 us
  other arithmetic: 4.8 us -> 16.2 us
  waiting for transfers between devices: 221 us -> 211 us
    dot_general x4, matrix products: 36 us -> 48.5 us  [plain_dot(): return jnp.dot(left, right, preferred_element_type=jnp.float32)]
    concatenate x0 -> x2, other arithmetic: none -> 12.1 us  [the longest x1 10.7 us: local(): inner_cat = jnp.concatenate([inner_weight, inner_down], axis=1)]
    all_gather x1, waiting for transfers between devices: 119 us -> 109 us  [local(): lax.all_gather(jnp.stack([tokens_in, gated_local]), 'col', axis=2, tiled=...]
    unnamed x26 -> x20, local copies, waits for them, and re-layouts: 15.8 us -> 13.5 us
  transfers between devices with their start and end apart: 9 -> 9, of which waited for: 9 -> 9; matrix products, arithmetic and copies ran while one was open for 6% -> 10% of each run, Pallas kernels for 0% -> 0%
where the time goes in v13:
time: 339 us; the launch traced here: 338 us
  waiting for transfers between devices  211 us (62%)
  matrix products  58.4 us (17%)
  other arithmetic  16.2 us (5%)
  Pallas kernels  16.2 us (5%)
  local copies, waits for them, and re-layouts  16.1 us (5%)
  between operations  14.3 us (4%)
  starting transfers between devices  5.53 us (2%)
    all_gather x1, waiting for transfers between devices, local(): lax.all_gather(jnp.stack([tokens_in, gated_local]), 'col', axis=2, tiled=...  109 us
    ppermute x7, waiting for transfers between devices, tree_sum(): value = value + lax.ppermute(value, axis, pairs)  69.6 us
    dot_general x4, matrix products, plain_dot(): return jnp.dot(left, right, preferred_element_type=jnp.float32)  48.5 us
    reduce_scatter x1, waiting for transfers between devices, local(): lax.psum_scatter(block_t.T, 'col', scatter_dimension=1, tiled=True)  32.3 us
    pallas_call x1, Pallas kernels, block_product(): pl.pallas_call(block_kernel, out_shape=jax.ShapeDtypeStruct((features, to...  16.2 us
    unnamed x20, local copies, waits for them, and re-layouts  13.5 us
    concatenate x1, other arithmetic, local(): inner_cat = jnp.concatenate([inner_weight, inner_down], axis=1)  10.7 us
  transfers between devices with their start and end apart: 9, of which 9 were waited for; matrix products, arithmetic and copies ran while one was open for 10% of the time, Pallas kernels for 0%

profile of v13, /device:TPU:1, one launch (start us, length us, event | category | flops | bytes accessed | tf_op | source)
XLA Modules:
  0.0 337.9 jit_solution(17679603840742066796)
XLA Ops:
  8.1 1.3 fusion.14
  9.4 2.3 pad_maximum_fusion.2
  12.5 12.7 %copy.15 = bf16[5120,864]{1,0:T(8,128)(2,1)} copy(bf16[5120,864]{0,1:T(8,128)(2,1)} %param.13) | data formatting | bytes 17694720 | tf_op args[3]
  25.3 10.7 %pad_maximum_fusion.weight_ref = bf16[5120,928]{1,0:T(8,128)(2,1)} fusion(bf16[5120,64]{1,0:T(8,128)(2,1)S(1)} %copy.16, bf16[5120,864]{1,0:T(8,128)(2,1)} %copy.15), kind=kLoop, calls=%fused_computation.4 | loop fusion | flops 19005440 | bytes 19005440 | tf_op jit(solution)/shard_map/concatenate | solution.py:99
  35.9 109.3 %all-gather.2.cloned.1.call-done = bf16[2,1024,5120]{1,2,0:T(8,128)(2,1)} async-done(((bf16[2,1024,320]{1,2,0:T(8,128)(2,1)}), bf16[2,1024,5120]{1,2,0:T(8,128)(2,1)}) %all-gather.2.cloned.1.call-update) | async-done | bytes 20971536 | tf_op jit(solution)/shard_map/all_gather | solution.py:97
  145.2 24.4 %fusion = f32[1024,928]{0,1:T(8,128)} fusion(bf16[2,1024,5120]{1,2,0:T(8,128)(2,1)} %all-gather.2.cloned.1.call-done, bf16[5120,64]{1,0:T(8,128)(2,1)S(1)} %copy.16, bf16[5120,864]{1,0:T(8,128)(2,1)} %copy.15), kind=kOutput, calls=%fused_computation.1 | convolution fusion | flops 9749790720 | bytes 24117248 | tf_op jit(solution)/shard_map/dot_general | solution.py:27
  169.6 6.0 %multiply_convert_fusion = (bf16[1024,864]{0,1:T(8,128)(2,1)}, f32[1024,864]{0,1:T(8,128)}) fusion(f32[864]{0:T(1024)S(1)} %copy-done.8, bf16[64,864]{1,0:T(8,128)(2,1)S(1)} %copy-done, f32[1024,928]{0,1:T(8,128)} %fusion), kind=kOutput, calls=%fused_computation.20 | convolution fusion | flops 123043840 | bytes 9223552 | tf_op jit(solution)/shard_map/dot_general | solution.py:27
  175.7 16.0 %fusion.1 = f32[1024,928]{0,1:T(8,128)S(1)} fusion(bf16[2,1024,5120]{1,2,0:T(8,128)(2,1)} %all-gather.2.cloned.1.call-done, bf16[5120,64]{0,1:T(8,128)(2,1)S(1)} %bitcast.32, bf16[5120,864]{0,1:T(8,128)(2,1)} %param.15), kind=kOutput, calls=%fused_computation.3 | convolution fusion | flops 9749790720 | bytes 23789568 | tf_op jit(solution)/shard_map/dot_general | solution.py:27
  191.7 5.5 %fusion.11 = bf16[1024,864]{0,1:T(8,128)(2,1)S(1)} fusion(f32[1024,864]{0,1:T(8,128)} %get-tuple-element.10, f32[1024,928]{0,1:T(8,128)S(1)} %fusion.1, bf16[864,64]{0,1:T(8,128)(2,1)S(1)} %copy-done.5), kind=kOutput, calls=%fused_computation.16 | convolution fusion | flops 131006464 | bytes 9220096 | tf_op jit(solution)/shard_map/dot_general | solution.py:31
  197.7 1.4 pad_maximum_fusion.1.grad_ref
  199.1 16.2 %shard_map.137 = bf16[5120,1024]{1,0:T(8,128)(2,1)} custom-call(bf16[5120,928]{1,0:T(8,128)(2,1)} %pad_maximum_fusion.weight_ref, bf16[928,1024]{1,0:T(8,128)(2,1)} %pad_maximum_fusion.1.grad_ref), custom_call_target="tpu_custom_call" | custom-call | flops 9730785280 | bytes 21889024 | tf_op jit(solution)/shard_map/pallas_call | solution.py:59
  215.3 2.0 fusion.23
  217.7 1.7 collective-permute-done
  219.6 14.7 %collective-permute-done.1 = f32[1024,128]{0,1:T(8,128)S(1)} collective-permute-done((f32[1024,128]{0,1:T(8,128)S(1)}, f32[1024,128]{0,1:T(8,128)S(1)}, u32[]{:S(2)}, u32[]{:S(2)}) %collective-permute-start.1) | collective-permute-done | bytes 524320 | tf_op jit(solution)/shard_map/ppermute | solution.py:46
  234.5 12.3 %collective-permute-done.2 = f32[1024,128]{0,1:T(8,128)S(1)} collective-permute-done((f32[1024,128]{0,1:T(8,128)S(1)}, f32[1024,128]{0,1:T(8,128)S(1)}, u32[]{:S(2)}, u32[]{:S(2)}) %collective-permute-start.2) | collective-permute-done | bytes 524320 | tf_op jit(solution)/shard_map/ppermute | solution.py:46
  246.9 1.1 collective-permute-start.3
  248.0 1.6 fusion.17
  249.6 1.6 fusion.18
  251.2 14.5 %collective-permute-done.3 = f32[1024,128]{0,1:T(8,128)S(1)} collective-permute-done((f32[1024,128]{0,1:T(8,128)S(1)}, f32[1024,128]{0,1:T(8,128)S(1)}, u32[]{:S(2)}, u32[]{:S(2)}) %collective-permute-start.3) | collective-permute-done | bytes 524320 | tf_op jit(solution)/shard_map/ppermute | solution.py:46
  266.9 9.5 %collective-permute-done.4 = f32[2368,64]{0,1:T(8,128)S(1)} collective-permute-done((f32[2368,64]{0,1:T(8,128)S(1)}, f32[2368,64]{0,1:T(8,128)S(1)}, u32[]{:S(2)}, u32[]{:S(2)}) %collective-permute-start.4) | collective-permute-done | bytes 606240 | tf_op jit(solution)/shard_map/ppermute | solution.py:46
  277.5 8.5 %collective-permute-done.5 = f32[2368,64]{0,1:T(8,128)S(1)} collective-permute-done((f32[2368,64]{0,1:T(8,128)S(1)}, f32[2368,64]{0,1:T(8,128)S(1)}, u32[]{:S(2)}, u32[]{:S(2)}) %collective-permute-start.5) | collective-permute-done | bytes 606240 | tf_op jit(solution)/shard_map/ppermute | solution.py:46
  286.1 2.7 collective-permute-start.6
  288.7 8.4 %collective-permute-done.6 = f32[2368,64]{0,1:T(8,128)S(1)} collective-permute-done((f32[2368,64]{0,1:T(8,128)S(1)}, f32[2368,64]{0,1:T(8,128)S(1)}, u32[]{:S(2)}, u32[]{:S(2)}) %collective-permute-start.6) | collective-permute-done | bytes 606240 | tf_op jit(solution)/shard_map/ppermute | solution.py:46
  298.8 32.3 %reduce-scatter.2.cloned.1.call-done = bf16[1024,320]{0,1:T(8,128)(2,1)} async-done(((bf16[1024,5120]{0,1:T(8,128)(2,1)}), bf16[1024,320]{0,1:T(8,128)(2,1)}) %reduce-scatter.2.cloned.1.call-update) | async-done | bytes 655376 | tf_op jit(solution)/shard_map/reduce_scatter | solution.py:115
  (44 shorter events, 6.9 us)
Async XLA Ops:
  7.2 162.5 %copy-start = (bf16[64,864]{1,0:T(8,128)(2,1)S(1)}, bf16[64,864]{1,0:T(8,128)(2,1)}, u32[]{:S(2)}) copy-start(bf16[64,864]{1,0:T(8,128)(2,1)} %param.17) | copy-start | bytes 331780
  7.2 4.6 %copy-start.4 = (bf16[5120,64]{0,1:T(8,128)(2,1)S(1)}, bf16[5120,64]{0,1:T(8,128)(2,1)}, u32[]{:S(2)}) copy-start(bf16[5120,64]{0,1:T(8,128)(2,1)} %param.16) | copy-start | bytes 1966084
  7.2 138.0 %all-gather.2.cloned.1.call-start = ((), (), s32[]{:S(2)}) async-start(), calls=%async_computation.1 | async-start | bytes 22282240 | tf_op jit(solution)/shard_map/all_gather | solution.py:97
  11.7 319.3 %reduce-scatter.2.cloned.1.call-start = ((), (), s32[]{:S(2)}) async-start(), calls=%async_computation.2 | async-start | bytes 11141120 | tf_op jit(solution)/shard_map/reduce_scatter | solution.py:115
  35.9 133.7 %copy-start.8 = (f32[864]{0:T(1024)S(1)}, f32[864]{0:T(1024)}, u32[]{:S(2)}) copy-start(f32[864]{0:T(1024)} %param.14) | copy-start | bytes 10372
  169.6 6.0 %copy-start.7 = (bf16[64,5120]{1,0:T(8,128)(2,1)S(1)}, bf16[64,5120]{1,0:T(8,128)(2,1)}, u32[]{:S(2)}) copy-start(bf16[64,5120]{1,0:T(8,128)(2,1)} %param.19) | copy-start | bytes 1966084
  175.7 16.0 %copy-start.5 = (bf16[864,64]{0,1:T(8,128)(2,1)S(1)}, bf16[864,64]{0,1:T(8,128)(2,1)}, u32[]{:S(2)}) copy-start(bf16[864,64]{0,1:T(8,128)(2,1)} %param.18) | copy-start | bytes 331780
  191.7 5.5 %copy-start.6 = (f32[1024,928]{0,1:T(8,128)}, f32[1024,928]{0,1:T(8,128)S(1)}, u32[]{:S(2)}) copy-start(f32[1024,928]{0,1:T(8,128)S(1)} %fusion.1) | copy-start | bytes 11403268
  215.3 32.7 %copy-start.1 = (bf16[1024,864]{0,1:T(8,128)(2,1)S(1)}, bf16[1024,864]{0,1:T(8,128)(2,1)}, u32[]{:S(2)}) copy-start(bf16[1024,864]{0,1:T(8,128)(2,1)} %get-tuple-element.9) | copy-start | bytes 5308420
  217.4 2.0 collective-permute-start
  219.5 14.9 %collective-permute-start.1 = (f32[1024,128]{0,1:T(8,128)S(1)}, f32[1024,128]{0,1:T(8,128)S(1)}, u32[]{:S(2)}, u32[]{:S(2)}) collective-permute-start(f32[1024,128]{0,1:T(8,128)S(1)} %fusion.20), channel_id=1, source_target_pairs={{0,2},{1,3},{2,0},{3,1},{4,6},{5,7},{6,4},{7,5},{8,10},{9,11},{10,... | collective-permute-start | bytes 1572872 | tf_op jit(solution)/shard_map/ppermute | solution.py:46
  234.4 31.4 %copy-start.2 = (bf16[1024,320]{0,1:T(8,128)(2,1)S(1)}, bf16[1024,320]{0,1:T(8,128)(2,1)}, u32[]{:S(2)}) copy-start(bf16[1024,320]{0,1:T(8,128)(2,1)} %param.10) | copy-start | bytes 1966084
  234.4 12.4 %collective-permute-start.2 = (f32[1024,128]{0,1:T(8,128)S(1)}, f32[1024,128]{0,1:T(8,128)S(1)}, u32[]{:S(2)}, u32[]{:S(2)}) collective-permute-start(f32[1024,128]{0,1:T(8,128)S(1)} %add.64), channel_id=1, source_target_pairs={{0,4},{1,5},{2,6},{3,7},{4,0},{5,1},{6,2},{7,3},{8,12},{9,13},{10,... | collective-permute-start | bytes 1572872 | tf_op jit(solution)/shard_map/ppermute | solution.py:46
  246.9 19.2 %copy-start.3 = (bf16[1024,320]{0,1:T(8,128)(2,1)S(1)}, bf16[1024,320]{0,1:T(8,128)(2,1)}, u32[]{:S(2)}) copy-start(bf16[1024,320]{0,1:T(8,128)(2,1)} %param.11) | copy-start | bytes 1966084
  246.9 18.8 %collective-permute-start.3 = (f32[1024,128]{0,1:T(8,128)S(1)}, f32[1024,128]{0,1:T(8,128)S(1)}, u32[]{:S(2)}, u32[]{:S(2)}) collective-permute-start(f32[1024,128]{0,1:T(8,128)S(1)} %add.65), channel_id=1, source_target_pairs={{0,8},{1,9},{2,10},{3,11},{4,12},{5,13},{6,14},{7,15},{8,0},{9,1},... | collective-permute-start | bytes 1572872 | tf_op jit(solution)/shard_map/ppermute | solution.py:46
  266.8 9.6 %collective-permute-start.4 = (f32[2368,64]{0,1:T(8,128)S(1)}, f32[2368,64]{0,1:T(8,128)S(1)}, u32[]{:S(2)}, u32[]{:S(2)}) collective-permute-start(f32[2368,64]{0,1:T(8,128)S(1)} %concatenate.19), channel_id=1, source_target_pairs={{0,16},{16,0},{32,48},{48,32},{64,80},{80,64},{96,112},{112,96},{1... | collective-permute-start | bytes 1818632 | tf_op jit(solution)/shard_map/ppermute | solution.py:46
  276.4 9.6 %collective-permute-start.5 = (f32[2368,64]{0,1:T(8,128)S(1)}, f32[2368,64]{0,1:T(8,128)S(1)}, u32[]{:S(2)}, u32[]{:S(2)}) collective-permute-start(f32[2368,64]{0,1:T(8,128)S(1)} %add.67), channel_id=1, source_target_pairs={{0,32},{16,48},{32,0},{48,16},{64,96},{80,112},{96,64},{112,80},{1... | collective-permute-start | bytes 1818632 | tf_op jit(solution)/shard_map/ppermute | solution.py:46
  286.1 11.1 %collective-permute-start.6 = (f32[2368,64]{0,1:T(8,128)S(1)}, f32[2368,64]{0,1:T(8,128)S(1)}, u32[]{:S(2)}, u32[]{:S(2)}) collective-permute-start(f32[2368,64]{0,1:T(8,128)S(1)} %add.68), channel_id=1, source_target_pairs={{0,64},{16,80},{32,96},{48,112},{64,0},{80,16},{96,32},{112,48},{1... | collective-permute-start | bytes 1818632 | tf_op jit(solution)/shard_map/ppermute | solution.py:46
Sparse Core Ops, SparseCore 0:
  11.8 133.3 all-gather.1
  215.4 115.5 reduce-scatter.1

commit v14 on v13

--- a/solution.py
+++ b/solution.py
@@ -110,7 +110,8 @@
     grad_pre = (grad_hidden * gelu_slope(pre)).astype(jnp.bfloat16)
     pre_low_part = dot_rows(grad_pre, inner_up)
     block_t = block_product(
-        inner_cat, jnp.concatenate([grad_pre.T, pre_low_part.astype(jnp.bfloat16).T], axis=0)
+        jnp.concatenate([inner_down, inner_weight], axis=1),
+        jnp.concatenate([pre_low_part.astype(jnp.bfloat16).T, grad_pre.T], axis=0),
     )
     tokens_grad = lax.psum_scatter(block_t.T, "col", scatter_dimension=1, tiled=True)
 

time: 339 us -> 328 us (0.968)
  matrix products: 58.4 us -> 47.5 us
    dot_general x4, matrix products: 48.5 us -> 37.6 us  [plain_dot(): return jnp.dot(left, right, preferred_element_type=jnp.float32)]
    unnamed x20 -> x22, local copies, waits for them, and re-layouts: 13.5 us -> 13.6 us
where the time goes in v14:
time: 328 us; the launch traced here: 327 us
  waiting for transfers between devices  210 us (64%)
  matrix products  47.5 us (14%)
  other arithmetic  17.2 us (5%)
  local copies, waits for them, and re-layouts  16.2 us (5%)
  Pallas kernels  16.2 us (5%)
  between operations  14.3 us (4%)
  starting transfers between devices  5.87 us (2%)
    all_gather x1, waiting for transfers between devices, local(): lax.all_gather(jnp.stack([tokens_in, gated_local]), 'col', axis=2, tiled=...  108 us
    ppermute x7, waiting for transfers between devices, tree_sum(): value = value + lax.ppermute(value, axis, pairs)  69.3 us
    dot_general x4, matrix products, plain_dot(): return jnp.dot(left, right, preferred_element_type=jnp.float32)  37.6 us
    reduce_scatter x1, waiting for transfers between devices, local(): lax.psum_scatter(block_t.T, 'col', scatter_dimension=1, tiled=True)  32.2 us
    pallas_call x1, Pallas kernels, block_product(): pl.pallas_call(block_kernel, out_shape=jax.ShapeDtypeStruct((features, to...  16.2 us
    unnamed x22, local copies, waits for them, and re-layouts  13.6 us
    concatenate x1, other arithmetic, local(): jnp.concatenate([inner_down, inner_weight], axis=1)  11.7 us
  transfers between devices with their start and end apart: 9, of which 9 were waited for; matrix products, arithmetic and copies ran while one was open for 10% of the time, Pallas kernels for 0%

profile of v14, /device:TPU:1, one launch (start us, length us, event | category | flops | bytes accessed | tf_op | source)
XLA Modules:
  0.0 327.0 jit_solution(5176840837760548024)
XLA Ops:
  8.1 1.3 fusion.17
  9.4 2.3 pad_maximum_fusion.2
  12.5 12.8 %copy.16 = bf16[5120,864]{1,0:T(8,128)(2,1)} copy(bf16[5120,864]{0,1:T(8,128)(2,1)} %param.13) | data formatting | bytes 17694720 | tf_op args[3]
  25.4 11.7 %pad_maximum_fusion.weight_ref = bf16[5120,928]{1,0:T(8,128)(2,1)} fusion(bf16[5120,864]{1,0:T(8,128)(2,1)} %copy.16, bf16[5120,64]{1,0:T(8,128)(2,1)S(1)} %copy.15), kind=kLoop, calls=%fused_computation.4 | loop fusion | flops 19005440 | bytes 19005440 | tf_op jit(solution)/shard_map/concatenate | solution.py:113
  37.1 108.1 %all-gather.2.cloned.1.call-done = bf16[2,1024,5120]{1,2,0:T(8,128)(2,1)} async-done(((bf16[2,1024,320]{1,2,0:T(8,128)(2,1)}), bf16[2,1024,5120]{1,2,0:T(8,128)(2,1)}) %all-gather.2.cloned.1.call-update) | async-done | bytes 20971536 | tf_op jit(solution)/shard_map/all_gather | solution.py:97
  145.2 15.8 %fusion = f32[1024,928]{0,1:T(8,128)S(1)} fusion(bf16[2,1024,5120]{1,2,0:T(8,128)(2,1)} %all-gather.2.cloned.1.call-done, bf16[5120,64]{0,1:T(8,128)(2,1)S(1)} %copy-done.4, bf16[5120,864]{0,1:T(8,128)(2,1)} %param.13), kind=kOutput, calls=%fused_computation.1 | convolution fusion | flops 9749790720 | bytes 23789568 | tf_op jit(solution)/shard_map/dot_general | solution.py:27
  161.1 3.9 %multiply_convert_fusion = (bf16[1024,864]{0,1:T(8,128)(2,1)}, f32[1024,864]{0,1:T(8,128)}) fusion(f32[864]{0:T(1024)S(1)} %copy-done.9, bf16[64,864]{1,0:T(8,128)(2,1)S(1)} %copy-done, f32[1024,928]{0,1:T(8,128)S(1)} %fusion), kind=kOutput, calls=%fused_computation.23 | convolution fusion | flops 123043840 | bytes 9223552 | tf_op jit(solution)/shard_map/dot_general | solution.py:27
  165.0 15.8 %fusion.1 = f32[1024,928]{0,1:T(8,128)S(1)} fusion(bf16[2,1024,5120]{1,2,0:T(8,128)(2,1)} %all-gather.2.cloned.1.call-done, bf16[5120,64]{0,1:T(8,128)(2,1)S(1)} %bitcast.32, bf16[5120,864]{0,1:T(8,128)(2,1)} %param.15), kind=kOutput, calls=%fused_computation.3 | convolution fusion | flops 9749790720 | bytes 23789568 | tf_op jit(solution)/shard_map/dot_general | solution.py:27
  180.9 5.5 %fusion.14 = bf16[1024,864]{0,1:T(8,128)(2,1)S(1)} fusion(f32[1024,864]{0,1:T(8,128)} %get-tuple-element.10, f32[1024,928]{0,1:T(8,128)S(1)} %fusion.1, bf16[864,64]{0,1:T(8,128)(2,1)S(1)} %copy-done.5), kind=kOutput, calls=%fused_computation.19 | convolution fusion | flops 131006464 | bytes 9220096 | tf_op jit(solution)/shard_map/dot_general | solution.py:31
  186.9 1.4 pad_maximum_fusion.1.grad_ref
  188.3 16.2 %shard_map.137 = bf16[5120,1024]{1,0:T(8,128)(2,1)} custom-call(bf16[5120,928]{1,0:T(8,128)(2,1)} %pad_maximum_fusion.weight_ref, bf16[928,1024]{1,0:T(8,128)(2,1)} %pad_maximum_fusion.1.grad_ref), custom_call_target="tpu_custom_call" | custom-call | flops 9730785280 | bytes 21889024 | tf_op jit(solution)/shard_map/pallas_call | solution.py:59
  204.5 2.1 fusion.27
  206.9 1.7 collective-permute-done
  208.8 14.7 %collective-permute-done.1 = f32[1024,128]{0,1:T(8,128)S(1)} collective-permute-done((f32[1024,128]{0,1:T(8,128)S(1)}, f32[1024,128]{0,1:T(8,128)S(1)}, u32[]{:S(2)}, u32[]{:S(2)}) %collective-permute-start.1) | collective-permute-done | bytes 524320 | tf_op jit(solution)/shard_map/ppermute | solution.py:46
  223.7 12.3 %collective-permute-done.2 = f32[1024,128]{0,1:T(8,128)S(1)} collective-permute-done((f32[1024,128]{0,1:T(8,128)S(1)}, f32[1024,128]{0,1:T(8,128)S(1)}, u32[]{:S(2)}, u32[]{:S(2)}) %collective-permute-start.2) | collective-permute-done | bytes 524320 | tf_op jit(solution)/shard_map/ppermute | solution.py:46
  237.2 1.6 fusion.20
  238.9 1.6 fusion.21
  240.5 14.5 %collective-permute-done.3 = f32[1024,128]{0,1:T(8,128)S(1)} collective-permute-done((f32[1024,128]{0,1:T(8,128)S(1)}, f32[1024,128]{0,1:T(8,128)S(1)}, u32[]{:S(2)}, u32[]{:S(2)}) %collective-permute-start.3) | collective-permute-done | bytes 524320 | tf_op jit(solution)/shard_map/ppermute | solution.py:46
  256.1 9.5 %collective-permute-done.4 = f32[2368,64]{0,1:T(8,128)S(1)} collective-permute-done((f32[2368,64]{0,1:T(8,128)S(1)}, f32[2368,64]{0,1:T(8,128)S(1)}, u32[]{:S(2)}, u32[]{:S(2)}) %collective-permute-start.4) | collective-permute-done | bytes 606240 | tf_op jit(solution)/shard_map/ppermute | solution.py:46
  265.6 1.2 collective-permute-start.5
  266.8 8.4 %collective-permute-done.5 = f32[2368,64]{0,1:T(8,128)S(1)} collective-permute-done((f32[2368,64]{0,1:T(8,128)S(1)}, f32[2368,64]{0,1:T(8,128)S(1)}, u32[]{:S(2)}, u32[]{:S(2)}) %collective-permute-start.5) | collective-permute-done | bytes 606240 | tf_op jit(solution)/shard_map/ppermute | solution.py:46
  275.3 2.8 collective-permute-start.6
  278.0 8.3 %collective-permute-done.6 = f32[2368,64]{0,1:T(8,128)S(1)} collective-permute-done((f32[2368,64]{0,1:T(8,128)S(1)}, f32[2368,64]{0,1:T(8,128)S(1)}, u32[]{:S(2)}, u32[]{:S(2)}) %collective-permute-start.6) | collective-permute-done | bytes 606240 | tf_op jit(solution)/shard_map/ppermute | solution.py:46
  288.0 32.2 %reduce-scatter.2.cloned.1.call-done = bf16[1024,320]{0,1:T(8,128)(2,1)} async-done(((bf16[1024,5120]{0,1:T(8,128)(2,1)}), bf16[1024,320]{0,1:T(8,128)(2,1)}) %reduce-scatter.2.cloned.1.call-update) | async-done | bytes 655376 | tf_op jit(solution)/shard_map/reduce_scatter | solution.py:116
  (46 shorter events, 7.1 us)
Async XLA Ops:
  7.2 153.9 %copy-start = (bf16[64,864]{1,0:T(8,128)(2,1)S(1)}, bf16[64,864]{1,0:T(8,128)(2,1)}, u32[]{:S(2)}) copy-start(bf16[64,864]{1,0:T(8,128)(2,1)} %param.17) | copy-start | bytes 331780
  7.2 4.6 %copy-start.4 = (bf16[5120,64]{0,1:T(8,128)(2,1)S(1)}, bf16[5120,64]{0,1:T(8,128)(2,1)}, u32[]{:S(2)}) copy-start(bf16[5120,64]{0,1:T(8,128)(2,1)} %param.16) | copy-start | bytes 1966084
  7.2 138.0 %all-gather.2.cloned.1.call-start = ((), (), s32[]{:S(2)}) async-start(), calls=%async_computation.1 | async-start | bytes 22282240 | tf_op jit(solution)/shard_map/all_gather | solution.py:97
  11.7 308.5 %reduce-scatter.2.cloned.1.call-start = ((), (), s32[]{:S(2)}) async-start(), calls=%async_computation.2 | async-start | bytes 11141120 | tf_op jit(solution)/shard_map/reduce_scatter | solution.py:116
  37.1 124.0 %copy-start.9 = (f32[864]{0:T(1024)S(1)}, f32[864]{0:T(1024)}, u32[]{:S(2)}) copy-start(f32[864]{0:T(1024)} %param.14) | copy-start | bytes 10372
  161.1 3.9 %copy-start.6 = (f32[1024,928]{0,1:T(8,128)}, f32[1024,928]{0,1:T(8,128)S(1)}, u32[]{:S(2)}) copy-start(f32[1024,928]{0,1:T(8,128)S(1)} %fusion) | copy-start | bytes 11403268
  161.1 3.9 %copy-start.8 = (bf16[64,5120]{1,0:T(8,128)(2,1)S(1)}, bf16[64,5120]{1,0:T(8,128)(2,1)}, u32[]{:S(2)}) copy-start(bf16[64,5120]{1,0:T(8,128)(2,1)} %param.19) | copy-start | bytes 1966084
  165.0 15.9 %copy-start.5 = (bf16[864,64]{0,1:T(8,128)(2,1)S(1)}, bf16[864,64]{0,1:T(8,128)(2,1)}, u32[]{:S(2)}) copy-start(bf16[864,64]{0,1:T(8,128)(2,1)} %param.18) | copy-start | bytes 331780
  180.8 5.5 %copy-start.7 = (f32[1024,928]{0,1:T(8,128)}, f32[1024,928]{0,1:T(8,128)S(1)}, u32[]{:S(2)}) copy-start(f32[1024,928]{0,1:T(8,128)S(1)} %fusion.1) | copy-start | bytes 11403268
  204.5 32.8 %copy-start.1 = (bf16[1024,864]{0,1:T(8,128)(2,1)S(1)}, bf16[1024,864]{0,1:T(8,128)(2,1)}, u32[]{:S(2)}) copy-start(bf16[1024,864]{0,1:T(8,128)(2,1)} %get-tuple-element.9) | copy-start | bytes 5308420
  206.6 2.0 collective-permute-start
  208.6 14.9 %collective-permute-start.1 = (f32[1024,128]{0,1:T(8,128)S(1)}, f32[1024,128]{0,1:T(8,128)S(1)}, u32[]{:S(2)}, u32[]{:S(2)}) collective-permute-start(f32[1024,128]{0,1:T(8,128)S(1)} %fusion.24), channel_id=1, source_target_pairs={{0,2},{1,3},{2,0},{3,1},{4,6},{5,7},{6,4},{7,5},{8,10},{9,11},{10,... | collective-permute-start | bytes 1572872 | tf_op jit(solution)/shard_map/ppermute | solution.py:46
  223.6 31.4 %copy-start.2 = (bf16[1024,320]{0,1:T(8,128)(2,1)S(1)}, bf16[1024,320]{0,1:T(8,128)(2,1)}, u32[]{:S(2)}) copy-start(bf16[1024,320]{0,1:T(8,128)(2,1)} %param.10) | copy-start | bytes 1966084
  223.6 12.4 %collective-permute-start.2 = (f32[1024,128]{0,1:T(8,128)S(1)}, f32[1024,128]{0,1:T(8,128)S(1)}, u32[]{:S(2)}, u32[]{:S(2)}) collective-permute-start(f32[1024,128]{0,1:T(8,128)S(1)} %add.64), channel_id=1, source_target_pairs={{0,4},{1,5},{2,6},{3,7},{4,0},{5,1},{6,2},{7,3},{8,12},{9,13},{10,... | collective-permute-start | bytes 1572872 | tf_op jit(solution)/shard_map/ppermute | solution.py:46
  236.1 19.3 %copy-start.3 = (bf16[1024,320]{0,1:T(8,128)(2,1)S(1)}, bf16[1024,320]{0,1:T(8,128)(2,1)}, u32[]{:S(2)}) copy-start(bf16[1024,320]{0,1:T(8,128)(2,1)} %param.11) | copy-start | bytes 1966084
  236.1 18.8 %collective-permute-start.3 = (f32[1024,128]{0,1:T(8,128)S(1)}, f32[1024,128]{0,1:T(8,128)S(1)}, u32[]{:S(2)}, u32[]{:S(2)}) collective-permute-start(f32[1024,128]{0,1:T(8,128)S(1)} %add.65), channel_id=1, source_target_pairs={{0,8},{1,9},{2,10},{3,11},{4,12},{5,13},{6,14},{7,15},{8,0},{9,1},... | collective-permute-start | bytes 1572872 | tf_op jit(solution)/shard_map/ppermute | solution.py:46
  256.0 9.6 %collective-permute-start.4 = (f32[2368,64]{0,1:T(8,128)S(1)}, f32[2368,64]{0,1:T(8,128)S(1)}, u32[]{:S(2)}, u32[]{:S(2)}) collective-permute-start(f32[2368,64]{0,1:T(8,128)S(1)} %concatenate.23), channel_id=1, source_target_pairs={{0,16},{16,0},{32,48},{48,32},{64,80},{80,64},{96,112},{112,96},{1... | collective-permute-start | bytes 1818632 | tf_op jit(solution)/shard_map/ppermute | solution.py:46
  265.6 9.6 %collective-permute-start.5 = (f32[2368,64]{0,1:T(8,128)S(1)}, f32[2368,64]{0,1:T(8,128)S(1)}, u32[]{:S(2)}, u32[]{:S(2)}) collective-permute-start(f32[2368,64]{0,1:T(8,128)S(1)} %add.67), channel_id=1, source_target_pairs={{0,32},{16,48},{32,0},{48,16},{64,96},{80,112},{96,64},{112,80},{1... | collective-permute-start | bytes 1818632 | tf_op jit(solution)/shard_map/ppermute | solution.py:46
  275.3 11.1 %collective-permute-start.6 = (f32[2368,64]{0,1:T(8,128)S(1)}, f32[2368,64]{0,1:T(8,128)S(1)}, u32[]{:S(2)}, u32[]{:S(2)}) collective-permute-start(f32[2368,64]{0,1:T(8,128)S(1)} %add.68), channel_id=1, source_target_pairs={{0,64},{16,80},{32,96},{48,112},{64,0},{80,16},{96,32},{112,48},{1... | collective-permute-start | bytes 1818632 | tf_op jit(solution)/shard_map/ppermute | solution.py:46
Sparse Core Ops, SparseCore 0:
  11.8 133.3 all-gather.1
  204.6 115.5 reduce-scatter.1

commit v15 on v14

--- a/solution.py
+++ b/solution.py
@@ -53,7 +53,7 @@
     out_ref[...] = block.astype(out_ref.dtype)
 
 
-def block_product(weight, grad_t, tile=640):
+def block_product(weight, grad_t, tile=1280):
     features, depth = weight.shape
     tokens = grad_t.shape[1]
     return pl.pallas_call(

time: 328 us -> 327 us (level)
  no operation moved by 1% of the time
where the time goes in v15:
time: 327 us; the launch traced here: 326 us
  waiting for transfers between devices  210 us (64%)
  matrix products  47.5 us (15%)
  other arithmetic  17.2 us (5%)
  local copies, waits for them, and re-layouts  16.2 us (5%)
  Pallas kernels  15.5 us (5%)
  between operations  14.3 us (4%)
  starting transfers between devices  5.88 us (2%)
    all_gather x1, waiting for transfers between devices, local(): lax.all_gather(jnp.stack([tokens_in, gated_local]), 'col', axis=2, tiled=...  108 us
    ppermute x7, waiting for transfers between devices, tree_sum(): value = value + lax.ppermute(value, axis, pairs)  69.3 us
    dot_general x4, matrix products, plain_dot(): return jnp.dot(left, right, preferred_element_type=jnp.float32)  37.6 us
    reduce_scatter x1, waiting for transfers between devices, local(): lax.psum_scatter(block_t.T, 'col', scatter_dimension=1, tiled=True)  32.2 us
    pallas_call x1, Pallas kernels, block_product(): pl.pallas_call(block_kernel, out_shape=jax.ShapeDtypeStruct((features, to...  15.5 us
    unnamed x22, local copies, waits for them, and re-layouts  13.6 us
    concatenate x1, other arithmetic, local(): jnp.concatenate([inner_down, inner_weight], axis=1)  11.7 us
  transfers between devices with their start and end apart: 9, of which 9 were waited for; matrix products, arithmetic and copies ran while one was open for 10% of the time, Pallas kernels for 0%

profile of v15, /device:TPU:1, one launch (start us, length us, event | category | flops | bytes accessed | tf_op | source)
XLA Modules:
  0.0 326.3 jit_solution(11381858372796694928)
XLA Ops:
  8.1 1.3 fusion.17
  9.4 2.3 pad_maximum_fusion.2
  12.5 12.8 %copy.16 = bf16[5120,864]{1,0:T(8,128)(2,1)} copy(bf16[5120,864]{0,1:T(8,128)(2,1)} %param.13) | data formatting | bytes 17694720 | tf_op args[3]
  25.4 11.7 %pad_maximum_fusion.weight_ref = bf16[5120,928]{1,0:T(8,128)(2,1)} fusion(bf16[5120,864]{1,0:T(8,128)(2,1)} %copy.16, bf16[5120,64]{1,0:T(8,128)(2,1)S(1)} %copy.15), kind=kLoop, calls=%fused_computation.4 | loop fusion | flops 19005440 | bytes 19005440 | tf_op jit(solution)/shard_map/concatenate | solution.py:113
  37.1 108.1 %all-gather.2.cloned.1.call-done = bf16[2,1024,5120]{1,2,0:T(8,128)(2,1)} async-done(((bf16[2,1024,320]{1,2,0:T(8,128)(2,1)}), bf16[2,1024,5120]{1,2,0:T(8,128)(2,1)}) %all-gather.2.cloned.1.call-update) | async-done | bytes 20971536 | tf_op jit(solution)/shard_map/all_gather | solution.py:97
  145.2 15.8 %fusion = f32[1024,928]{0,1:T(8,128)S(1)} fusion(bf16[2,1024,5120]{1,2,0:T(8,128)(2,1)} %all-gather.2.cloned.1.call-done, bf16[5120,64]{0,1:T(8,128)(2,1)S(1)} %copy-done.4, bf16[5120,864]{0,1:T(8,128)(2,1)} %param.13), kind=kOutput, calls=%fused_computation.1 | convolution fusion | flops 9749790720 | bytes 23789568 | tf_op jit(solution)/shard_map/dot_general | solution.py:27
  161.1 3.9 %multiply_convert_fusion = (bf16[1024,864]{0,1:T(8,128)(2,1)}, f32[1024,864]{0,1:T(8,128)}) fusion(f32[864]{0:T(1024)S(1)} %copy-done.9, bf16[64,864]{1,0:T(8,128)(2,1)S(1)} %copy-done, f32[1024,928]{0,1:T(8,128)S(1)} %fusion), kind=kOutput, calls=%fused_computation.23 | convolution fusion | flops 123043840 | bytes 9223552 | tf_op jit(solution)/shard_map/dot_general | solution.py:27
  165.0 15.8 %fusion.1 = f32[1024,928]{0,1:T(8,128)S(1)} fusion(bf16[2,1024,5120]{1,2,0:T(8,128)(2,1)} %all-gather.2.cloned.1.call-done, bf16[5120,64]{0,1:T(8,128)(2,1)S(1)} %bitcast.32, bf16[5120,864]{0,1:T(8,128)(2,1)} %param.15), kind=kOutput, calls=%fused_computation.3 | convolution fusion | flops 9749790720 | bytes 23789568 | tf_op jit(solution)/shard_map/dot_general | solution.py:27
  180.9 5.5 %fusion.14 = bf16[1024,864]{0,1:T(8,128)(2,1)S(1)} fusion(f32[1024,864]{0,1:T(8,128)} %get-tuple-element.10, f32[1024,928]{0,1:T(8,128)S(1)} %fusion.1, bf16[864,64]{0,1:T(8,128)(2,1)S(1)} %copy-done.5), kind=kOutput, calls=%fused_computation.19 | convolution fusion | flops 131006464 | bytes 9220096 | tf_op jit(solution)/shard_map/dot_general | solution.py:31
  186.9 1.4 pad_maximum_fusion.1.grad_ref
  188.3 15.5 %shard_map.137 = bf16[5120,1024]{1,0:T(8,128)(2,1)} custom-call(bf16[5120,928]{1,0:T(8,128)(2,1)} %pad_maximum_fusion.weight_ref, bf16[928,1024]{1,0:T(8,128)(2,1)} %pad_maximum_fusion.1.grad_ref), custom_call_target="tpu_custom_call" | custom-call | flops 9730785280 | bytes 21889024 | tf_op jit(solution)/shard_map/pallas_call | solution.py:59
  203.8 2.1 fusion.27
  206.2 1.7 collective-permute-done
  208.1 14.7 %collective-permute-done.1 = f32[1024,128]{0,1:T(8,128)S(1)} collective-permute-done((f32[1024,128]{0,1:T(8,128)S(1)}, f32[1024,128]{0,1:T(8,128)S(1)}, u32[]{:S(2)}, u32[]{:S(2)}) %collective-permute-start.1) | collective-permute-done | bytes 524320 | tf_op jit(solution)/shard_map/ppermute | solution.py:46
  223.0 12.3 %collective-permute-done.2 = f32[1024,128]{0,1:T(8,128)S(1)} collective-permute-done((f32[1024,128]{0,1:T(8,128)S(1)}, f32[1024,128]{0,1:T(8,128)S(1)}, u32[]{:S(2)}, u32[]{:S(2)}) %collective-permute-start.2) | collective-permute-done | bytes 524320 | tf_op jit(solution)/shard_map/ppermute | solution.py:46
  236.5 1.6 fusion.20
  238.1 1.6 fusion.21
  239.8 14.5 %collective-permute-done.3 = f32[1024,128]{0,1:T(8,128)S(1)} collective-permute-done((f32[1024,128]{0,1:T(8,128)S(1)}, f32[1024,128]{0,1:T(8,128)S(1)}, u32[]{:S(2)}, u32[]{:S(2)}) %collective-permute-start.3) | collective-permute-done | bytes 524320 | tf_op jit(solution)/shard_map/ppermute | solution.py:46
  255.4 9.5 %collective-permute-done.4 = f32[2368,64]{0,1:T(8,128)S(1)} collective-permute-done((f32[2368,64]{0,1:T(8,128)S(1)}, f32[2368,64]{0,1:T(8,128)S(1)}, u32[]{:S(2)}, u32[]{:S(2)}) %collective-permute-start.4) | collective-permute-done | bytes 606240 | tf_op jit(solution)/shard_map/ppermute | solution.py:46
  264.9 1.2 collective-permute-start.5
  266.1 8.4 %collective-permute-done.5 = f32[2368,64]{0,1:T(8,128)S(1)} collective-permute-done((f32[2368,64]{0,1:T(8,128)S(1)}, f32[2368,64]{0,1:T(8,128)S(1)}, u32[]{:S(2)}, u32[]{:S(2)}) %collective-permute-start.5) | collective-permute-done | bytes 606240 | tf_op jit(solution)/shard_map/ppermute | solution.py:46
  274.6 2.8 collective-permute-start.6
  277.3 8.3 %collective-permute-done.6 = f32[2368,64]{0,1:T(8,128)S(1)} collective-permute-done((f32[2368,64]{0,1:T(8,128)S(1)}, f32[2368,64]{0,1:T(8,128)S(1)}, u32[]{:S(2)}, u32[]{:S(2)}) %collective-permute-start.6) | collective-permute-done | bytes 606240 | tf_op jit(solution)/shard_map/ppermute | solution.py:46
  287.3 32.2 %reduce-scatter.2.cloned.1.call-done = bf16[1024,320]{0,1:T(8,128)(2,1)} async-done(((bf16[1024,5120]{0,1:T(8,128)(2,1)}), bf16[1024,320]{0,1:T(8,128)(2,1)}) %reduce-scatter.2.cloned.1.call-update) | async-done | bytes 655376 | tf_op jit(solution)/shard_map/reduce_scatter | solution.py:116
  (46 shorter events, 7.1 us)
Async XLA Ops:
  7.2 153.9 %copy-start = (bf16[64,864]{1,0:T(8,128)(2,1)S(1)}, bf16[64,864]{1,0:T(8,128)(2,1)}, u32[]{:S(2)}) copy-start(bf16[64,864]{1,0:T(8,128)(2,1)} %param.17) | copy-start | bytes 331780
  7.2 4.6 %copy-start.4 = (bf16[5120,64]{0,1:T(8,128)(2,1)S(1)}, bf16[5120,64]{0,1:T(8,128)(2,1)}, u32[]{:S(2)}) copy-start(bf16[5120,64]{0,1:T(8,128)(2,1)} %param.16) | copy-start | bytes 1966084
  7.2 138.0 %all-gather.2.cloned.1.call-start = ((), (), s32[]{:S(2)}) async-start(), calls=%async_computation.1 | async-start | bytes 22282240 | tf_op jit(solution)/shard_map/all_gather | solution.py:97
  11.7 307.8 %reduce-scatter.2.cloned.1.call-start = ((), (), s32[]{:S(2)}) async-start(), calls=%async_computation.2 | async-start | bytes 11141120 | tf_op jit(solution)/shard_map/reduce_scatter | solution.py:116
  37.1 124.0 %copy-start.9 = (f32[864]{0:T(1024)S(1)}, f32[864]{0:T(1024)}, u32[]{:S(2)}) copy-start(f32[864]{0:T(1024)} %param.14) | copy-start | bytes 10372
  161.1 3.9 %copy-start.6 = (f32[1024,928]{0,1:T(8,128)}, f32[1024,928]{0,1:T(8,128)S(1)}, u32[]{:S(2)}) copy-start(f32[1024,928]{0,1:T(8,128)S(1)} %fusion) | copy-start | bytes 11403268
  161.1 3.9 %copy-start.8 = (bf16[64,5120]{1,0:T(8,128)(2,1)S(1)}, bf16[64,5120]{1,0:T(8,128)(2,1)}, u32[]{:S(2)}) copy-start(bf16[64,5120]{1,0:T(8,128)(2,1)} %param.19) | copy-start | bytes 1966084
  165.0 15.9 %copy-start.5 = (bf16[864,64]{0,1:T(8,128)(2,1)S(1)}, bf16[864,64]{0,1:T(8,128)(2,1)}, u32[]{:S(2)}) copy-start(bf16[864,64]{0,1:T(8,128)(2,1)} %param.18) | copy-start | bytes 331780
  180.8 5.5 %copy-start.7 = (f32[1024,928]{0,1:T(8,128)}, f32[1024,928]{0,1:T(8,128)S(1)}, u32[]{:S(2)}) copy-start(f32[1024,928]{0,1:T(8,128)S(1)} %fusion.1) | copy-start | bytes 11403268
  203.8 32.8 %copy-start.1 = (bf16[1024,864]{0,1:T(8,128)(2,1)S(1)}, bf16[1024,864]{0,1:T(8,128)(2,1)}, u32[]{:S(2)}) copy-start(bf16[1024,864]{0,1:T(8,128)(2,1)} %get-tuple-element.9) | copy-start | bytes 5308420
  205.9 2.0 collective-permute-start
  207.9 14.9 %collective-permute-start.1 = (f32[1024,128]{0,1:T(8,128)S(1)}, f32[1024,128]{0,1:T(8,128)S(1)}, u32[]{:S(2)}, u32[]{:S(2)}) collective-permute-start(f32[1024,128]{0,1:T(8,128)S(1)} %fusion.24), channel_id=1, source_target_pairs={{0,2},{1,3},{2,0},{3,1},{4,6},{5,7},{6,4},{7,5},{8,10},{9,11},{10,... | collective-permute-start | bytes 1572872 | tf_op jit(solution)/shard_map/ppermute | solution.py:46
  222.9 31.4 %copy-start.2 = (bf16[1024,320]{0,1:T(8,128)(2,1)S(1)}, bf16[1024,320]{0,1:T(8,128)(2,1)}, u32[]{:S(2)}) copy-start(bf16[1024,320]{0,1:T(8,128)(2,1)} %param.10) | copy-start | bytes 1966084
  222.9 12.4 %collective-permute-start.2 = (f32[1024,128]{0,1:T(8,128)S(1)}, f32[1024,128]{0,1:T(8,128)S(1)}, u32[]{:S(2)}, u32[]{:S(2)}) collective-permute-start(f32[1024,128]{0,1:T(8,128)S(1)} %add.64), channel_id=1, source_target_pairs={{0,4},{1,5},{2,6},{3,7},{4,0},{5,1},{6,2},{7,3},{8,12},{9,13},{10,... | collective-permute-start | bytes 1572872 | tf_op jit(solution)/shard_map/ppermute | solution.py:46
  235.4 19.3 %copy-start.3 = (bf16[1024,320]{0,1:T(8,128)(2,1)S(1)}, bf16[1024,320]{0,1:T(8,128)(2,1)}, u32[]{:S(2)}) copy-start(bf16[1024,320]{0,1:T(8,128)(2,1)} %param.11) | copy-start | bytes 1966084
  235.4 18.8 %collective-permute-start.3 = (f32[1024,128]{0,1:T(8,128)S(1)}, f32[1024,128]{0,1:T(8,128)S(1)}, u32[]{:S(2)}, u32[]{:S(2)}) collective-permute-start(f32[1024,128]{0,1:T(8,128)S(1)} %add.65), channel_id=1, source_target_pairs={{0,8},{1,9},{2,10},{3,11},{4,12},{5,13},{6,14},{7,15},{8,0},{9,1},... | collective-permute-start | bytes 1572872 | tf_op jit(solution)/shard_map/ppermute | solution.py:46
  255.3 9.6 %collective-permute-start.4 = (f32[2368,64]{0,1:T(8,128)S(1)}, f32[2368,64]{0,1:T(8,128)S(1)}, u32[]{:S(2)}, u32[]{:S(2)}) collective-permute-start(f32[2368,64]{0,1:T(8,128)S(1)} %concatenate.23), channel_id=1, source_target_pairs={{0,16},{16,0},{32,48},{48,32},{64,80},{80,64},{96,112},{112,96},{1... | collective-permute-start | bytes 1818632 | tf_op jit(solution)/shard_map/ppermute | solution.py:46
  264.9 9.6 %collective-permute-start.5 = (f32[2368,64]{0,1:T(8,128)S(1)}, f32[2368,64]{0,1:T(8,128)S(1)}, u32[]{:S(2)}, u32[]{:S(2)}) collective-permute-start(f32[2368,64]{0,1:T(8,128)S(1)} %add.67), channel_id=1, source_target_pairs={{0,32},{16,48},{32,0},{48,16},{64,96},{80,112},{96,64},{112,80},{1... | collective-permute-start | bytes 1818632 | tf_op jit(solution)/shard_map/ppermute | solution.py:46
  274.6 11.1 %collective-permute-start.6 = (f32[2368,64]{0,1:T(8,128)S(1)}, f32[2368,64]{0,1:T(8,128)S(1)}, u32[]{:S(2)}, u32[]{:S(2)}) collective-permute-start(f32[2368,64]{0,1:T(8,128)S(1)} %add.68), channel_id=1, source_target_pairs={{0,64},{16,80},{32,96},{48,112},{64,0},{80,16},{96,32},{112,48},{1... | collective-permute-start | bytes 1818632 | tf_op jit(solution)/shard_map/ppermute | solution.py:46
Sparse Core Ops, SparseCore 0:
  11.8 133.3 all-gather.1
  203.9 115.5 reduce-scatter.1

commit v16 on v15

--- a/solution.py
+++ b/solution.py
@@ -53,7 +53,7 @@
     out_ref[...] = block.astype(out_ref.dtype)
 
 
-def block_product(weight, grad_t, tile=1280):
+def block_product(weight, grad_t, tile=2560):
     features, depth = weight.shape
     tokens = grad_t.shape[1]
     return pl.pallas_call(

time: 327 us -> 328 us (level)
  no operation moved by 1% of the time
where the time goes in v16:
time: 328 us
  waiting for transfers between devices  210 us (64%)
  matrix products  47.5 us (14%)
  other arithmetic  17.2 us (5%)
  Pallas kernels  16.7 us (5%)
  local copies, waits for them, and re-layouts  16.2 us (5%)
  between operations  14.3 us (4%)
  starting transfers between devices  5.88 us (2%)
    all_gather x1, waiting for transfers between devices, local(): lax.all_gather(jnp.stack([tokens_in, gated_local]), 'col', axis=2, tiled=...  108 us
    ppermute x7, waiting for transfers between devices, tree_sum(): value = value + lax.ppermute(value, axis, pairs)  69.3 us
    dot_general x4, matrix products, plain_dot(): return jnp.dot(left, right, preferred_element_type=jnp.float32)  37.6 us
    reduce_scatter x1, waiting for transfers between devices, local(): lax.psum_scatter(block_t.T, 'col', scatter_dimension=1, tiled=True)  32.2 us
    pallas_call x1, Pallas kernels, block_product(): pl.pallas_call(block_kernel, out_shape=jax.ShapeDtypeStruct((features, to...  16.7 us
    unnamed x22, local copies, waits for them, and re-layouts  13.6 us
    concatenate x1, other arithmetic, local(): jnp.concatenate([inner_down, inner_weight], axis=1)  11.7 us
  transfers between devices with their start and end apart: 9, of which 9 were waited for; matrix products, arithmetic and copies ran while one was open for 10% of the time, Pallas kernels for 0%

profile of v16, /device:TPU:1, one launch (start us, length us, event | category | flops | bytes accessed | tf_op | source)
XLA Modules:
  0.0 327.6 jit_solution(12046566759614254880)
XLA Ops:
  8.1 1.3 fusion.17
  9.4 2.3 pad_maximum_fusion.2
  12.5 12.8 %copy.16 = bf16[5120,864]{1,0:T(8,128)(2,1)} copy(bf16[5120,864]{0,1:T(8,128)(2,1)} %param.13) | data formatting | bytes 17694720 | tf_op args[3]
  25.4 11.7 %pad_maximum_fusion.weight_ref = bf16[5120,928]{1,0:T(8,128)(2,1)} fusion(bf16[5120,864]{1,0:T(8,128)(2,1)} %copy.16, bf16[5120,64]{1,0:T(8,128)(2,1)S(1)} %copy.15), kind=kLoop, calls=%fused_computation.4 | loop fusion | flops 19005440 | bytes 19005440 | tf_op jit(solution)/shard_map/concatenate | solution.py:113
  37.1 108.1 %all-gather.2.cloned.1.call-done = bf16[2,1024,5120]{1,2,0:T(8,128)(2,1)} async-done(((bf16[2,1024,320]{1,2,0:T(8,128)(2,1)}), bf16[2,1024,5120]{1,2,0:T(8,128)(2,1)}) %all-gather.2.cloned.1.call-update) | async-done | bytes 20971536 | tf_op jit(solution)/shard_map/all_gather | solution.py:97
  145.2 15.8 %fusion = f32[1024,928]{0,1:T(8,128)S(1)} fusion(bf16[2,1024,5120]{1,2,0:T(8,128)(2,1)} %all-gather.2.cloned.1.call-done, bf16[5120,64]{0,1:T(8,128)(2,1)S(1)} %copy-done.4, bf16[5120,864]{0,1:T(8,128)(2,1)} %param.13), kind=kOutput, calls=%fused_computation.1 | convolution fusion | flops 9749790720 | bytes 23789568 | tf_op jit(solution)/shard_map/dot_general | solution.py:27
  161.1 3.9 %multiply_convert_fusion = (bf16[1024,864]{0,1:T(8,128)(2,1)}, f32[1024,864]{0,1:T(8,128)}) fusion(f32[864]{0:T(1024)S(1)} %copy-done.9, bf16[64,864]{1,0:T(8,128)(2,1)S(1)} %copy-done, f32[1024,928]{0,1:T(8,128)S(1)} %fusion), kind=kOutput, calls=%fused_computation.23 | convolution fusion | flops 123043840 | bytes 9223552 | tf_op jit(solution)/shard_map/dot_general | solution.py:27
  165.0 15.8 %fusion.1 = f32[1024,928]{0,1:T(8,128)S(1)} fusion(bf16[2,1024,5120]{1,2,0:T(8,128)(2,1)} %all-gather.2.cloned.1.call-done, bf16[5120,64]{0,1:T(8,128)(2,1)S(1)} %bitcast.32, bf16[5120,864]{0,1:T(8,128)(2,1)} %param.15), kind=kOutput, calls=%fused_computation.3 | convolution fusion | flops 9749790720 | bytes 23789568 | tf_op jit(solution)/shard_map/dot_general | solution.py:27
  180.9 5.5 %fusion.14 = bf16[1024,864]{0,1:T(8,128)(2,1)S(1)} fusion(f32[1024,864]{0,1:T(8,128)} %get-tuple-element.10, f32[1024,928]{0,1:T(8,128)S(1)} %fusion.1, bf16[864,64]{0,1:T(8,128)(2,1)S(1)} %copy-done.5), kind=kOutput, calls=%fused_computation.19 | convolution fusion | flops 131006464 | bytes 9220096 | tf_op jit(solution)/shard_map/dot_general | solution.py:31
  186.9 1.4 pad_maximum_fusion.1.grad_ref
  188.3 16.7 %shard_map.137 = bf16[5120,1024]{1,0:T(8,128)(2,1)} custom-call(bf16[5120,928]{1,0:T(8,128)(2,1)} %pad_maximum_fusion.weight_ref, bf16[928,1024]{1,0:T(8,128)(2,1)} %pad_maximum_fusion.1.grad_ref), custom_call_target="tpu_custom_call" | custom-call | flops 9730785280 | bytes 21889024 | tf_op jit(solution)/shard_map/pallas_call | solution.py:59
  205.0 2.1 fusion.27
  207.5 1.7 collective-permute-done
  209.4 14.7 %collective-permute-done.1 = f32[1024,128]{0,1:T(8,128)S(1)} collective-permute-done((f32[1024,128]{0,1:T(8,128)S(1)}, f32[1024,128]{0,1:T(8,128)S(1)}, u32[]{:S(2)}, u32[]{:S(2)}) %collective-permute-start.1) | collective-permute-done | bytes 524320 | tf_op jit(solution)/shard_map/ppermute | solution.py:46
  224.2 12.3 %collective-permute-done.2 = f32[1024,128]{0,1:T(8,128)S(1)} collective-permute-done((f32[1024,128]{0,1:T(8,128)S(1)}, f32[1024,128]{0,1:T(8,128)S(1)}, u32[]{:S(2)}, u32[]{:S(2)}) %collective-permute-start.2) | collective-permute-done | bytes 524320 | tf_op jit(solution)/shard_map/ppermute | solution.py:46
  237.8 1.6 fusion.20
  239.4 1.6 fusion.21
  241.0 14.5 %collective-permute-done.3 = f32[1024,128]{0,1:T(8,128)S(1)} collective-permute-done((f32[1024,128]{0,1:T(8,128)S(1)}, f32[1024,128]{0,1:T(8,128)S(1)}, u32[]{:S(2)}, u32[]{:S(2)}) %collective-permute-start.3) | collective-permute-done | bytes 524320 | tf_op jit(solution)/shard_map/ppermute | solution.py:46
  256.6 9.5 %collective-permute-done.4 = f32[2368,64]{0,1:T(8,128)S(1)} collective-permute-done((f32[2368,64]{0,1:T(8,128)S(1)}, f32[2368,64]{0,1:T(8,128)S(1)}, u32[]{:S(2)}, u32[]{:S(2)}) %collective-permute-start.4) | collective-permute-done | bytes 606240 | tf_op jit(solution)/shard_map/ppermute | solution.py:46
  266.2 1.2 collective-permute-start.5
  267.4 8.4 %collective-permute-done.5 = f32[2368,64]{0,1:T(8,128)S(1)} collective-permute-done((f32[2368,64]{0,1:T(8,128)S(1)}, f32[2368,64]{0,1:T(8,128)S(1)}, u32[]{:S(2)}, u32[]{:S(2)}) %collective-permute-start.5) | collective-permute-done | bytes 606240 | tf_op jit(solution)/shard_map/ppermute | solution.py:46
  275.8 2.8 collective-permute-start.6
  278.6 8.3 %collective-permute-done.6 = f32[2368,64]{0,1:T(8,128)S(1)} collective-permute-done((f32[2368,64]{0,1:T(8,128)S(1)}, f32[2368,64]{0,1:T(8,128)S(1)}, u32[]{:S(2)}, u32[]{:S(2)}) %collective-permute-start.6) | collective-permute-done | bytes 606240 | tf_op jit(solution)/shard_map/ppermute | solution.py:46
  288.5 32.2 %reduce-scatter.2.cloned.1.call-done = bf16[1024,320]{0,1:T(8,128)(2,1)} async-done(((bf16[1024,5120]{0,1:T(8,128)(2,1)}), bf16[1024,320]{0,1:T(8,128)(2,1)}) %reduce-scatter.2.cloned.1.call-update) | async-done | bytes 655376 | tf_op jit(solution)/shard_map/reduce_scatter | solution.py:116
  (46 shorter events, 7.1 us)
Async XLA Ops:
  7.2 153.9 %copy-start = (bf16[64,864]{1,0:T(8,128)(2,1)S(1)}, bf16[64,864]{1,0:T(8,128)(2,1)}, u32[]{:S(2)}) copy-start(bf16[64,864]{1,0:T(8,128)(2,1)} %param.17) | copy-start | bytes 331780
  7.2 4.6 %copy-start.4 = (bf16[5120,64]{0,1:T(8,128)(2,1)S(1)}, bf16[5120,64]{0,1:T(8,128)(2,1)}, u32[]{:S(2)}) copy-start(bf16[5120,64]{0,1:T(8,128)(2,1)} %param.16) | copy-start | bytes 1966084
  7.2 138.0 %all-gather.2.cloned.1.call-start = ((), (), s32[]{:S(2)}) async-start(), calls=%async_computation.1 | async-start | bytes 22282240 | tf_op jit(solution)/shard_map/all_gather | solution.py:97
  11.7 309.0 %reduce-scatter.2.cloned.1.call-start = ((), (), s32[]{:S(2)}) async-start(), calls=%async_computation.2 | async-start | bytes 11141120 | tf_op jit(solution)/shard_map/reduce_scatter | solution.py:116
  37.1 124.0 %copy-start.9 = (f32[864]{0:T(1024)S(1)}, f32[864]{0:T(1024)}, u32[]{:S(2)}) copy-start(f32[864]{0:T(1024)} %param.14) | copy-start | bytes 10372
  161.1 3.9 %copy-start.6 = (f32[1024,928]{0,1:T(8,128)}, f32[1024,928]{0,1:T(8,128)S(1)}, u32[]{:S(2)}) copy-start(f32[1024,928]{0,1:T(8,128)S(1)} %fusion) | copy-start | bytes 11403268
  161.1 3.9 %copy-start.8 = (bf16[64,5120]{1,0:T(8,128)(2,1)S(1)}, bf16[64,5120]{1,0:T(8,128)(2,1)}, u32[]{:S(2)}) copy-start(bf16[64,5120]{1,0:T(8,128)(2,1)} %param.19) | copy-start | bytes 1966084
  165.0 15.9 %copy-start.5 = (bf16[864,64]{0,1:T(8,128)(2,1)S(1)}, bf16[864,64]{0,1:T(8,128)(2,1)}, u32[]{:S(2)}) copy-start(bf16[864,64]{0,1:T(8,128)(2,1)} %param.18) | copy-start | bytes 331780
  180.8 5.5 %copy-start.7 = (f32[1024,928]{0,1:T(8,128)}, f32[1024,928]{0,1:T(8,128)S(1)}, u32[]{:S(2)}) copy-start(f32[1024,928]{0,1:T(8,128)S(1)} %fusion.1) | copy-start | bytes 11403268
  205.0 32.8 %copy-start.1 = (bf16[1024,864]{0,1:T(8,128)(2,1)S(1)}, bf16[1024,864]{0,1:T(8,128)(2,1)}, u32[]{:S(2)}) copy-start(bf16[1024,864]{0,1:T(8,128)(2,1)} %get-tuple-element.9) | copy-start | bytes 5308420
  207.1 2.0 collective-permute-start
  209.2 14.9 %collective-permute-start.1 = (f32[1024,128]{0,1:T(8,128)S(1)}, f32[1024,128]{0,1:T(8,128)S(1)}, u32[]{:S(2)}, u32[]{:S(2)}) collective-permute-start(f32[1024,128]{0,1:T(8,128)S(1)} %fusion.24), channel_id=1, source_target_pairs={{0,2},{1,3},{2,0},{3,1},{4,6},{5,7},{6,4},{7,5},{8,10},{9,11},{10,... | collective-permute-start | bytes 1572872 | tf_op jit(solution)/shard_map/ppermute | solution.py:46
  224.1 31.4 %copy-start.2 = (bf16[1024,320]{0,1:T(8,128)(2,1)S(1)}, bf16[1024,320]{0,1:T(8,128)(2,1)}, u32[]{:S(2)}) copy-start(bf16[1024,320]{0,1:T(8,128)(2,1)} %param.10) | copy-start | bytes 1966084
  224.1 12.4 %collective-permute-start.2 = (f32[1024,128]{0,1:T(8,128)S(1)}, f32[1024,128]{0,1:T(8,128)S(1)}, u32[]{:S(2)}, u32[]{:S(2)}) collective-permute-start(f32[1024,128]{0,1:T(8,128)S(1)} %add.64), channel_id=1, source_target_pairs={{0,4},{1,5},{2,6},{3,7},{4,0},{5,1},{6,2},{7,3},{8,12},{9,13},{10,... | collective-permute-start | bytes 1572872 | tf_op jit(solution)/shard_map/ppermute | solution.py:46
  236.6 19.3 %copy-start.3 = (bf16[1024,320]{0,1:T(8,128)(2,1)S(1)}, bf16[1024,320]{0,1:T(8,128)(2,1)}, u32[]{:S(2)}) copy-start(bf16[1024,320]{0,1:T(8,128)(2,1)} %param.11) | copy-start | bytes 1966084
  236.6 18.8 %collective-permute-start.3 = (f32[1024,128]{0,1:T(8,128)S(1)}, f32[1024,128]{0,1:T(8,128)S(1)}, u32[]{:S(2)}, u32[]{:S(2)}) collective-permute-start(f32[1024,128]{0,1:T(8,128)S(1)} %add.65), channel_id=1, source_target_pairs={{0,8},{1,9},{2,10},{3,11},{4,12},{5,13},{6,14},{7,15},{8,0},{9,1},... | collective-permute-start | bytes 1572872 | tf_op jit(solution)/shard_map/ppermute | solution.py:46
  256.5 9.6 %collective-permute-start.4 = (f32[2368,64]{0,1:T(8,128)S(1)}, f32[2368,64]{0,1:T(8,128)S(1)}, u32[]{:S(2)}, u32[]{:S(2)}) collective-permute-start(f32[2368,64]{0,1:T(8,128)S(1)} %concatenate.23), channel_id=1, source_target_pairs={{0,16},{16,0},{32,48},{48,32},{64,80},{80,64},{96,112},{112,96},{1... | collective-permute-start | bytes 1818632 | tf_op jit(solution)/shard_map/ppermute | solution.py:46
  266.2 9.6 %collective-permute-start.5 = (f32[2368,64]{0,1:T(8,128)S(1)}, f32[2368,64]{0,1:T(8,128)S(1)}, u32[]{:S(2)}, u32[]{:S(2)}) collective-permute-start(f32[2368,64]{0,1:T(8,128)S(1)} %add.67), channel_id=1, source_target_pairs={{0,32},{16,48},{32,0},{48,16},{64,96},{80,112},{96,64},{112,80},{1... | collective-permute-start | bytes 1818632 | tf_op jit(solution)/shard_map/ppermute | solution.py:46
  275.8 11.1 %collective-permute-start.6 = (f32[2368,64]{0,1:T(8,128)S(1)}, f32[2368,64]{0,1:T(8,128)S(1)}, u32[]{:S(2)}, u32[]{:S(2)}) collective-permute-start(f32[2368,64]{0,1:T(8,128)S(1)} %add.68), channel_id=1, source_target_pairs={{0,64},{16,80},{32,96},{48,112},{64,0},{80,16},{96,32},{112,48},{1... | collective-permute-start | bytes 1818632 | tf_op jit(solution)/shard_map/ppermute | solution.py:46
Sparse Core Ops, SparseCore 0:
  11.8 133.3 all-gather.1
  205.1 115.5 reduce-scatter.1

commit v17 on v13

--- a/solution.py
+++ b/solution.py
@@ -48,14 +48,15 @@
     return value
 
 
-def block_kernel(weight_ref, grad_ref, out_ref):
+def block_kernel(weight_ref, grad_ref, down_ref, low_ref, out_ref):
     block = jnp.dot(weight_ref[...], grad_ref[...], preferred_element_type=jnp.float32)
+    block += jnp.dot(down_ref[...], low_ref[...], preferred_element_type=jnp.float32)
     out_ref[...] = block.astype(out_ref.dtype)
 
 
-def block_product(weight, grad_t, tile=640):
+def block_product(weight, grad_t, down, low_t, tile=1280):
     features, depth = weight.shape
-    tokens = grad_t.shape[1]
+    rank, tokens = low_t.shape
     return pl.pallas_call(
         block_kernel,
         out_shape=jax.ShapeDtypeStruct((features, tokens), jnp.bfloat16),
@@ -63,14 +64,16 @@
         in_specs=[
             pl.BlockSpec((tile, depth), lambda i: (i, 0)),
             pl.BlockSpec((depth, tokens), lambda i: (0, 0)),
+            pl.BlockSpec((tile, rank), lambda i: (i, 0)),
+            pl.BlockSpec((rank, tokens), lambda i: (0, 0)),
         ],
         out_specs=pl.BlockSpec((tile, tokens), lambda i: (i, 0)),
         cost_estimate=pl.CostEstimate(
-            flops=2 * features * tokens * depth,
+            flops=2 * features * tokens * (depth + rank),
             transcendentals=0,
-            bytes_accessed=2 * (depth * features + depth * tokens + features * tokens),
+            bytes_accessed=2 * ((depth + rank) * (features + tokens) + features * tokens),
         ),
-    )(weight, grad_t)
+    )(weight, grad_t, down, low_t)
 
 
 def local(
@@ -110,7 +113,7 @@
     grad_pre = (grad_hidden * gelu_slope(pre)).astype(jnp.bfloat16)
     pre_low_part = dot_rows(grad_pre, inner_up)
     block_t = block_product(
-        inner_cat, jnp.concatenate([grad_pre.T, pre_low_part.astype(jnp.bfloat16).T], axis=0)
+        inner_weight, grad_pre.T, inner_down, pre_low_part.astype(jnp.bfloat16).T
     )
     tokens_grad = lax.psum_scatter(block_t.T, "col", scatter_dimension=1, tiled=True)
 

time: 339 us -> 329 us (0.971)
  matrix products: 58.4 us -> 45.9 us
  other arithmetic: 16.2 us -> 4.8 us
  waiting for transfers between devices: 211 us -> 220 us
    dot_general x4, matrix products: 48.5 us -> 36 us  [plain_dot(): return jnp.dot(left, right, preferred_element_type=jnp.float32)]
    concatenate x2 -> x0, other arithmetic: 12.1 us -> none  [the longest x1 10.7 us: local(): inner_cat = jnp.concatenate([inner_weight, inner_down], axis=1)]
    all_gather x1, waiting for transfers between devices: 109 us -> 119 us  [local(): lax.all_gather(jnp.stack([tokens_in, gated_local]), 'col', axis=2, tiled=...]
    unnamed x20 -> x26, local copies, waits for them, and re-layouts: 13.5 us -> 15.8 us
  transfers between devices with their start and end apart: 9 -> 9, of which waited for: 9 -> 9; matrix products, arithmetic and copies ran while one was open for 10% -> 6% of each run, Pallas kernels for 0% -> 0%
where the time goes in v17:
time: 329 us; the launch traced here: 328 us
  waiting for transfers between devices  220 us (67%)
  matrix products  45.9 us (14%)
  local copies, waits for them, and re-layouts  18.4 us (6%)
  Pallas kernels  18.1 us (6%)
  between operations  14.3 us (4%)
  starting transfers between devices  6.25 us (2%)
  other arithmetic  4.8 us (1%)
    all_gather x1, waiting for transfers between devices, local(): lax.all_gather(jnp.stack([tokens_in, gated_local]), 'col', axis=2, tiled=...  119 us
    ppermute x7, waiting for transfers between devices, tree_sum(): value = value + lax.ppermute(value, axis, pairs)  69 us
    dot_general x4, matrix products, plain_dot(): return jnp.dot(left, right, preferred_element_type=jnp.float32)  36 us
    reduce_scatter x1, waiting for transfers between devices, local(): lax.psum_scatter(block_t.T, 'col', scatter_dimension=1, tiled=True)  32.1 us
    pallas_call x1, Pallas kernels, block_product(): pl.pallas_call(block_kernel, out_shape=jax.ShapeDtypeStruct((features, to...  18.1 us
    unnamed x26, local copies, waits for them, and re-layouts  15.8 us
  transfers between devices with their start and end apart: 9, of which 9 were waited for; matrix products, arithmetic and copies ran while one was open for 6% of the time, Pallas kernels for 0%

profile of v17, /device:TPU:1, one launch (start us, length us, event | category | flops | bytes accessed | tf_op | source)
XLA Modules:
  0.0 328.1 jit_solution(8691705555889036246)
XLA Ops:
  8.1 1.3 fusion.17
  9.4 2.3 pad_maximum_fusion
  11.7 1.4 copy.16.down_ref
  13.1 12.9 %copy.15.weight_ref = bf16[5120,864]{1,0:T(8,128)(2,1)} copy(bf16[5120,864]{0,1:T(8,128)(2,1)} %param.13) | data formatting | bytes 17694720 | tf_op args[3]
  26.0 119.1 %all-gather.2.cloned.1.call-done = bf16[2,1024,5120]{1,2,0:T(8,128)(2,1)} async-done(((bf16[2,1024,320]{1,2,0:T(8,128)(2,1)}), bf16[2,1024,5120]{1,2,0:T(8,128)(2,1)}) %all-gather.2.cloned.1.call-update) | async-done | bytes 20971536 | tf_op jit(solution)/shard_map/all_gather | solution.py:100
  145.1 15.8 %fusion = f32[1024,928]{0,1:T(8,128)S(1)} fusion(bf16[2,1024,5120]{1,2,0:T(8,128)(2,1)} %all-gather.2.cloned.1.call-done, bf16[5120,64]{0,1:T(8,128)(2,1)S(1)} %copy-done.6, bf16[5120,864]{0,1:T(8,128)(2,1)} %param.13), kind=kOutput, calls=%fused_computation.1 | convolution fusion | flops 9749790720 | bytes 23789568 | tf_op jit(solution)/shard_map/dot_general | solution.py:27
  161.0 3.9 %multiply_convert_fusion = (bf16[1024,864]{0,1:T(8,128)(2,1)}, f32[1024,864]{0,1:T(8,128)}) fusion(f32[864]{0:T(1024)S(1)} %copy-done.11, bf16[64,864]{1,0:T(8,128)(2,1)S(1)} %copy-done, f32[1024,928]{0,1:T(8,128)S(1)} %fusion), kind=kOutput, calls=%fused_computation.22 | convolution fusion | flops 123043840 | bytes 9223552 | tf_op jit(solution)/shard_map/dot_general | solution.py:27
  164.9 15.9 %fusion.1 = f32[1024,928]{0,1:T(8,128)S(1)} fusion(bf16[2,1024,5120]{1,2,0:T(8,128)(2,1)} %all-gather.2.cloned.1.call-done, bf16[5120,64]{0,1:T(8,128)(2,1)S(1)} %bitcast.32, bf16[5120,864]{0,1:T(8,128)(2,1)} %param.15), kind=kOutput, calls=%fused_computation.3 | convolution fusion | flops 9749790720 | bytes 23789568 | tf_op jit(solution)/shard_map/dot_general | solution.py:27
  180.8 5.5 %fusion.14 = bf16[1024,864]{0,1:T(8,128)(2,1)S(1)} fusion(f32[1024,864]{0,1:T(8,128)} %get-tuple-element.10, f32[1024,928]{0,1:T(8,128)S(1)} %fusion.1, bf16[864,64]{0,1:T(8,128)(2,1)S(1)} %copy-done.7), kind=kOutput, calls=%fused_computation.18 | convolution fusion | flops 131006464 | bytes 9220096 | tf_op jit(solution)/shard_map/dot_general | solution.py:31
  187.6 18.1 %shard_map.137 = bf16[5120,1024]{1,0:T(8,128)(2,1)} custom-call(bf16[5120,864]{1,0:T(8,128)(2,1)} %copy.15.weight_ref, bf16[864,1024]{1,0:T(8,128)(2,1)} %bitcast.30, bf16[5120,64]{1,0:T(8,128)(2,1)} %copy.16.down_ref, bf16[64,1024]{1,0:T(8,128)(2,1)} %convert_bitcast_fusion.low_ref), custom_call_target="tpu_custom_call" | custom-call | flops 9730785280 | bytes 21889024 | tf_op jit(solution)/shard_map/pallas_call | solution.py:60
  205.7 1.4 copy-done.3
  208.0 1.6 collective-permute-done
  209.9 14.6 %collective-permute-done.1 = f32[1024,128]{0,1:T(8,128)S(1)} collective-permute-done((f32[1024,128]{0,1:T(8,128)S(1)}, f32[1024,128]{0,1:T(8,128)S(1)}, u32[]{:S(2)}, u32[]{:S(2)}) %collective-permute-start.1) | collective-permute-done | bytes 524320 | tf_op jit(solution)/shard_map/ppermute | solution.py:46
  224.7 12.3 %collective-permute-done.2 = f32[1024,128]{0,1:T(8,128)S(1)} collective-permute-done((f32[1024,128]{0,1:T(8,128)S(1)}, f32[1024,128]{0,1:T(8,128)S(1)}, u32[]{:S(2)}, u32[]{:S(2)}) %collective-permute-start.2) | collective-permute-done | bytes 524320 | tf_op jit(solution)/shard_map/ppermute | solution.py:46
  237.1 1.2 collective-permute-start.3
  238.3 1.6 fusion.20
  239.9 1.6 fusion.21
  241.5 14.2 %collective-permute-done.3 = f32[1024,128]{0,1:T(8,128)S(1)} collective-permute-done((f32[1024,128]{0,1:T(8,128)S(1)}, f32[1024,128]{0,1:T(8,128)S(1)}, u32[]{:S(2)}, u32[]{:S(2)}) %collective-permute-start.3) | collective-permute-done | bytes 524320 | tf_op jit(solution)/shard_map/ppermute | solution.py:46
  256.9 9.5 %collective-permute-done.4 = f32[2368,64]{0,1:T(8,128)S(1)} collective-permute-done((f32[2368,64]{0,1:T(8,128)S(1)}, f32[2368,64]{0,1:T(8,128)S(1)}, u32[]{:S(2)}, u32[]{:S(2)}) %collective-permute-start.4) | collective-permute-done | bytes 606240 | tf_op jit(solution)/shard_map/ppermute | solution.py:46
  266.5 1.4 collective-permute-start.5
  267.8 8.2 %collective-permute-done.5 = f32[2368,64]{0,1:T(8,128)S(1)} collective-permute-done((f32[2368,64]{0,1:T(8,128)S(1)}, f32[2368,64]{0,1:T(8,128)S(1)}, u32[]{:S(2)}, u32[]{:S(2)}) %collective-permute-start.5) | collective-permute-done | bytes 606240 | tf_op jit(solution)/shard_map/ppermute | solution.py:46
  276.1 3.0 collective-permute-start.6
  279.0 8.5 %collective-permute-done.6 = f32[2368,64]{0,1:T(8,128)S(1)} collective-permute-done((f32[2368,64]{0,1:T(8,128)S(1)}, f32[2368,64]{0,1:T(8,128)S(1)}, u32[]{:S(2)}, u32[]{:S(2)}) %collective-permute-start.6) | collective-permute-done | bytes 606240 | tf_op jit(solution)/shard_map/ppermute | solution.py:46
  289.2 32.1 %reduce-scatter.2.cloned.1.call-done = bf16[1024,320]{0,1:T(8,128)(2,1)} async-done(((bf16[1024,5120]{0,1:T(8,128)(2,1)}), bf16[1024,320]{0,1:T(8,128)(2,1)}) %reduce-scatter.2.cloned.1.call-update) | async-done | bytes 655376 | tf_op jit(solution)/shard_map/reduce_scatter | solution.py:118
  (48 shorter events, 6.4 us)
Async XLA Ops:
  7.2 153.8 %copy-start = (bf16[64,864]{1,0:T(8,128)(2,1)S(1)}, bf16[64,864]{1,0:T(8,128)(2,1)}, u32[]{:S(2)}) copy-start(bf16[64,864]{1,0:T(8,128)(2,1)} %param.17) | copy-start | bytes 331780
  7.2 4.5 %copy-start.6 = (bf16[5120,64]{0,1:T(8,128)(2,1)S(1)}, bf16[5120,64]{0,1:T(8,128)(2,1)}, u32[]{:S(2)}) copy-start(bf16[5120,64]{0,1:T(8,128)(2,1)} %param.16) | copy-start | bytes 1966084
  7.2 137.9 %all-gather.2.cloned.1.call-start = ((), (), s32[]{:S(2)}) async-start(), calls=%async_computation.1 | async-start | bytes 22282240 | tf_op jit(solution)/shard_map/all_gather | solution.py:100
  11.7 309.6 %reduce-scatter.2.cloned.1.call-start = ((), (), s32[]{:S(2)}) async-start(), calls=%async_computation.2 | async-start | bytes 11141120 | tf_op jit(solution)/shard_map/reduce_scatter | solution.py:118
  26.0 135.0 %copy-start.11 = (f32[864]{0:T(1024)S(1)}, f32[864]{0:T(1024)}, u32[]{:S(2)}) copy-start(f32[864]{0:T(1024)} %param.14) | copy-start | bytes 10372
  161.0 3.9 %copy-start.8 = (f32[1024,928]{0,1:T(8,128)}, f32[1024,928]{0,1:T(8,128)S(1)}, u32[]{:S(2)}) copy-start(f32[1024,928]{0,1:T(8,128)S(1)} %fusion) | copy-start | bytes 11403268
  161.0 3.9 %copy-start.10 = (bf16[64,5120]{1,0:T(8,128)(2,1)S(1)}, bf16[64,5120]{1,0:T(8,128)(2,1)}, u32[]{:S(2)}) copy-start(bf16[64,5120]{1,0:T(8,128)(2,1)} %param.19) | copy-start | bytes 1966084
  164.9 15.9 %copy-start.7 = (bf16[864,64]{0,1:T(8,128)(2,1)S(1)}, bf16[864,64]{0,1:T(8,128)(2,1)}, u32[]{:S(2)}) copy-start(bf16[864,64]{0,1:T(8,128)(2,1)} %param.18) | copy-start | bytes 331780
  180.8 5.5 %copy-start.9 = (f32[1024,928]{0,1:T(8,128)}, f32[1024,928]{0,1:T(8,128)S(1)}, u32[]{:S(2)}) copy-start(f32[1024,928]{0,1:T(8,128)S(1)} %fusion.1) | copy-start | bytes 11403268
  186.3 1.2 copy-start.1
  205.7 1.5 copy-start.3
  207.7 32.2 %copy-start.2 = (bf16[1024,864]{0,1:T(8,128)(2,1)S(1)}, bf16[1024,864]{0,1:T(8,128)(2,1)}, u32[]{:S(2)}) copy-start(bf16[1024,864]{0,1:T(8,128)(2,1)} %copy-done.1) | copy-start | bytes 5308420
  207.7 2.0 collective-permute-start
  209.7 14.8 %collective-permute-start.1 = (f32[1024,128]{0,1:T(8,128)S(1)}, f32[1024,128]{0,1:T(8,128)S(1)}, u32[]{:S(2)}, u32[]{:S(2)}) collective-permute-start(f32[1024,128]{0,1:T(8,128)S(1)} %fusion.24), channel_id=1, source_target_pairs={{0,2},{1,3},{2,0},{3,1},{4,6},{5,7},{6,4},{7,5},{8,10},{9,11},{10,... | collective-permute-start | bytes 1572872 | tf_op jit(solution)/shard_map/ppermute | solution.py:46
  224.6 31.2 %copy-start.4 = (bf16[1024,320]{0,1:T(8,128)(2,1)S(1)}, bf16[1024,320]{0,1:T(8,128)(2,1)}, u32[]{:S(2)}) copy-start(bf16[1024,320]{0,1:T(8,128)(2,1)} %param.10) | copy-start | bytes 1966084
  224.6 12.4 %collective-permute-start.2 = (f32[1024,128]{0,1:T(8,128)S(1)}, f32[1024,128]{0,1:T(8,128)S(1)}, u32[]{:S(2)}, u32[]{:S(2)}) collective-permute-start(f32[1024,128]{0,1:T(8,128)S(1)} %add.64), channel_id=1, source_target_pairs={{0,4},{1,5},{2,6},{3,7},{4,0},{5,1},{6,2},{7,3},{8,12},{9,13},{10,... | collective-permute-start | bytes 1572872 | tf_op jit(solution)/shard_map/ppermute | solution.py:46
  237.1 19.1 %copy-start.5 = (bf16[1024,320]{0,1:T(8,128)(2,1)S(1)}, bf16[1024,320]{0,1:T(8,128)(2,1)}, u32[]{:S(2)}) copy-start(bf16[1024,320]{0,1:T(8,128)(2,1)} %param.11) | copy-start | bytes 1966084
  237.1 18.6 %collective-permute-start.3 = (f32[1024,128]{0,1:T(8,128)S(1)}, f32[1024,128]{0,1:T(8,128)S(1)}, u32[]{:S(2)}, u32[]{:S(2)}) collective-permute-start(f32[1024,128]{0,1:T(8,128)S(1)} %add.65), channel_id=1, source_target_pairs={{0,8},{1,9},{2,10},{3,11},{4,12},{5,13},{6,14},{7,15},{8,0},{9,1},... | collective-permute-start | bytes 1572872 | tf_op jit(solution)/shard_map/ppermute | solution.py:46
  256.8 9.6 %collective-permute-start.4 = (f32[2368,64]{0,1:T(8,128)S(1)}, f32[2368,64]{0,1:T(8,128)S(1)}, u32[]{:S(2)}, u32[]{:S(2)}) collective-permute-start(f32[2368,64]{0,1:T(8,128)S(1)} %concatenate.15), channel_id=1, source_target_pairs={{0,16},{16,0},{32,48},{48,32},{64,80},{80,64},{96,112},{112,96},{1... | collective-permute-start | bytes 1818632 | tf_op jit(solution)/shard_map/ppermute | solution.py:46
  266.5 9.6 %collective-permute-start.5 = (f32[2368,64]{0,1:T(8,128)S(1)}, f32[2368,64]{0,1:T(8,128)S(1)}, u32[]{:S(2)}, u32[]{:S(2)}) collective-permute-start(f32[2368,64]{0,1:T(8,128)S(1)} %add.67), channel_id=1, source_target_pairs={{0,32},{16,48},{32,0},{48,16},{64,96},{80,112},{96,64},{112,80},{1... | collective-permute-start | bytes 1818632 | tf_op jit(solution)/shard_map/ppermute | solution.py:46
  276.1 11.5 %collective-permute-start.6 = (f32[2368,64]{0,1:T(8,128)S(1)}, f32[2368,64]{0,1:T(8,128)S(1)}, u32[]{:S(2)}, u32[]{:S(2)}) collective-permute-start(f32[2368,64]{0,1:T(8,128)S(1)} %add.68), channel_id=1, source_target_pairs={{0,64},{16,80},{32,96},{48,112},{64,0},{80,16},{96,32},{112,48},{1... | collective-permute-start | bytes 1818632 | tf_op jit(solution)/shard_map/ppermute | solution.py:46
Sparse Core Ops, SparseCore 0:
  11.8 133.3 all-gather.1
  205.8 115.3 reduce-scatter.1

commit v18 on v16

--- a/solution.py
+++ b/solution.py
@@ -53,7 +53,7 @@
     out_ref[...] = block.astype(out_ref.dtype)
 
 
-def block_product(weight, grad_t, tile=2560):
+def block_product(weight, grad_t, tile=1024):
     features, depth = weight.shape
     tokens = grad_t.shape[1]
     return pl.pallas_call(

time: 328 us -> 327 us (level)
  no operation moved by 1% of the time
where the time goes in v18:
time: 327 us; the launch traced here: 326 us
  waiting for transfers between devices  210 us (64%)
  matrix products  47.5 us (15%)
  other arithmetic  17.2 us (5%)
  local copies, waits for them, and re-layouts  16.2 us (5%)
  Pallas kernels  15.2 us (5%)
  between operations  14.3 us (4%)
  starting transfers between devices  5.88 us (2%)
    all_gather x1, waiting for transfers between devices, local(): lax.all_gather(jnp.stack([tokens_in, gated_local]), 'col', axis=2, tiled=...  108 us
    ppermute x7, waiting for transfers between devices, tree_sum(): value = value + lax.ppermute(value, axis, pairs)  69.3 us
    dot_general x4, matrix products, plain_dot(): return jnp.dot(left, right, preferred_element_type=jnp.float32)  37.6 us
    reduce_scatter x1, waiting for transfers between devices, local(): lax.psum_scatter(block_t.T, 'col', scatter_dimension=1, tiled=True)  32.2 us
    pallas_call x1, Pallas kernels, block_product(): pl.pallas_call(block_kernel, out_shape=jax.ShapeDtypeStruct((features, to...  15.2 us
    unnamed x22, local copies, waits for them, and re-layouts  13.6 us
    concatenate x1, other arithmetic, local(): jnp.concatenate([inner_down, inner_weight], axis=1)  11.7 us
  transfers between devices with their start and end apart: 9, of which 9 were waited for; matrix products, arithmetic and copies ran while one was open for 10% of the time, Pallas kernels for 0%

profile of v18, /device:TPU:1, one launch (start us, length us, event | category | flops | bytes accessed | tf_op | source)
XLA Modules:
  0.0 326.1 jit_solution(16674573520605686685)
XLA Ops:
  8.1 1.3 fusion.17
  9.4 2.3 pad_maximum_fusion.2
  12.5 12.8 %copy.16 = bf16[5120,864]{1,0:T(8,128)(2,1)} copy(bf16[5120,864]{0,1:T(8,128)(2,1)} %param.13) | data formatting | bytes 17694720 | tf_op args[3]
  25.4 11.7 %pad_maximum_fusion.weight_ref = bf16[5120,928]{1,0:T(8,128)(2,1)} fusion(bf16[5120,864]{1,0:T(8,128)(2,1)} %copy.16, bf16[5120,64]{1,0:T(8,128)(2,1)S(1)} %copy.15), kind=kLoop, calls=%fused_computation.4 | loop fusion | flops 19005440 | bytes 19005440 | tf_op jit(solution)/shard_map/concatenate | solution.py:113
  37.1 108.1 %all-gather.2.cloned.1.call-done = bf16[2,1024,5120]{1,2,0:T(8,128)(2,1)} async-done(((bf16[2,1024,320]{1,2,0:T(8,128)(2,1)}), bf16[2,1024,5120]{1,2,0:T(8,128)(2,1)}) %all-gather.2.cloned.1.call-update) | async-done | bytes 20971536 | tf_op jit(solution)/shard_map/all_gather | solution.py:97
  145.2 15.8 %fusion = f32[1024,928]{0,1:T(8,128)S(1)} fusion(bf16[2,1024,5120]{1,2,0:T(8,128)(2,1)} %all-gather.2.cloned.1.call-done, bf16[5120,64]{0,1:T(8,128)(2,1)S(1)} %copy-done.4, bf16[5120,864]{0,1:T(8,128)(2,1)} %param.13), kind=kOutput, calls=%fused_computation.1 | convolution fusion | flops 9749790720 | bytes 23789568 | tf_op jit(solution)/shard_map/dot_general | solution.py:27
  161.1 3.9 %multiply_convert_fusion = (bf16[1024,864]{0,1:T(8,128)(2,1)}, f32[1024,864]{0,1:T(8,128)}) fusion(f32[864]{0:T(1024)S(1)} %copy-done.9, bf16[64,864]{1,0:T(8,128)(2,1)S(1)} %copy-done, f32[1024,928]{0,1:T(8,128)S(1)} %fusion), kind=kOutput, calls=%fused_computation.23 | convolution fusion | flops 123043840 | bytes 9223552 | tf_op jit(solution)/shard_map/dot_general | solution.py:27
  165.0 15.8 %fusion.1 = f32[1024,928]{0,1:T(8,128)S(1)} fusion(bf16[2,1024,5120]{1,2,0:T(8,128)(2,1)} %all-gather.2.cloned.1.call-done, bf16[5120,64]{0,1:T(8,128)(2,1)S(1)} %bitcast.32, bf16[5120,864]{0,1:T(8,128)(2,1)} %param.15), kind=kOutput, calls=%fused_computation.3 | convolution fusion | flops 9749790720 | bytes 23789568 | tf_op jit(solution)/shard_map/dot_general | solution.py:27
  180.9 5.5 %fusion.14 = bf16[1024,864]{0,1:T(8,128)(2,1)S(1)} fusion(f32[1024,864]{0,1:T(8,128)} %get-tuple-element.10, f32[1024,928]{0,1:T(8,128)S(1)} %fusion.1, bf16[864,64]{0,1:T(8,128)(2,1)S(1)} %copy-done.5), kind=kOutput, calls=%fused_computation.19 | convolution fusion | flops 131006464 | bytes 9220096 | tf_op jit(solution)/shard_map/dot_general | solution.py:31
  186.9 1.4 pad_maximum_fusion.1.grad_ref
  188.3 15.2 %shard_map.137 = bf16[5120,1024]{1,0:T(8,128)(2,1)} custom-call(bf16[5120,928]{1,0:T(8,128)(2,1)} %pad_maximum_fusion.weight_ref, bf16[928,1024]{1,0:T(8,128)(2,1)} %pad_maximum_fusion.1.grad_ref), custom_call_target="tpu_custom_call" | custom-call | flops 9730785280 | bytes 21889024 | tf_op jit(solution)/shard_map/pallas_call | solution.py:59
  203.6 2.1 fusion.27
  206.0 1.7 collective-permute-done
  207.9 14.7 %collective-permute-done.1 = f32[1024,128]{0,1:T(8,128)S(1)} collective-permute-done((f32[1024,128]{0,1:T(8,128)S(1)}, f32[1024,128]{0,1:T(8,128)S(1)}, u32[]{:S(2)}, u32[]{:S(2)}) %collective-permute-start.1) | collective-permute-done | bytes 524320 | tf_op jit(solution)/shard_map/ppermute | solution.py:46
  222.8 12.3 %collective-permute-done.2 = f32[1024,128]{0,1:T(8,128)S(1)} collective-permute-done((f32[1024,128]{0,1:T(8,128)S(1)}, f32[1024,128]{0,1:T(8,128)S(1)}, u32[]{:S(2)}, u32[]{:S(2)}) %collective-permute-start.2) | collective-permute-done | bytes 524320 | tf_op jit(solution)/shard_map/ppermute | solution.py:46
  236.3 1.6 fusion.20
  237.9 1.6 fusion.21
  239.5 14.5 %collective-permute-done.3 = f32[1024,128]{0,1:T(8,128)S(1)} collective-permute-done((f32[1024,128]{0,1:T(8,128)S(1)}, f32[1024,128]{0,1:T(8,128)S(1)}, u32[]{:S(2)}, u32[]{:S(2)}) %collective-permute-start.3) | collective-permute-done | bytes 524320 | tf_op jit(solution)/shard_map/ppermute | solution.py:46
  255.2 9.5 %collective-permute-done.4 = f32[2368,64]{0,1:T(8,128)S(1)} collective-permute-done((f32[2368,64]{0,1:T(8,128)S(1)}, f32[2368,64]{0,1:T(8,128)S(1)}, u32[]{:S(2)}, u32[]{:S(2)}) %collective-permute-start.4) | collective-permute-done | bytes 606240 | tf_op jit(solution)/shard_map/ppermute | solution.py:46
  264.7 1.2 collective-permute-start.5
  265.9 8.4 %collective-permute-done.5 = f32[2368,64]{0,1:T(8,128)S(1)} collective-permute-done((f32[2368,64]{0,1:T(8,128)S(1)}, f32[2368,64]{0,1:T(8,128)S(1)}, u32[]{:S(2)}, u32[]{:S(2)}) %collective-permute-start.5) | collective-permute-done | bytes 606240 | tf_op jit(solution)/shard_map/ppermute | solution.py:46
  274.3 2.8 collective-permute-start.6
  277.1 8.3 %collective-permute-done.6 = f32[2368,64]{0,1:T(8,128)S(1)} collective-permute-done((f32[2368,64]{0,1:T(8,128)S(1)}, f32[2368,64]{0,1:T(8,128)S(1)}, u32[]{:S(2)}, u32[]{:S(2)}) %collective-permute-start.6) | collective-permute-done | bytes 606240 | tf_op jit(solution)/shard_map/ppermute | solution.py:46
  287.0 32.2 %reduce-scatter.2.cloned.1.call-done = bf16[1024,320]{0,1:T(8,128)(2,1)} async-done(((bf16[1024,5120]{0,1:T(8,128)(2,1)}), bf16[1024,320]{0,1:T(8,128)(2,1)}) %reduce-scatter.2.cloned.1.call-update) | async-done | bytes 655376 | tf_op jit(solution)/shard_map/reduce_scatter | solution.py:116
  (46 shorter events, 7.1 us)
Async XLA Ops:
  7.2 153.9 %copy-start = (bf16[64,864]{1,0:T(8,128)(2,1)S(1)}, bf16[64,864]{1,0:T(8,128)(2,1)}, u32[]{:S(2)}) copy-start(bf16[64,864]{1,0:T(8,128)(2,1)} %param.17) | copy-start | bytes 331780
  7.2 4.6 %copy-start.4 = (bf16[5120,64]{0,1:T(8,128)(2,1)S(1)}, bf16[5120,64]{0,1:T(8,128)(2,1)}, u32[]{:S(2)}) copy-start(bf16[5120,64]{0,1:T(8,128)(2,1)} %param.16) | copy-start | bytes 1966084
  7.2 138.0 %all-gather.2.cloned.1.call-start = ((), (), s32[]{:S(2)}) async-start(), calls=%async_computation.1 | async-start | bytes 22282240 | tf_op jit(solution)/shard_map/all_gather | solution.py:97
  11.7 307.5 %reduce-scatter.2.cloned.1.call-start = ((), (), s32[]{:S(2)}) async-start(), calls=%async_computation.2 | async-start | bytes 11141120 | tf_op jit(solution)/shard_map/reduce_scatter | solution.py:116
  37.1 124.0 %copy-start.9 = (f32[864]{0:T(1024)S(1)}, f32[864]{0:T(1024)}, u32[]{:S(2)}) copy-start(f32[864]{0:T(1024)} %param.14) | copy-start | bytes 10372
  161.1 3.9 %copy-start.6 = (f32[1024,928]{0,1:T(8,128)}, f32[1024,928]{0,1:T(8,128)S(1)}, u32[]{:S(2)}) copy-start(f32[1024,928]{0,1:T(8,128)S(1)} %fusion) | copy-start | bytes 11403268
  161.1 3.9 %copy-start.8 = (bf16[64,5120]{1,0:T(8,128)(2,1)S(1)}, bf16[64,5120]{1,0:T(8,128)(2,1)}, u32[]{:S(2)}) copy-start(bf16[64,5120]{1,0:T(8,128)(2,1)} %param.19) | copy-start | bytes 1966084
  165.0 15.9 %copy-start.5 = (bf16[864,64]{0,1:T(8,128)(2,1)S(1)}, bf16[864,64]{0,1:T(8,128)(2,1)}, u32[]{:S(2)}) copy-start(bf16[864,64]{0,1:T(8,128)(2,1)} %param.18) | copy-start | bytes 331780
  180.8 5.5 %copy-start.7 = (f32[1024,928]{0,1:T(8,128)}, f32[1024,928]{0,1:T(8,128)S(1)}, u32[]{:S(2)}) copy-start(f32[1024,928]{0,1:T(8,128)S(1)} %fusion.1) | copy-start | bytes 11403268
  203.5 32.8 %copy-start.1 = (bf16[1024,864]{0,1:T(8,128)(2,1)S(1)}, bf16[1024,864]{0,1:T(8,128)(2,1)}, u32[]{:S(2)}) copy-start(bf16[1024,864]{0,1:T(8,128)(2,1)} %get-tuple-element.9) | copy-start | bytes 5308420
  205.7 2.0 collective-permute-start
  207.7 14.9 %collective-permute-start.1 = (f32[1024,128]{0,1:T(8,128)S(1)}, f32[1024,128]{0,1:T(8,128)S(1)}, u32[]{:S(2)}, u32[]{:S(2)}) collective-permute-start(f32[1024,128]{0,1:T(8,128)S(1)} %fusion.24), channel_id=1, source_target_pairs={{0,2},{1,3},{2,0},{3,1},{4,6},{5,7},{6,4},{7,5},{8,10},{9,11},{10,... | collective-permute-start | bytes 1572872 | tf_op jit(solution)/shard_map/ppermute | solution.py:46
  222.7 31.4 %copy-start.2 = (bf16[1024,320]{0,1:T(8,128)(2,1)S(1)}, bf16[1024,320]{0,1:T(8,128)(2,1)}, u32[]{:S(2)}) copy-start(bf16[1024,320]{0,1:T(8,128)(2,1)} %param.10) | copy-start | bytes 1966084
  222.7 12.4 %collective-permute-start.2 = (f32[1024,128]{0,1:T(8,128)S(1)}, f32[1024,128]{0,1:T(8,128)S(1)}, u32[]{:S(2)}, u32[]{:S(2)}) collective-permute-start(f32[1024,128]{0,1:T(8,128)S(1)} %add.64), channel_id=1, source_target_pairs={{0,4},{1,5},{2,6},{3,7},{4,0},{5,1},{6,2},{7,3},{8,12},{9,13},{10,... | collective-permute-start | bytes 1572872 | tf_op jit(solution)/shard_map/ppermute | solution.py:46
  235.2 19.3 %copy-start.3 = (bf16[1024,320]{0,1:T(8,128)(2,1)S(1)}, bf16[1024,320]{0,1:T(8,128)(2,1)}, u32[]{:S(2)}) copy-start(bf16[1024,320]{0,1:T(8,128)(2,1)} %param.11) | copy-start | bytes 1966084
  235.2 18.8 %collective-permute-start.3 = (f32[1024,128]{0,1:T(8,128)S(1)}, f32[1024,128]{0,1:T(8,128)S(1)}, u32[]{:S(2)}, u32[]{:S(2)}) collective-permute-start(f32[1024,128]{0,1:T(8,128)S(1)} %add.65), channel_id=1, source_target_pairs={{0,8},{1,9},{2,10},{3,11},{4,12},{5,13},{6,14},{7,15},{8,0},{9,1},... | collective-permute-start | bytes 1572872 | tf_op jit(solution)/shard_map/ppermute | solution.py:46
  255.1 9.6 %collective-permute-start.4 = (f32[2368,64]{0,1:T(8,128)S(1)}, f32[2368,64]{0,1:T(8,128)S(1)}, u32[]{:S(2)}, u32[]{:S(2)}) collective-permute-start(f32[2368,64]{0,1:T(8,128)S(1)} %concatenate.23), channel_id=1, source_target_pairs={{0,16},{16,0},{32,48},{48,32},{64,80},{80,64},{96,112},{112,96},{1... | collective-permute-start | bytes 1818632 | tf_op jit(solution)/shard_map/ppermute | solution.py:46
  264.7 9.6 %collective-permute-start.5 = (f32[2368,64]{0,1:T(8,128)S(1)}, f32[2368,64]{0,1:T(8,128)S(1)}, u32[]{:S(2)}, u32[]{:S(2)}) collective-permute-start(f32[2368,64]{0,1:T(8,128)S(1)} %add.67), channel_id=1, source_target_pairs={{0,32},{16,48},{32,0},{48,16},{64,96},{80,112},{96,64},{112,80},{1... | collective-permute-start | bytes 1818632 | tf_op jit(solution)/shard_map/ppermute | solution.py:46
  274.3 11.1 %collective-permute-start.6 = (f32[2368,64]{0,1:T(8,128)S(1)}, f32[2368,64]{0,1:T(8,128)S(1)}, u32[]{:S(2)}, u32[]{:S(2)}) collective-permute-start(f32[2368,64]{0,1:T(8,128)S(1)} %add.68), channel_id=1, source_target_pairs={{0,64},{16,80},{32,96},{48,112},{64,0},{80,16},{96,32},{112,48},{1... | collective-permute-start | bytes 1818632 | tf_op jit(solution)/shard_map/ppermute | solution.py:46
Sparse Core Ops, SparseCore 0:
  11.8 133.3 all-gather.1
  203.7 115.5 reduce-scatter.1
